TPU v7x, 32 devices: a whole 2x2x4 slice. The times are simulated.
32 devices in a mesh: grp: 2 (over x), ka: 16 (over z, y, core).
Axes of the slice: x: 2, y: 2, z: 4, core: 2. Of those that a mesh axis runs over, the one named last changes fastest.
Arguments:
- wannier_table: float32 [2, 2048, 8192], P(None, 'grp', 'ka'), parts along dimension 1, may hold values from -0.125 to 0.125
- lattice: int32 [3, 2048], P(None, 'grp'), parts along dimension 1, may hold values from -12 to 12
- kpoint_grid: int32 [3, 2048], P(None, ('grp', 'ka')), parts along dimension 1, may hold values from 0 to 63
- eigen_vectors: float32 [2048, 64, 128], P(('grp', 'ka')), parts along dimension 0, may hold values from -0.5 to 0.5
- target_owner: int32 [2048], P(('grp', 'ka')), parts along dimension 0, may hold values from 0 to 15, as said below
- target_slot: int32 [2048], P(('grp', 'ka')), parts along dimension 0, may hold values from 0 to 63
Outputs:
- rotated_coupling: float32 [2048, 2, 64, 128], P(('grp', 'ka')), parts along dimension 0
There are 2 independent parts, one for each index of `grp`. A program takes and returns all parts, laid end to end along the dimension named above; each array names one. Nothing has to cross between parts.
Inputs may be any that keep to these rules, and one draw needn't show every extreme that they name: target_owner[k] * 64 + target_slot[k] over all k is a permutation of the 1024 k-points. The 64 k-points of one index of ka ask at most 8 of them of any one owner, and every device asks exactly 8 of some owner.
All inputs are finite; a program needn't handle non-finite values.
Results may differ from a plain program's by a relative error of at most 0.0003.
Values sent between devices are 32-bit elements; how exact they have to be, the bound alone decides.
No kernel may reach another device: no remote copies, remote signals or barrier semaphores. Data moves between devices by JAX's collectives and lax.ppermute only.
A program may use at most 128 MiB of HBM per device.

v0:
```python
import math

import jax
import jax.numpy as jnp
from jax import lax
from jax.experimental import pallas as pl
from jax.experimental.pallas import tpu as pltpu
from jax.sharding import PartitionSpec as P


KMESH = 64
SHIFTED = 16

SIN_TERMS = [(-1.0) ** i * math.pi ** (2 * i + 1) / math.factorial(2 * i + 1) for i in range(7)]
COS_TERMS = [(-1.0) ** i * math.pi ** (2 * i) / math.factorial(2 * i) for i in range(8)]


def horner(terms, x):
    total = jnp.full_like(x, terms[-1])
    for term in terms[-2::-1]:
        total = total * x + term
    return total


def split(x):
    high = x.astype(jnp.bfloat16)
    return high, (x - high.astype(jnp.float32)).astype(jnp.bfloat16)


def dot(a, b):
    return jnp.dot(a, b, preferred_element_type=jnp.float32)


def dot3(a, b):
    return dot(a[0], b[0]) + dot(a[0], b[1]) + dot(a[1], b[0])


def table_kernel(table, high, low):
    half = pl.program_id(0)
    pairs = table.shape[2]
    lane = lax.broadcasted_iota(jnp.int32, (table.shape[1], 128), 1)
    first = lane < 64
    for block in range(pairs // 128):
        cut = slice(block * 128, (block + 1) * 128)

        def put(at, value):
            a, b = split(value)
            high[:, at * 128 : (at + 1) * 128] = a
            low[:, at * 128 : (at + 1) * 128] = b

        @pl.when(half == 0)
        def _():
            real, imag = table[0, :, cut], table[1, :, cut]
            put(2 * block, jnp.where(first, real, pltpu.roll(imag, 64, 1)))
            put(2 * block + 1, jnp.where(first, pltpu.roll(real, 64, 1), imag))

        @pl.when(half == 1)
        def _():
            real, imag = table[0, :, cut], table[1, :, cut]
            put(2 * block, jnp.where(first, -imag, pltpu.roll(real, 64, 1)))
            put(2 * block + 1, jnp.where(first, -pltpu.roll(imag, 64, 1), real))


def prepare_table(table):
    vectors, pairs = table.shape[1:]
    rows = min(vectors, 256)
    steps = vectors // rows
    return pl.pallas_call(
        table_kernel,
        out_shape=[jax.ShapeDtypeStruct((2 * vectors, 2 * pairs), jnp.bfloat16)] * 2,
        grid=(2, steps),
        in_specs=[pl.BlockSpec((2, rows, pairs), lambda h, i: (0, i, 0))],
        out_specs=[pl.BlockSpec((rows, 2 * pairs), lambda h, i: (h * steps + i, 0))] * 2,
        name="table",
    )(table)


def interpolate_kernel(grid_rows, lattice, high, low, out, *, mrows):
    turns = dot(grid_rows[...].astype(jnp.bfloat16), lattice[...].astype(jnp.bfloat16)) * (1.0 / KMESH)
    part = turns - jnp.round(turns)
    square = part * part
    sine = horner(SIN_TERMS, square) * part
    cosine = horner(COS_TERMS, square)
    phase = jnp.concatenate([1.0 - 2.0 * sine * sine, 2.0 * sine * cosine], 1)
    result = dot3(split(phase), (high[...], low[...]))
    rows = result.shape[0]
    for m in range(mrows):
        out[pl.ds(m, rows, stride=mrows), :] = result[:, m * 128 : (m + 1) * 128]


def interpolate(grid_rows, lattice, high, low, mrows):
    rows = grid_rows.shape[0]
    step = min(rows, 256)
    whole = lambda a: pl.BlockSpec(a.shape, lambda i: (0, 0))
    return pl.pallas_call(
        lambda *refs: interpolate_kernel(*refs, mrows=mrows),
        out_shape=jax.ShapeDtypeStruct((rows * mrows, 128), jnp.float32),
        grid=(rows // step,),
        in_specs=[
            pl.BlockSpec((step, grid_rows.shape[1]), lambda i: (i, 0)),
            whole(lattice),
            whole(high),
            whole(low),
        ],
        out_specs=pl.BlockSpec((step * mrows, 128), lambda i: (i, 0)),
        name="interpolate",
    )(grid_rows, lattice, high, low)


def rotate_one(values, u, far, orbitals):
    lanes = 2 * orbitals
    first = lax.broadcasted_iota(jnp.int32, (orbitals, lanes), 1) < orbitals
    first_all = lax.broadcasted_iota(jnp.int32, (values.shape[0], lanes), 1) < orbitals
    u_turned = pltpu.roll(u, orbitals, 1)
    u_full = jnp.concatenate([u, jnp.where(first, -u_turned, u_turned)], 0)
    right = dot3(split(values), split(u_full))
    turned = pltpu.roll(right, orbitals, 1)
    turned = jnp.where(first_all, turned, -turned)
    v = far.T
    left = jnp.concatenate([v[:orbitals], v[orbitals:]], 1)
    modes = values.shape[0] // orbitals
    by_mode = lambda x: jnp.concatenate([x[a * orbitals : (a + 1) * orbitals] for a in range(modes)], 1)
    done = dot3(split(left), split(jnp.concatenate([by_mode(right), by_mode(turned)], 0)))
    return [done[:, a * lanes : (a + 1) * lanes] for a in range(modes)]


def rotate_kernel(place, *refs, block, mrows, parts, orbitals):
    pieces = refs[:parts]
    near, far = refs[parts : parts + 2]
    out, gathered = refs[-2:]
    for k in range(block):
        if parts == 1 and mrows:
            values = pieces[0][:, k * mrows : (k + 1) * mrows, :].reshape(gathered.shape[1:])
        elif mrows:
            for s in range(parts):
                at = pl.multiple_of(lax.rem(place[0] + (parts - s), parts) * mrows, mrows)
                gathered[k, pl.ds(at, mrows), :] = pieces[s][k * mrows : (k + 1) * mrows, :]
            values = gathered[k]
        else:
            values = pieces[0][k]
        for a, done in enumerate(rotate_one(values, near[k], far[k], orbitals)):
            out[k, a] = done


def rotate(pieces, near, far, mrows, modes, start, place, before):
    total, orbitals = near.shape[:2]
    block = 8
    first = start // block
    lanes = 2 * orbitals
    if mrows and len(pieces) == 1:
        kpoints = pieces[0].shape[1] // mrows
        piece_spec = pl.BlockSpec((pieces[0].shape[0], block * mrows, lanes), lambda i, _: (0, i, 0))
    elif mrows:
        kpoints = pieces[0].shape[0] // mrows
        piece_spec = pl.BlockSpec((block * mrows, lanes), lambda i, _: (i, 0))
    else:
        kpoints = pieces[0].shape[0]
        piece_spec = pl.BlockSpec((block, modes * orbitals, lanes), lambda i, _: (i, 0, 0))
    prior = [] if before is None else [before]
    return pl.pallas_call(
        lambda *refs: rotate_kernel(
            *refs, block=block, mrows=mrows, parts=len(pieces), orbitals=orbitals
        ),
        out_shape=jax.ShapeDtypeStruct((total, modes, orbitals, lanes), jnp.float32),
        grid_spec=pltpu.PrefetchScalarGridSpec(
            num_scalar_prefetch=1,
            grid=(kpoints // block,),
            in_specs=[piece_spec] * len(pieces)
            + [
                pl.BlockSpec((block, orbitals, lanes), lambda i, _: (first + i, 0, 0)),
                pl.BlockSpec((block, orbitals, lanes), lambda i, _: (first + i, 0, 0)),
            ]
            + [pl.BlockSpec(memory_space=pl.ANY)] * len(prior),
            out_specs=pl.BlockSpec((block, modes, orbitals, lanes), lambda i, _: (first + i, 0, 0, 0)),
            scratch_shapes=[pltpu.VMEM((block, modes * orbitals, lanes), jnp.float32)],
        ),
        input_output_aliases={len(pieces) + 3: 0} if prior else {},
        name="rotate",
    )(place, *pieces, near, far, *prior)


def exchange(x):
    return lax.all_to_all(x, "ka", split_axis=0, concat_axis=0, tiled=True)


def shift_order(devices):
    far_first = sorted(range(1, devices), key=lambda s: -min(s, devices - s))
    order = []
    while far_first:
        order.append(far_first.pop(0))
        if far_first:
            order.append(far_first.pop())
    return order


def spread(blocks, devices):
    got = {0: blocks(0)}
    for s in shift_order(devices):
        got[s] = lax.ppermute(blocks(s), "ka", [(d, (d + s) % devices) for d in range(devices)])
    return [got[s] for s in range(devices)]


def placed_local(wannier_table, lattice, kpoint_grid, eigen_vectors, target_owner, target_slot):
    kpoints, orbitals = eigen_vectors.shape[:2]
    vectors, pairs = wannier_table.shape[1:]
    devices = lax.axis_size("ka")
    me = lax.axis_index("ka")
    mrows = pairs // orbitals
    modes = devices * mrows // orbitals
    lanes = 2 * orbitals
    capacity = 2 * kpoints // devices
    tiled = mrows % 8 == 0
    by_shift = devices <= SHIFTED and tiled

    own = jnp.concatenate(
        [kpoint_grid, target_owner[None], target_slot[None], jnp.zeros((3, kpoints), jnp.int32)], 0
    )
    known = exchange(jnp.broadcast_to(own[None], (devices, 8, kpoints)))
    asked = known[:, 3] == me
    position = jnp.cumsum(asked.astype(jnp.int32), 1) - 1
    chosen = asked[:, None, :] & (position[:, None, :] == jnp.arange(capacity)[None, :, None])
    wanted = jnp.sum(jnp.where(chosen, known[:, 4][:, None, :], 0), 2)
    picked = eigen_vectors[wanted.reshape(-1)].reshape(devices, capacity * orbitals, lanes)
    fetched = exchange(picked).reshape(devices * capacity, orbitals, lanes)
    high, low = prepare_table(wannier_table)

    owners = (target_owner[:, None] == jnp.arange(devices, dtype=jnp.int32)[None, :]).astype(jnp.int32)
    before = jnp.cumsum(owners, 0) - owners
    far = fetched[target_owner * capacity + jnp.sum(before * owners, 1)]

    grid_rows = known.transpose(0, 2, 1).astype(jnp.float32)
    turned_rows = lax.dynamic_slice_in_dim(jnp.concatenate([grid_rows, grid_rows], 0), me, devices, 0)
    lattice_rows = jnp.concatenate([lattice, jnp.zeros((5, vectors), jnp.int32)], 0).astype(jnp.float32)
    cuts = [(0, kpoints // 4 * 3, by_shift), (kpoints // 4 * 3, kpoints, False)]
    sent = []
    for start, end, shifted in cuts:
        rows = (turned_rows if shifted else grid_rows)[:, start:end].reshape(devices * (end - start), 8)
        values = interpolate(rows, lattice_rows, high, low, mrows)
        values = values.reshape(devices, (end - start) * mrows, lanes)
        if shifted:
            sent.append(spread(lambda s: values[s], devices))
        elif tiled:
            sent.append([exchange(values)])
        else:
            got = exchange(values)
            got = got.reshape(devices, end - start, mrows, lanes)
            sent.append([got.transpose(1, 0, 2, 3).reshape(end - start, devices * mrows, lanes)])
    out = None
    place = me.astype(jnp.int32).reshape(1)
    for (start, end, shifted), pieces in zip(cuts, sent):
        out = rotate(pieces, eigen_vectors, far, mrows if tiled else 0, modes, start, place, out)
    return out


def solution(mesh):
    placed = (
        P(None, "grp", "ka"),
        P(None, "grp"),
        P(None, ("grp", "ka")),
        P(("grp", "ka"), None, None),
        P(("grp", "ka")),
        P(("grp", "ka")),
    )
    return jax.shard_map(
        placed_local,
        mesh=mesh,
        in_specs=placed,
        out_specs=P(("grp", "ka"), None, None, None),
        check_vma=False,
    )
```

profile of v0, /device:TPU:0, one launch (start us, length us, event | category | flops | bytes accessed | tf_op | source)
XLA Modules:
  0.0 243.6 jit_solution(13442373192686847382)
XLA Ops:
  0.1 0.8 add_add_fusion
  0.9 0.7 reshape.115
  1.6 7.4 %all-to-all-start = ((s32[16,1,512]{2,1,0:T(1,128)}), s32[16,1,512]{2,1,0:T(1,128)S(1)}, u32[]{:S(2)}, u32[]{:S(2)}) async-start(s32[16,1,512]{2,1,0:T(1,128)} %reshape.115), calls=%async_computation | async-start | bytes 65536 | tf_op jit(solution)/shard_map/all_to_all | solution.py:183
  9.0 6.6 %all-to-all-done = s32[16,1,512]{2,1,0:T(1,128)S(1)} async-done(((s32[16,1,512]{2,1,0:T(1,128)}), s32[16,1,512]{2,1,0:T(1,128)S(1)}, u32[]{:S(2)}, u32[]{:S(2)}) %all-to-all-start) | async-done | bytes 32800 | tf_op jit(solution)/shard_map/all_to_all | solution.py:183
  16.2 0.7 reduce
  17.7 4.4 %gather_fusion = f32[128,64,128]{2,1,0:T(8,128)} fusion(f32[64,64,128]{2,1,0:T(8,128)} %refs_2_.1, s32[1024]{0:T(1024)S(1)} %pad_clamp_fusion.1), kind=kCustom, calls=%fused_computation | custom fusion | bytes 8389120 | tf_op jit(solution)/shard_map/gather | solution.py:223
  22.1 4.7 %all-to-all-start.2 = ((f32[16,512,128]{2,1,0:T(8,128)}), f32[16,512,128]{2,1,0:T(8,128)}, u32[]{:S(2)}, u32[]{:S(2)}) async-start(f32[16,512,128]{2,1,0:T(8,128)} %bitcast.17), calls=%async_computation.2 | async-start | bytes 8388608 | tf_op jit(solution)/shard_map/all_to_all | solution.py:183
  26.8 10.6 %table.2 = (bf16[2048,1024]{1,0:T(8,128)(2,1)}, bf16[2048,1024]{1,0:T(8,128)(2,1)}) custom-call(f32[2,1024,512]{2,1,0:T(8,128)} %table.3), custom_call_target="tpu_custom_call" | custom-call | tf_op jit(solution)/shard_map/table/pallas_call | solution.py:68
  38.0 0.8 copy.17
  38.8 9.3 %interpolate.2 = f32[2048,128]{1,0:T(8,128)} custom-call(f32[256,8]{1,0:T(8,128)} %bitcast.20, f32[8,1024]{1,0:T(8,128)} %pad_convert_fusion.refs_1_, bf16[2048,1024]{1,0:T(8,128)(2,1)} %get-tuple-element.7.refs_2_, bf16[2048,1024]{1,0:T(8,128)(2,1)} %get-tuple-element.8.refs_3_), custom_call_target="tpu_custom_call" | custom-call | tf_op jit(solution)/shard_map/interpolate/pallas_call | solution.py:95
  48.1 56.2 %all-to-all-done.2 = f32[16,512,128]{2,1,0:T(8,128)} async-done(((f32[16,512,128]{2,1,0:T(8,128)}), f32[16,512,128]{2,1,0:T(8,128)}, u32[]{:S(2)}, u32[]{:S(2)}) %all-to-all-start.2) | async-done | bytes 4194336 | tf_op jit(solution)/shard_map/all_to_all | solution.py:183
  104.2 19.6 %all-to-all-start.1 = ((f32[16,128,128]{2,1,0:T(8,128)}), f32[16,128,128]{2,1,0:T(8,128)S(1)}, u32[]{:S(2)}, u32[]{:S(2)}) async-start(f32[16,128,128]{2,1,0:T(8,128)} %bitcast.18), calls=%async_computation.1 | async-start | bytes 2097152 | tf_op jit(solution)/shard_map/all_to_all | solution.py:183
  123.9 0.9 copy.19
  124.9 18.6 %interpolate.3 = f32[6144,128]{1,0:T(8,128)} custom-call(f32[768,8]{1,0:T(8,128)} %bitcast.19, f32[8,1024]{1,0:T(8,128)} %pad_convert_fusion.refs_1_, bf16[2048,1024]{1,0:T(8,128)(2,1)} %get-tuple-element.7.refs_2_, bf16[2048,1024]{1,0:T(8,128)(2,1)} %get-tuple-element.8.refs_3_), custom_call_target="tpu_custom_call" | custom-call | tf_op jit(solution)/shard_map/interpolate/pallas_call | solution.py:95
  143.5 2.8 %fusion.5 = (f32[384,128]{1,0:T(8,128)S(1)}, f32[384,128]{1,0:T(8,128)S(1)}, f32[384,128]{1,0:T(8,128)S(1)}, f32[384,128]{1,0:T(8,128)S(1)}, f32[384,128]{1,0:T(...) fusion(f32[6144,128]{1,0:T(8,128)} %interpolate.3), kind=kLoop, calls=%fused_computation.22 | loop fusion | bytes 6291456 | tf_op jit(solution)/shard_map/slice | solution.py:241
  146.3 4.3 %collective-permute-start.14 = (f32[384,128]{1,0:T(8,128)S(1)}, f32[384,128]{1,0:T(8,128)S(1)}, u32[]{:S(2)}, u32[]{:S(2)}) collective-permute-start(f32[384,128]{1,0:T(8,128)S(1)} %get-tuple-element.11), channel_id=1, source_target_pairs={{0,15},{1,0},{2,1},{3,2},{4,3},{5,4},{6,5},{7,6},{8,7},{9,8},{10,9... | collective-permute-start | bytes 589832 | tf_op jit(solution)/shard_map/ppermute | solution.py:199
  152.2 3.8 %collective-permute-done.14.refs_16_ = f32[384,128]{1,0:T(8,128)S(1)} collective-permute-done((f32[384,128]{1,0:T(8,128)S(1)}, f32[384,128]{1,0:T(8,128)S(1)}, u32[]{:S(2)}, u32[]{:S(2)}) %collective-permute-start.14) | collective-permute-done | bytes 196640 | tf_op jit(solution)/shard_map/ppermute | solution.py:199
  156.5 3.7 %collective-permute-done.13.refs_15_ = f32[384,128]{1,0:T(8,128)S(1)} collective-permute-done((f32[384,128]{1,0:T(8,128)S(1)}, f32[384,128]{1,0:T(8,128)S(1)}, u32[]{:S(2)}, u32[]{:S(2)}) %collective-permute-start.13) | collective-permute-done | bytes 196640 | tf_op jit(solution)/shard_map/ppermute | solution.py:199
  160.2 4.2 %collective-permute-done.12.refs_14_ = f32[384,128]{1,0:T(8,128)S(1)} collective-permute-done((f32[384,128]{1,0:T(8,128)S(1)}, f32[384,128]{1,0:T(8,128)S(1)}, u32[]{:S(2)}, u32[]{:S(2)}) %collective-permute-start.12) | collective-permute-done | bytes 196640 | tf_op jit(solution)/shard_map/ppermute | solution.py:199
  164.4 4.2 %collective-permute-done.11.refs_13_ = f32[384,128]{1,0:T(8,128)S(1)} collective-permute-done((f32[384,128]{1,0:T(8,128)S(1)}, f32[384,128]{1,0:T(8,128)S(1)}, u32[]{:S(2)}, u32[]{:S(2)}) %collective-permute-start.11) | collective-permute-done | bytes 196640 | tf_op jit(solution)/shard_map/ppermute | solution.py:199
  168.7 4.2 %collective-permute-done.10.refs_12_ = f32[384,128]{1,0:T(8,128)S(1)} collective-permute-done((f32[384,128]{1,0:T(8,128)S(1)}, f32[384,128]{1,0:T(8,128)S(1)}, u32[]{:S(2)}, u32[]{:S(2)}) %collective-permute-start.10) | collective-permute-done | bytes 196640 | tf_op jit(solution)/shard_map/ppermute | solution.py:199
  172.9 0.7 copy-done.5
  173.9 3.2 %collective-permute-done.9.refs_11_ = f32[384,128]{1,0:T(8,128)} collective-permute-done((f32[384,128]{1,0:T(8,128)S(1)}, f32[384,128]{1,0:T(8,128)}, u32[]{:S(2)}, u32[]{:S(2)}) %collective-permute-start.9) | collective-permute-done | bytes 196640 | tf_op jit(solution)/shard_map/ppermute | solution.py:199
  177.1 13.7 %collective-permute-start.4 = (f32[384,128]{1,0:T(8,128)S(1)}, f32[384,128]{1,0:T(8,128)S(1)}, u32[]{:S(2)}, u32[]{:S(2)}) collective-permute-start(f32[384,128]{1,0:T(8,128)S(1)} %get-tuple-element.21), channel_id=1, source_target_pairs={{0,5},{1,6},{2,7},{3,8},{4,9},{5,10},{6,11},{7,12},{8,13},{9,14},{... | collective-permute-start | bytes 589832 | tf_op jit(solution)/shard_map/ppermute | solution.py:199
  190.8 8.6 %collective-permute-start.3 = (f32[384,128]{1,0:T(8,128)S(1)}, f32[384,128]{1,0:T(8,128)S(1)}, u32[]{:S(2)}, u32[]{:S(2)}) collective-permute-start(f32[384,128]{1,0:T(8,128)S(1)} %get-tuple-element.22), channel_id=1, source_target_pairs={{0,4},{1,5},{2,6},{3,7},{4,8},{5,9},{6,10},{7,11},{8,12},{9,13},{1... | collective-permute-start | bytes 589832 | tf_op jit(solution)/shard_map/ppermute | solution.py:199
  199.3 17.8 %collective-permute-done.7.refs_9_ = f32[384,128]{1,0:T(8,128)} collective-permute-done((f32[384,128]{1,0:T(8,128)S(1)}, f32[384,128]{1,0:T(8,128)}, u32[]{:S(2)}, u32[]{:S(2)}) %collective-permute-start.7) | collective-permute-done | bytes 196640 | tf_op jit(solution)/shard_map/ppermute | solution.py:199
  217.3 4.2 %gather_fusion.1 = f32[64,64,128]{2,1,0:T(8,128)} fusion(f32[128,64,128]{2,1,0:T(8,128)} %bitcast.10, s32[1024]{0:T(1024)S(1)} %pad_clamp_fusion), kind=kCustom, calls=%fused_computation.1 | custom fusion | bytes 4194560 | tf_op jit(solution)/shard_map/gather | solution.py:229
  221.5 2.5 %collective-permute-done.2.refs_4_ = f32[384,128]{1,0:T(8,128)S(1)} collective-permute-done((f32[384,128]{1,0:T(8,128)S(1)}, f32[384,128]{1,0:T(8,128)S(1)}, u32[]{:S(2)}, u32[]{:S(2)}) %collective-permute-start.2) | collective-permute-done | bytes 196640 | tf_op jit(solution)/shard_map/ppermute | solution.py:199
  224.1 3.1 %collective-permute-done.1.refs_3_ = f32[384,128]{1,0:T(8,128)S(1)} collective-permute-done((f32[384,128]{1,0:T(8,128)S(1)}, f32[384,128]{1,0:T(8,128)S(1)}, u32[]{:S(2)}, u32[]{:S(2)}) %collective-permute-start.1) | collective-permute-done | bytes 196640 | tf_op jit(solution)/shard_map/ppermute | solution.py:199
  227.9 10.2 %rotate.2.refs_4_ = f32[64,2,64,128]{3,2,1,0:T(8,128)} custom-call(s32[1]{0:T(128)} %bitcast.refs_0_, f32[384,128]{1,0:T(8,128)} %get-tuple-element.26.refs_1_, f32[384,128]{1,0:T(8,128)} %copy-done.10, f32[384,128]{1,0:T(8,128)} %copy-done.9, f32[384,128]{1,0:T(8,128)} %copy-done.8, f32[384,128]{1,0:T(8,128)} %copy-done.7, f32[384,128]{1,0:T(8,128)} %copy-done.6, ...), custom_call_target="tpu_custom_call" | custom-call | tf_op jit(solution)/shard_map/rotate/pallas_call | solution.py:160
  238.1 1.0 copy-done
  239.1 4.5 %rotate.3 = f32[64,2,64,128]{3,2,1,0:T(8,128)} custom-call(s32[1]{0:T(128)} %bitcast.refs_0_, f32[16,128,128]{2,1,0:T(8,128)} %copy-done, f32[64,64,128]{2,1,0:T(8,128)} %refs_2_.1, f32[64,64,128]{2,1,0:T(8,128)} %gather_fusion.1, f32[64,2,64,128]{3,2,1,0:T(8,128)} %rotate.2.refs_4_), custom_call_target="tpu_custom_call", output_to_operand_aliasing={{}: (4, {})} | custom-call | tf_op jit(solution)/shard_map/rotate/pallas_call | solution.py:160
  (65 shorter events, 5.3 us)
Async XLA Ops:
  1.6 14.1 %all-to-all-start = ((s32[16,1,512]{2,1,0:T(1,128)}), s32[16,1,512]{2,1,0:T(1,128)S(1)}, u32[]{:S(2)}, u32[]{:S(2)}) async-start(s32[16,1,512]{2,1,0:T(1,128)} %reshape.115), calls=%async_computation | async-start | bytes 65536 | tf_op jit(solution)/shard_map/all_to_all | solution.py:183
  22.1 15.3 %copy-start.11 = (s32[3,1024]{1,0:T(4,128)S(1)}, s32[3,1024]{1,0:T(4,128)}, u32[]{:S(2)}) copy-start(s32[3,1024]{1,0:T(4,128)} %param.7) | copy-start | bytes 36868
  22.1 82.2 %all-to-all-start.2 = ((f32[16,512,128]{2,1,0:T(8,128)}), f32[16,512,128]{2,1,0:T(8,128)}, u32[]{:S(2)}, u32[]{:S(2)}) async-start(f32[16,512,128]{2,1,0:T(8,128)} %bitcast.17), calls=%async_computation.2 | async-start | bytes 8388608 | tf_op jit(solution)/shard_map/all_to_all | solution.py:183
  104.2 133.8 %all-to-all-start.1 = ((f32[16,128,128]{2,1,0:T(8,128)}), f32[16,128,128]{2,1,0:T(8,128)S(1)}, u32[]{:S(2)}, u32[]{:S(2)}) async-start(f32[16,128,128]{2,1,0:T(8,128)} %bitcast.18), calls=%async_computation.1 | async-start | bytes 2097152 | tf_op jit(solution)/shard_map/all_to_all | solution.py:183
  143.5 30.1 %copy-start.12 = (s32[64]{0:T(128)S(1)}, s32[64]{0:T(128)}, u32[]{:S(2)}) copy-start(s32[64]{0:T(128)} %param.10) | copy-start | bytes 772
  146.3 9.7 %collective-permute-start.14 = (f32[384,128]{1,0:T(8,128)S(1)}, f32[384,128]{1,0:T(8,128)S(1)}, u32[]{:S(2)}, u32[]{:S(2)}) collective-permute-start(f32[384,128]{1,0:T(8,128)S(1)} %get-tuple-element.11), channel_id=1, source_target_pairs={{0,15},{1,0},{2,1},{3,2},{4,3},{5,4},{6,5},{7,6},{8,7},{9,8},{10,9... | collective-permute-start | bytes 589832 | tf_op jit(solution)/shard_map/ppermute | solution.py:199
  150.7 9.5 %collective-permute-start.13 = (f32[384,128]{1,0:T(8,128)S(1)}, f32[384,128]{1,0:T(8,128)S(1)}, u32[]{:S(2)}, u32[]{:S(2)}) collective-permute-start(f32[384,128]{1,0:T(8,128)S(1)} %get-tuple-element.12), channel_id=1, source_target_pairs={{0,14},{1,15},{2,0},{3,1},{4,2},{5,3},{6,4},{7,5},{8,6},{9,7},{10,... | collective-permute-start | bytes 589832 | tf_op jit(solution)/shard_map/ppermute | solution.py:199
  151.2 13.2 %collective-permute-start.12 = (f32[384,128]{1,0:T(8,128)S(1)}, f32[384,128]{1,0:T(8,128)S(1)}, u32[]{:S(2)}, u32[]{:S(2)}) collective-permute-start(f32[384,128]{1,0:T(8,128)S(1)} %get-tuple-element.13), channel_id=1, source_target_pairs={{0,13},{1,14},{2,15},{3,0},{4,1},{5,2},{6,3},{7,4},{8,5},{9,6},{10... | collective-permute-start | bytes 589832 | tf_op jit(solution)/shard_map/ppermute | solution.py:199
  151.4 17.3 %collective-permute-start.11 = (f32[384,128]{1,0:T(8,128)S(1)}, f32[384,128]{1,0:T(8,128)S(1)}, u32[]{:S(2)}, u32[]{:S(2)}) collective-permute-start(f32[384,128]{1,0:T(8,128)S(1)} %get-tuple-element.14), channel_id=1, source_target_pairs={{0,12},{1,13},{2,14},{3,15},{4,0},{5,1},{6,2},{7,3},{8,4},{9,5},{1... | collective-permute-start | bytes 589832 | tf_op jit(solution)/shard_map/ppermute | solution.py:199
  151.9 20.9 %collective-permute-start.10 = (f32[384,128]{1,0:T(8,128)S(1)}, f32[384,128]{1,0:T(8,128)S(1)}, u32[]{:S(2)}, u32[]{:S(2)}) collective-permute-start(f32[384,128]{1,0:T(8,128)S(1)} %get-tuple-element.15), channel_id=1, source_target_pairs={{0,11},{1,12},{2,13},{3,14},{4,15},{5,0},{6,1},{7,2},{8,3},{9,4},{... | collective-permute-start | bytes 589832 | tf_op jit(solution)/shard_map/ppermute | solution.py:199
  156.0 71.1 %copy-start.1 = (f32[384,128]{1,0:T(8,128)}, f32[384,128]{1,0:T(8,128)S(1)}, u32[]{:S(2)}) copy-start(f32[384,128]{1,0:T(8,128)S(1)} %collective-permute-done.14.refs_16_) | copy-start | bytes 589828
  156.0 21.1 %collective-permute-start.9 = (f32[384,128]{1,0:T(8,128)S(1)}, f32[384,128]{1,0:T(8,128)}, u32[]{:S(2)}, u32[]{:S(2)}) collective-permute-start(f32[384,128]{1,0:T(8,128)S(1)} %get-tuple-element.16), channel_id=1, source_target_pairs={{0,10},{1,11},{2,12},{3,13},{4,14},{5,15},{6,0},{7,1},{8,2},{9,3},... | collective-permute-start | bytes 589832 | tf_op jit(solution)/shard_map/ppermute | solution.py:199
  160.2 66.9 %copy-start.2 = (f32[384,128]{1,0:T(8,128)}, f32[384,128]{1,0:T(8,128)S(1)}, u32[]{:S(2)}) copy-start(f32[384,128]{1,0:T(8,128)S(1)} %collective-permute-done.13.refs_15_) | copy-start | bytes 589828
  160.2 30.6 %collective-permute-start.8 = (f32[384,128]{1,0:T(8,128)S(1)}, f32[384,128]{1,0:T(8,128)}, u32[]{:S(2)}, u32[]{:S(2)}) collective-permute-start(f32[384,128]{1,0:T(8,128)S(1)} %get-tuple-element.17), channel_id=1, source_target_pairs={{0,9},{1,10},{2,11},{3,12},{4,13},{5,14},{6,15},{7,0},{8,1},{9,2},... | collective-permute-start | bytes 589832 | tf_op jit(solution)/shard_map/ppermute | solution.py:199
  164.4 8.4 %copy-start.3 = (f32[384,128]{1,0:T(8,128)}, f32[384,128]{1,0:T(8,128)S(1)}, u32[]{:S(2)}) copy-start(f32[384,128]{1,0:T(8,128)S(1)} %collective-permute-done.12.refs_14_) | copy-start | bytes 589828
  164.4 52.7 %collective-permute-start.7 = (f32[384,128]{1,0:T(8,128)S(1)}, f32[384,128]{1,0:T(8,128)}, u32[]{:S(2)}, u32[]{:S(2)}) collective-permute-start(f32[384,128]{1,0:T(8,128)S(1)} %get-tuple-element.18), channel_id=1, source_target_pairs={{0,8},{1,9},{2,10},{3,11},{4,12},{5,13},{6,14},{7,15},{8,0},{9,1},... | collective-permute-start | bytes 589832 | tf_op jit(solution)/shard_map/ppermute | solution.py:199
  168.7 4.2 %copy-start.4 = (f32[384,128]{1,0:T(8,128)}, f32[384,128]{1,0:T(8,128)S(1)}, u32[]{:S(2)}) copy-start(f32[384,128]{1,0:T(8,128)S(1)} %collective-permute-done.11.refs_13_) | copy-start | bytes 589828
  168.7 48.5 %collective-permute-start.6 = (f32[384,128]{1,0:T(8,128)S(1)}, f32[384,128]{1,0:T(8,128)}, u32[]{:S(2)}, u32[]{:S(2)}) collective-permute-start(f32[384,128]{1,0:T(8,128)S(1)} %get-tuple-element.19), channel_id=1, source_target_pairs={{0,7},{1,8},{2,9},{3,10},{4,11},{5,12},{6,13},{7,14},{8,15},{9,0},... | collective-permute-start | bytes 589832 | tf_op jit(solution)/shard_map/ppermute | solution.py:199
  172.9 0.7 copy-start.5
  173.6 43.6 %collective-permute-start.5 = (f32[384,128]{1,0:T(8,128)S(1)}, f32[384,128]{1,0:T(8,128)}, u32[]{:S(2)}, u32[]{:S(2)}) collective-permute-start(f32[384,128]{1,0:T(8,128)S(1)} %get-tuple-element.20), channel_id=1, source_target_pairs={{0,6},{1,7},{2,8},{3,9},{4,10},{5,11},{6,12},{7,13},{8,14},{9,15},... | collective-permute-start | bytes 589832 | tf_op jit(solution)/shard_map/ppermute | solution.py:199
  177.1 44.4 %collective-permute-start.4 = (f32[384,128]{1,0:T(8,128)S(1)}, f32[384,128]{1,0:T(8,128)S(1)}, u32[]{:S(2)}, u32[]{:S(2)}) collective-permute-start(f32[384,128]{1,0:T(8,128)S(1)} %get-tuple-element.21), channel_id=1, source_target_pairs={{0,5},{1,6},{2,7},{3,8},{4,9},{5,10},{6,11},{7,12},{8,13},{9,14},{... | collective-permute-start | bytes 589832 | tf_op jit(solution)/shard_map/ppermute | solution.py:199
  190.8 30.7 %collective-permute-start.3 = (f32[384,128]{1,0:T(8,128)S(1)}, f32[384,128]{1,0:T(8,128)S(1)}, u32[]{:S(2)}, u32[]{:S(2)}) collective-permute-start(f32[384,128]{1,0:T(8,128)S(1)} %get-tuple-element.22), channel_id=1, source_target_pairs={{0,4},{1,5},{2,6},{3,7},{4,8},{5,9},{6,10},{7,11},{8,12},{9,13},{1... | collective-permute-start | bytes 589832 | tf_op jit(solution)/shard_map/ppermute | solution.py:199
  217.2 6.9 %collective-permute-start.2 = (f32[384,128]{1,0:T(8,128)S(1)}, f32[384,128]{1,0:T(8,128)S(1)}, u32[]{:S(2)}, u32[]{:S(2)}) collective-permute-start(f32[384,128]{1,0:T(8,128)S(1)} %get-tuple-element.23), channel_id=1, source_target_pairs={{0,3},{1,4},{2,5},{3,6},{4,7},{5,8},{6,9},{7,10},{8,11},{9,12},{10... | collective-permute-start | bytes 589832 | tf_op jit(solution)/shard_map/ppermute | solution.py:199
  217.2 10.0 %collective-permute-start.1 = (f32[384,128]{1,0:T(8,128)S(1)}, f32[384,128]{1,0:T(8,128)S(1)}, u32[]{:S(2)}, u32[]{:S(2)}) collective-permute-start(f32[384,128]{1,0:T(8,128)S(1)} %get-tuple-element.24), channel_id=1, source_target_pairs={{0,2},{1,3},{2,4},{3,5},{4,6},{5,7},{6,8},{7,9},{8,10},{9,11},{10,... | collective-permute-start | bytes 589832 | tf_op jit(solution)/shard_map/ppermute | solution.py:199
  217.2 10.0 %collective-permute-start = (f32[384,128]{1,0:T(8,128)S(1)}, f32[384,128]{1,0:T(8,128)S(1)}, u32[]{:S(2)}, u32[]{:S(2)}) collective-permute-start(f32[384,128]{1,0:T(8,128)S(1)} %get-tuple-element.25), channel_id=1, source_target_pairs={{0,1},{1,2},{2,3},{3,4},{4,5},{5,6},{6,7},{7,8},{8,9},{9,10},{10,1... | collective-permute-start | bytes 589832 | tf_op jit(solution)/shard_map/ppermute | solution.py:199
  221.5 5.7 %copy-start.6 = (f32[384,128]{1,0:T(8,128)}, f32[384,128]{1,0:T(8,128)S(1)}, u32[]{:S(2)}) copy-start(f32[384,128]{1,0:T(8,128)S(1)} %collective-permute-done.4.refs_6_) | copy-start | bytes 589828
  221.5 5.7 %copy-start.7 = (f32[384,128]{1,0:T(8,128)}, f32[384,128]{1,0:T(8,128)S(1)}, u32[]{:S(2)}) copy-start(f32[384,128]{1,0:T(8,128)S(1)} %collective-permute-done.3.refs_5_) | copy-start | bytes 589828
  224.1 3.1 %copy-start.8 = (f32[384,128]{1,0:T(8,128)}, f32[384,128]{1,0:T(8,128)S(1)}, u32[]{:S(2)}) copy-start(f32[384,128]{1,0:T(8,128)S(1)} %collective-permute-done.2.refs_4_) | copy-start | bytes 589828
  227.1 0.7 copy-start.9
  227.1 0.7 copy-start.10
  238.1 1.0 copy-start
where the time goes:
time: 244 us
  waiting for transfers between devices  110 us (45%)
  starting transfers between devices  60.4 us (25%)
  Pallas kernels  53.2 us (22%)
  local copies, waits for them, and re-layouts  17.1 us (7%)
  other arithmetic  3.11 us (1%)
    all_to_all x3, waiting for transfers between devices, exchange(): return lax.all_to_all(x, 'ka', split_axis=0, concat_axis=0, tiled=True)  62.8 us
    ppermute x15, waiting for transfers between devices, spread(): lax.ppermute(blocks(s), 'ka', [(d, (d + s) % devices) for d in range(devi...  46.7 us
    all_to_all x3, starting transfers between devices, exchange(): return lax.all_to_all(x, 'ka', split_axis=0, concat_axis=0, tiled=True)  31.7 us
    ppermute x15, starting transfers between devices, spread(): lax.ppermute(blocks(s), 'ka', [(d, (d + s) % devices) for d in range(devi...  28.7 us
    pallas_call x2, Pallas kernels, interpolate(): pl.pallas_call(lambda *refs: interpolate_kernel(*refs, mrows=mrows), out_...  27.9 us
    pallas_call x2, Pallas kernels, rotate(): pl.pallas_call(lambda *refs: rotate_kernel(*refs, block=block, mrows=mrow...  14.7 us
    pallas_call x1, Pallas kernels, prepare_table(): pl.pallas_call(table_kernel, out_shape=[jax.ShapeDtypeStruct((2 * vectors...  10.6 us
  transfers between devices with their start and end apart: 18, of which 11 were waited for; matrix products, arithmetic and copies ran while one was open for 4% of the time, Pallas kernels for 20%

commit v1 on v0

--- a/solution.py
+++ b/solution.py
@@ -212,21 +212,38 @@
     tiled = mrows % 8 == 0
     by_shift = devices <= SHIFTED and tiled
 
+    half = devices // 2
+    base = me // half * half
+    away = lax.rem(me + half, devices)
+    groups = [list(range(half)), list(range(half, devices))]
+
+    mirrored = lax.ppermute(eigen_vectors, "ka", [(d, (d + half) % devices) for d in range(devices)])
     own = jnp.concatenate(
         [kpoint_grid, target_owner[None], target_slot[None], jnp.zeros((3, kpoints), jnp.int32)], 0
     )
     known = exchange(jnp.broadcast_to(own[None], (devices, 8, kpoints)))
-    asked = known[:, 3] == me
-    position = jnp.cumsum(asked.astype(jnp.int32), 1) - 1
-    chosen = asked[:, None, :] & (position[:, None, :] == jnp.arange(capacity)[None, :, None])
-    wanted = jnp.sum(jnp.where(chosen, known[:, 4][:, None, :], 0), 2)
-    picked = eigen_vectors[wanted.reshape(-1)].reshape(devices, capacity * orbitals, lanes)
-    fetched = exchange(picked).reshape(devices * capacity, orbitals, lanes)
+    near_known = lax.dynamic_slice_in_dim(known, base, half, 0)
+
+    def serve(held, owner):
+        asked = near_known[:, 3] == owner
+        position = jnp.cumsum(asked.astype(jnp.int32), 1) - 1
+        chosen = asked[:, None, :] & (position[:, None, :] == jnp.arange(capacity)[None, :, None])
+        wanted = jnp.sum(jnp.where(chosen, near_known[:, 4][:, None, :], 0), 2)
+        picked = held[wanted.reshape(-1)].reshape(half, capacity * orbitals, lanes)
+        got = lax.all_to_all(
+            picked, "ka", split_axis=0, concat_axis=0, tiled=True, axis_index_groups=groups
+        )
+        return got.reshape(half * capacity, orbitals, lanes)
+
+    from_near = serve(eigen_vectors, me)
+    from_far = serve(mirrored, away)
     high, low = prepare_table(wannier_table)
 
     owners = (target_owner[:, None] == jnp.arange(devices, dtype=jnp.int32)[None, :]).astype(jnp.int32)
     before = jnp.cumsum(owners, 0) - owners
-    far = fetched[target_owner * capacity + jnp.sum(before * owners, 1)]
+    at = lax.rem(target_owner, half) * capacity + jnp.sum(before * owners, 1)
+    is_near = target_owner // half == me // half
+    far = jnp.concatenate([from_near, from_far], 0)[jnp.where(is_near, at, at + half * capacity)]
 
     grid_rows = known.transpose(0, 2, 1).astype(jnp.float32)
     turned_rows = lax.dynamic_slice_in_dim(jnp.concatenate([grid_rows, grid_rows], 0), me, devices, 0)

time: 244 us -> 277 us (1.14)
  the two profiles are of different devices: /device:TPU:0 before, /device:TPU:9 now
where the time goes in v1:
time: 277 us; the launch traced here: 273 us
  waiting for transfers between devices  115 us (42%)
  starting transfers between devices  75.6 us (27%)
  Pallas kernels  53.1 us (19%)
  local copies, waits for them, and re-layouts  19.2 us (7%)
  other arithmetic  10.2 us (4%)
    ppermute x1, waiting for transfers between devices, placed_local(): lax.ppermute(eigen_vectors, 'ka', [(d, (d + half) % devices) for d in ran...  89.5 us
    ppermute x15, starting transfers between devices, spread(): lax.ppermute(blocks(s), 'ka', [(d, (d + s) % devices) for d in range(devi...  49.7 us
    pallas_call x2, Pallas kernels, interpolate(): pl.pallas_call(lambda *refs: interpolate_kernel(*refs, mrows=mrows), out_...  27.9 us
    ppermute x15, waiting for transfers between devices, spread(): lax.ppermute(blocks(s), 'ka', [(d, (d + s) % devices) for d in range(devi...  17.9 us
    pallas_call x2, Pallas kernels, rotate(): pl.pallas_call(lambda *refs: rotate_kernel(*refs, block=block, mrows=mrow...  14.7 us
    all_to_all x2, starting transfers between devices, serve(): lax.all_to_all(picked, 'ka', split_axis=0, concat_axis=0, tiled=True, axi...  13.9 us
    all_to_all x2, starting transfers between devices, exchange(): return lax.all_to_all(x, 'ka', split_axis=0, concat_axis=0, tiled=True)  11.9 us
    pallas_call x1, Pallas kernels, prepare_table(): pl.pallas_call(table_kernel, out_shape=[jax.ShapeDtypeStruct((2 * vectors...  10.5 us
  transfers between devices with their start and end apart: 20, of which 5 were waited for; matrix products, arithmetic and copies ran while one was open for 8% of the time, Pallas kernels for 18%

profile of v1, /device:TPU:9, one launch (start us, length us, event | category | flops | bytes accessed | tf_op | source)
XLA Modules:
  0.0 273.5 jit_solution(602403030803972137)
XLA Ops:
  1.6 6.6 %all-to-all-start = ((s32[16,1,512]{2,1,0:T(1,128)}), s32[16,1,512]{2,1,0:T(1,128)S(1)}, u32[]{:S(2)}, u32[]{:S(2)}) async-start(s32[16,1,512]{2,1,0:T(1,128)} %reshape.170), calls=%async_computation | async-start | bytes 65536 | tf_op jit(solution)/shard_map/all_to_all | solution.py:183
  8.2 5.0 %all-to-all-done = s32[16,1,512]{2,1,0:T(1,128)S(1)} async-done(((s32[16,1,512]{2,1,0:T(1,128)}), s32[16,1,512]{2,1,0:T(1,128)S(1)}, u32[]{:S(2)}, u32[]{:S(2)}) %all-to-all-start) | async-done | bytes 32800 | tf_op jit(solution)/shard_map/all_to_all | solution.py:183
  15.5 3.6 %gather_fusion = f32[64,64,128]{2,1,0:T(8,128)} fusion(f32[64,64,128]{2,1,0:T(8,128)} %refs_2_.1, s32[1024]{0:T(1024)S(1)} %pad_clamp_fusion.2), kind=kCustom, calls=%fused_computation | custom fusion | bytes 4194560 | tf_op jit(solution)/shard_map/gather | solution.py:232
  19.1 6.1 %all-to-all-start.2 = ((f32[8,512,128]{2,1,0:T(8,128)}), f32[8,512,128]{2,1,0:T(8,128)}, u32[]{:S(2)}, u32[]{:S(2)}) async-start(f32[8,512,128]{2,1,0:T(8,128)} %bitcast.26), calls=%async_computation.2 | async-start | bytes 4194304 | tf_op jit(solution)/shard_map/all_to_all | solution.py:233
  25.3 89.5 %collective-permute-done = f32[64,64,128]{2,1,0:T(8,128)} collective-permute-done((f32[64,64,128]{2,1,0:T(8,128)S(1)}, f32[64,64,128]{2,1,0:T(8,128)}, u32[]{:S(2)}, u32[]{:S(2)}) %collective-permute-start) | collective-permute-done | bytes 2097184 | tf_op jit(solution)/shard_map/ppermute | solution.py:220
  114.8 3.6 %gather_fusion.1 = f32[64,64,128]{2,1,0:T(8,128)} fusion(f32[64,64,128]{2,1,0:T(8,128)} %collective-permute-done, s32[1024]{0:T(1024)S(1)} %pad_clamp_fusion.1), kind=kCustom, calls=%fused_computation.1 | custom fusion | bytes 4194560 | tf_op jit(solution)/shard_map/gather | solution.py:232
  118.4 7.8 %all-to-all-start.3 = ((f32[8,512,128]{2,1,0:T(8,128)}), f32[8,512,128]{2,1,0:T(8,128)S(1)}, u32[]{:S(2)}, u32[]{:S(2)}) async-start(f32[8,512,128]{2,1,0:T(8,128)} %bitcast.13), calls=%async_computation.3 | async-start | bytes 4194304 | tf_op jit(solution)/shard_map/all_to_all | solution.py:233
  126.3 10.5 %table.2 = (bf16[2048,1024]{1,0:T(8,128)(2,1)}, bf16[2048,1024]{1,0:T(8,128)(2,1)}) custom-call(f32[2,1024,512]{2,1,0:T(8,128)} %table.3), custom_call_target="tpu_custom_call" | custom-call | tf_op jit(solution)/shard_map/table/pallas_call | solution.py:68
  138.3 9.2 %interpolate.2 = f32[2048,128]{1,0:T(8,128)} custom-call(f32[256,8]{1,0:T(8,128)} %bitcast.30, f32[8,1024]{1,0:T(8,128)} %pad_convert_fusion.refs_1_, bf16[2048,1024]{1,0:T(8,128)(2,1)} %get-tuple-element.7.refs_2_, bf16[2048,1024]{1,0:T(8,128)(2,1)} %get-tuple-element.8.refs_3_), custom_call_target="tpu_custom_call" | custom-call | tf_op jit(solution)/shard_map/interpolate/pallas_call | solution.py:95
  147.5 2.6 all-to-all-done.3
  150.1 5.4 %all-to-all-start.1 = ((f32[16,128,128]{2,1,0:T(8,128)}), f32[16,128,128]{2,1,0:T(8,128)S(1)}, u32[]{:S(2)}, u32[]{:S(2)}) async-start(f32[16,128,128]{2,1,0:T(8,128)} %bitcast.28), calls=%async_computation.1 | async-start | bytes 2097152 | tf_op jit(solution)/shard_map/all_to_all | solution.py:183
  156.5 18.7 %interpolate.3 = f32[6144,128]{1,0:T(8,128)} custom-call(f32[768,8]{1,0:T(8,128)} %bitcast.29, f32[8,1024]{1,0:T(8,128)} %pad_convert_fusion.refs_1_, bf16[2048,1024]{1,0:T(8,128)(2,1)} %get-tuple-element.7.refs_2_, bf16[2048,1024]{1,0:T(8,128)(2,1)} %get-tuple-element.8.refs_3_), custom_call_target="tpu_custom_call" | custom-call | tf_op jit(solution)/shard_map/interpolate/pallas_call | solution.py:95
  175.1 3.5 %fusion.8 = (f32[384,128]{1,0:T(8,128)}, f32[384,128]{1,0:T(8,128)}, f32[384,128]{1,0:T(8,128)}, f32[384,128]{1,0:T(8,128)}, f32[384,128]{1,0:T(8,128)}, /*index...) fusion(f32[6144,128]{1,0:T(8,128)} %interpolate.3), kind=kLoop, calls=%fused_computation.40 | loop fusion | bytes 6291456 | tf_op jit(solution)/shard_map/slice | solution.py:258
  179.0 1.2 collective-permute-start.14
  180.2 4.4 %collective-permute-start.13 = (f32[384,128]{1,0:T(8,128)}, f32[384,128]{1,0:T(8,128)}, u32[]{:S(2)}, u32[]{:S(2)}) collective-permute-start(f32[384,128]{1,0:T(8,128)} %get-tuple-element.17), channel_id=1, source_target_pairs={{0,13},{1,14},{2,15},{3,0},{4,1},{5,2},{6,3},{7,4},{8,5},{9,6},{10... | collective-permute-start | bytes 589832 | tf_op jit(solution)/shard_map/ppermute | solution.py:199
  185.6 1.4 reduce_window_sum.36
  187.0 0.9 select_reduce_fusion
  188.0 4.3 %collective-permute-start.10 = (f32[384,128]{1,0:T(8,128)}, f32[384,128]{1,0:T(8,128)S(1)}, u32[]{:S(2)}, u32[]{:S(2)}) collective-permute-start(f32[384,128]{1,0:T(8,128)} %get-tuple-element.20), channel_id=1, source_target_pairs={{0,10},{1,11},{2,12},{3,13},{4,14},{5,15},{6,0},{7,1},{8,2},{9,3},... | collective-permute-start | bytes 589832 | tf_op jit(solution)/shard_map/ppermute | solution.py:199
  192.2 4.5 %collective-permute-start.9 = (f32[384,128]{1,0:T(8,128)}, f32[384,128]{1,0:T(8,128)S(1)}, u32[]{:S(2)}, u32[]{:S(2)}) collective-permute-start(f32[384,128]{1,0:T(8,128)} %get-tuple-element.21), channel_id=1, source_target_pairs={{0,9},{1,10},{2,11},{3,12},{4,13},{5,14},{6,15},{7,0},{8,1},{9,2},... | collective-permute-start | bytes 589832 | tf_op jit(solution)/shard_map/ppermute | solution.py:199
  196.8 3.0 %collective-permute-start.8 = (f32[384,128]{1,0:T(8,128)}, f32[384,128]{1,0:T(8,128)S(1)}, u32[]{:S(2)}, u32[]{:S(2)}) collective-permute-start(f32[384,128]{1,0:T(8,128)} %get-tuple-element.22), channel_id=1, source_target_pairs={{0,8},{1,9},{2,10},{3,11},{4,12},{5,13},{6,14},{7,15},{8,0},{9,1},... | collective-permute-start | bytes 589832 | tf_op jit(solution)/shard_map/ppermute | solution.py:199
  199.8 4.5 %collective-permute-start.7 = (f32[384,128]{1,0:T(8,128)}, f32[384,128]{1,0:T(8,128)S(1)}, u32[]{:S(2)}, u32[]{:S(2)}) collective-permute-start(f32[384,128]{1,0:T(8,128)} %get-tuple-element.23), channel_id=1, source_target_pairs={{0,7},{1,8},{2,9},{3,10},{4,11},{5,12},{6,13},{7,14},{8,15},{9,0},... | collective-permute-start | bytes 589832 | tf_op jit(solution)/shard_map/ppermute | solution.py:199
  204.3 3.8 %collective-permute-start.6 = (f32[384,128]{1,0:T(8,128)}, f32[384,128]{1,0:T(8,128)S(1)}, u32[]{:S(2)}, u32[]{:S(2)}) collective-permute-start(f32[384,128]{1,0:T(8,128)} %get-tuple-element.24), channel_id=1, source_target_pairs={{0,6},{1,7},{2,8},{3,9},{4,10},{5,11},{6,12},{7,13},{8,14},{9,15},... | collective-permute-start | bytes 589832 | tf_op jit(solution)/shard_map/ppermute | solution.py:199
  208.1 13.7 %collective-permute-done.10.refs_11_ = f32[384,128]{1,0:T(8,128)S(1)} collective-permute-done((f32[384,128]{1,0:T(8,128)}, f32[384,128]{1,0:T(8,128)S(1)}, u32[]{:S(2)}, u32[]{:S(2)}) %collective-permute-start.10) | collective-permute-done | bytes 196640 | tf_op jit(solution)/shard_map/ppermute | solution.py:199
  221.8 4.2 %collective-permute-done.9.refs_10_ = f32[384,128]{1,0:T(8,128)S(1)} collective-permute-done((f32[384,128]{1,0:T(8,128)}, f32[384,128]{1,0:T(8,128)S(1)}, u32[]{:S(2)}, u32[]{:S(2)}) %collective-permute-start.9) | collective-permute-done | bytes 196640 | tf_op jit(solution)/shard_map/ppermute | solution.py:199
  226.0 6.5 %collective-permute-start.4 = (f32[384,128]{1,0:T(8,128)}, f32[384,128]{1,0:T(8,128)}, u32[]{:S(2)}, u32[]{:S(2)}) collective-permute-start(f32[384,128]{1,0:T(8,128)} %get-tuple-element.26), channel_id=1, source_target_pairs={{0,4},{1,5},{2,6},{3,7},{4,8},{5,9},{6,10},{7,11},{8,12},{9,13},{1... | collective-permute-start | bytes 589832 | tf_op jit(solution)/shard_map/ppermute | solution.py:199
  232.5 15.3 %collective-permute-start.3 = (f32[384,128]{1,0:T(8,128)}, f32[384,128]{1,0:T(8,128)}, u32[]{:S(2)}, u32[]{:S(2)}) collective-permute-start(f32[384,128]{1,0:T(8,128)} %get-tuple-element.27), channel_id=1, source_target_pairs={{0,3},{1,4},{2,5},{3,6},{4,7},{5,8},{6,9},{7,10},{8,11},{9,12},{10... | collective-permute-start | bytes 589832 | tf_op jit(solution)/shard_map/ppermute | solution.py:199
  247.9 1.5 collective-permute-start.1
  249.4 4.1 %pad_maximum_fusion = f32[128,64,128]{2,1,0:T(8,128)} fusion(f32[64,64,128]{2,1,0:T(8,128)S(1)} %bitcast.27, f32[64,64,128]{2,1,0:T(8,128)} %bitcast.10), kind=kLoop, calls=%fused_computation.3 | loop fusion | flops 1048576 | bytes 8388608 | tf_op jit(solution)/shard_map/concatenate | solution.py:246
  253.5 4.2 %gather_fusion.2 = f32[64,64,128]{2,1,0:T(8,128)} fusion(f32[128,64,128]{2,1,0:T(8,128)} %pad_maximum_fusion, s32[1024]{0:T(1024)S(1)} %pad_clamp_fusion), kind=kCustom, calls=%fused_computation.2 | custom fusion | bytes 4194560 | tf_op jit(solution)/shard_map/gather | solution.py:246
  257.8 10.2 %rotate.2.refs_4_ = f32[64,2,64,128]{3,2,1,0:T(8,128)} custom-call(s32[1]{0:T(128)} %bitcast.refs_0_, f32[384,128]{1,0:T(8,128)} %get-tuple-element.30.refs_1_, f32[384,128]{1,0:T(8,128)} %collective-permute-done.1.refs_2_, f32[384,128]{1,0:T(8,128)} %collective-permute-done.2.refs_3_, f32[384,128]{1,0:T(8,128)} %collective-permute-done.3.refs_4_, ...), custom_call_target="tpu_custom_call" | custom-call | tf_op jit(solution)/shard_map/rotate/pallas_call | solution.py:160
  268.0 1.0 copy-done.1
  268.9 4.5 %rotate.3 = f32[64,2,64,128]{3,2,1,0:T(8,128)} custom-call(s32[1]{0:T(128)} %bitcast.refs_0_, f32[16,128,128]{2,1,0:T(8,128)} %copy-done.1, f32[64,64,128]{2,1,0:T(8,128)} %refs_2_.1, f32[64,64,128]{2,1,0:T(8,128)} %gather_fusion.2, f32[64,2,64,128]{3,2,1,0:T(8,128)} %rotate.2.refs_4_), custom_call_target="tpu_custom_call", output_to_operand_aliasing={{}: (4, {})} | custom-call | tf_op jit(solution)/shard_map/rotate/pallas_call | solution.py:160
  (67 shorter events, 7.9 us)
Async XLA Ops:
  1.6 11.6 %all-to-all-start = ((s32[16,1,512]{2,1,0:T(1,128)}), s32[16,1,512]{2,1,0:T(1,128)S(1)}, u32[]{:S(2)}, u32[]{:S(2)}) async-start(s32[16,1,512]{2,1,0:T(1,128)} %reshape.170), calls=%async_computation | async-start | bytes 65536 | tf_op jit(solution)/shard_map/all_to_all | solution.py:183
  19.1 6.1 %copy-start = (f32[64,64,128]{2,1,0:T(8,128)S(1)}, f32[64,64,128]{2,1,0:T(8,128)}, u32[]{:S(2)}) copy-start(f32[64,64,128]{2,1,0:T(8,128)} %refs_2_.1) | copy-start | bytes 6291460
  19.1 99.4 %all-to-all-start.2 = ((f32[8,512,128]{2,1,0:T(8,128)}), f32[8,512,128]{2,1,0:T(8,128)}, u32[]{:S(2)}, u32[]{:S(2)}) async-start(f32[8,512,128]{2,1,0:T(8,128)} %bitcast.26), calls=%async_computation.2 | async-start | bytes 4194304 | tf_op jit(solution)/shard_map/all_to_all | solution.py:233
  25.1 89.7 %collective-permute-start = (f32[64,64,128]{2,1,0:T(8,128)S(1)}, f32[64,64,128]{2,1,0:T(8,128)}, u32[]{:S(2)}, u32[]{:S(2)}) collective-permute-start(f32[64,64,128]{2,1,0:T(8,128)S(1)} %copy-done), channel_id=1, source_target_pairs={{0,8},{1,9},{2,10},{3,11},{4,12},{5,13},{6,14},{7,15},{8,0},{9,1},... | collective-permute-start | bytes 6291464 | tf_op jit(solution)/shard_map/ppermute | solution.py:220
  118.4 31.7 %all-to-all-start.3 = ((f32[8,512,128]{2,1,0:T(8,128)}), f32[8,512,128]{2,1,0:T(8,128)S(1)}, u32[]{:S(2)}, u32[]{:S(2)}) async-start(f32[8,512,128]{2,1,0:T(8,128)} %bitcast.13), calls=%async_computation.3 | async-start | bytes 4194304 | tf_op jit(solution)/shard_map/all_to_all | solution.py:233
  126.3 10.5 %copy-start.7 = (s32[3,1024]{1,0:T(4,128)S(1)}, s32[3,1024]{1,0:T(4,128)}, u32[]{:S(2)}) copy-start(s32[3,1024]{1,0:T(4,128)} %param.7) | copy-start | bytes 36868
  150.1 117.9 %all-to-all-start.1 = ((f32[16,128,128]{2,1,0:T(8,128)}), f32[16,128,128]{2,1,0:T(8,128)S(1)}, u32[]{:S(2)}, u32[]{:S(2)}) async-start(f32[16,128,128]{2,1,0:T(8,128)} %bitcast.28), calls=%async_computation.1 | async-start | bytes 2097152 | tf_op jit(solution)/shard_map/all_to_all | solution.py:183
  175.1 9.8 %copy-start.8 = (s32[64]{0:T(128)S(1)}, s32[64]{0:T(128)}, u32[]{:S(2)}) copy-start(s32[64]{0:T(128)} %param.10) | copy-start | bytes 772
  178.6 9.4 %collective-permute-start.15 = (f32[384,128]{1,0:T(8,128)}, f32[384,128]{1,0:T(8,128)}, u32[]{:S(2)}, u32[]{:S(2)}) collective-permute-start(f32[384,128]{1,0:T(8,128)} %get-tuple-element.15), channel_id=1, source_target_pairs={{0,15},{1,0},{2,1},{3,2},{4,3},{5,4},{6,5},{7,6},{8,7},{9,8},{10,9... | collective-permute-start | bytes 589832 | tf_op jit(solution)/shard_map/ppermute | solution.py:199
  179.0 13.2 %collective-permute-start.14 = (f32[384,128]{1,0:T(8,128)}, f32[384,128]{1,0:T(8,128)}, u32[]{:S(2)}, u32[]{:S(2)}) collective-permute-start(f32[384,128]{1,0:T(8,128)} %get-tuple-element.16), channel_id=1, source_target_pairs={{0,14},{1,15},{2,0},{3,1},{4,2},{5,3},{6,4},{7,5},{8,6},{9,7},{10,... | collective-permute-start | bytes 589832 | tf_op jit(solution)/shard_map/ppermute | solution.py:199
  180.2 16.6 %collective-permute-start.13 = (f32[384,128]{1,0:T(8,128)}, f32[384,128]{1,0:T(8,128)}, u32[]{:S(2)}, u32[]{:S(2)}) collective-permute-start(f32[384,128]{1,0:T(8,128)} %get-tuple-element.17), channel_id=1, source_target_pairs={{0,13},{1,14},{2,15},{3,0},{4,1},{5,2},{6,3},{7,4},{8,5},{9,6},{10... | collective-permute-start | bytes 589832 | tf_op jit(solution)/shard_map/ppermute | solution.py:199
  184.6 15.2 %collective-permute-start.12 = (f32[384,128]{1,0:T(8,128)}, f32[384,128]{1,0:T(8,128)}, u32[]{:S(2)}, u32[]{:S(2)}) collective-permute-start(f32[384,128]{1,0:T(8,128)} %get-tuple-element.18), channel_id=1, source_target_pairs={{0,12},{1,13},{2,14},{3,15},{4,0},{5,1},{6,2},{7,3},{8,4},{9,5},{1... | collective-permute-start | bytes 589832 | tf_op jit(solution)/shard_map/ppermute | solution.py:199
  184.9 19.4 %collective-permute-start.11 = (f32[384,128]{1,0:T(8,128)}, f32[384,128]{1,0:T(8,128)}, u32[]{:S(2)}, u32[]{:S(2)}) collective-permute-start(f32[384,128]{1,0:T(8,128)} %get-tuple-element.19), channel_id=1, source_target_pairs={{0,11},{1,12},{2,13},{3,14},{4,15},{5,0},{6,1},{7,2},{8,3},{9,4},{... | collective-permute-start | bytes 589832 | tf_op jit(solution)/shard_map/ppermute | solution.py:199
  188.0 33.8 %collective-permute-start.10 = (f32[384,128]{1,0:T(8,128)}, f32[384,128]{1,0:T(8,128)S(1)}, u32[]{:S(2)}, u32[]{:S(2)}) collective-permute-start(f32[384,128]{1,0:T(8,128)} %get-tuple-element.20), channel_id=1, source_target_pairs={{0,10},{1,11},{2,12},{3,13},{4,14},{5,15},{6,0},{7,1},{8,2},{9,3},... | collective-permute-start | bytes 589832 | tf_op jit(solution)/shard_map/ppermute | solution.py:199
  192.2 33.8 %collective-permute-start.9 = (f32[384,128]{1,0:T(8,128)}, f32[384,128]{1,0:T(8,128)S(1)}, u32[]{:S(2)}, u32[]{:S(2)}) collective-permute-start(f32[384,128]{1,0:T(8,128)} %get-tuple-element.21), channel_id=1, source_target_pairs={{0,9},{1,10},{2,11},{3,12},{4,13},{5,14},{6,15},{7,0},{8,1},{9,2},... | collective-permute-start | bytes 589832 | tf_op jit(solution)/shard_map/ppermute | solution.py:199
  196.8 35.7 %collective-permute-start.8 = (f32[384,128]{1,0:T(8,128)}, f32[384,128]{1,0:T(8,128)S(1)}, u32[]{:S(2)}, u32[]{:S(2)}) collective-permute-start(f32[384,128]{1,0:T(8,128)} %get-tuple-element.22), channel_id=1, source_target_pairs={{0,8},{1,9},{2,10},{3,11},{4,12},{5,13},{6,14},{7,15},{8,0},{9,1},... | collective-permute-start | bytes 589832 | tf_op jit(solution)/shard_map/ppermute | solution.py:199
  199.8 48.1 %collective-permute-start.7 = (f32[384,128]{1,0:T(8,128)}, f32[384,128]{1,0:T(8,128)S(1)}, u32[]{:S(2)}, u32[]{:S(2)}) collective-permute-start(f32[384,128]{1,0:T(8,128)} %get-tuple-element.23), channel_id=1, source_target_pairs={{0,7},{1,8},{2,9},{3,10},{4,11},{5,12},{6,13},{7,14},{8,15},{9,0},... | collective-permute-start | bytes 589832 | tf_op jit(solution)/shard_map/ppermute | solution.py:199
  204.3 43.5 %collective-permute-start.6 = (f32[384,128]{1,0:T(8,128)}, f32[384,128]{1,0:T(8,128)S(1)}, u32[]{:S(2)}, u32[]{:S(2)}) collective-permute-start(f32[384,128]{1,0:T(8,128)} %get-tuple-element.24), channel_id=1, source_target_pairs={{0,6},{1,7},{2,8},{3,9},{4,10},{5,11},{6,12},{7,13},{8,14},{9,15},... | collective-permute-start | bytes 589832 | tf_op jit(solution)/shard_map/ppermute | solution.py:199
  221.8 27.5 %copy-start.2 = (f32[384,128]{1,0:T(8,128)}, f32[384,128]{1,0:T(8,128)S(1)}, u32[]{:S(2)}) copy-start(f32[384,128]{1,0:T(8,128)S(1)} %collective-permute-done.10.refs_11_) | copy-start | bytes 589828
  221.8 35.9 %collective-permute-start.5 = (f32[384,128]{1,0:T(8,128)}, f32[384,128]{1,0:T(8,128)}, u32[]{:S(2)}, u32[]{:S(2)}) collective-permute-start(f32[384,128]{1,0:T(8,128)} %get-tuple-element.25), channel_id=1, source_target_pairs={{0,5},{1,6},{2,7},{3,8},{4,9},{5,10},{6,11},{7,12},{8,13},{9,14},{... | collective-permute-start | bytes 589832 | tf_op jit(solution)/shard_map/ppermute | solution.py:199
  226.0 23.3 %copy-start.3 = (f32[384,128]{1,0:T(8,128)}, f32[384,128]{1,0:T(8,128)S(1)}, u32[]{:S(2)}) copy-start(f32[384,128]{1,0:T(8,128)S(1)} %collective-permute-done.9.refs_10_) | copy-start | bytes 589828
  226.0 31.7 %collective-permute-start.4 = (f32[384,128]{1,0:T(8,128)}, f32[384,128]{1,0:T(8,128)}, u32[]{:S(2)}, u32[]{:S(2)}) collective-permute-start(f32[384,128]{1,0:T(8,128)} %get-tuple-element.26), channel_id=1, source_target_pairs={{0,4},{1,5},{2,6},{3,7},{4,8},{5,9},{6,10},{7,11},{8,12},{9,13},{1... | collective-permute-start | bytes 589832 | tf_op jit(solution)/shard_map/ppermute | solution.py:199
  232.5 16.9 %copy-start.4 = (f32[384,128]{1,0:T(8,128)}, f32[384,128]{1,0:T(8,128)S(1)}, u32[]{:S(2)}) copy-start(f32[384,128]{1,0:T(8,128)S(1)} %collective-permute-done.8.refs_9_) | copy-start | bytes 589828
  232.5 25.2 %collective-permute-start.3 = (f32[384,128]{1,0:T(8,128)}, f32[384,128]{1,0:T(8,128)}, u32[]{:S(2)}, u32[]{:S(2)}) collective-permute-start(f32[384,128]{1,0:T(8,128)} %get-tuple-element.27), channel_id=1, source_target_pairs={{0,3},{1,4},{2,5},{3,6},{4,7},{5,8},{6,9},{7,10},{8,11},{9,12},{10... | collective-permute-start | bytes 589832 | tf_op jit(solution)/shard_map/ppermute | solution.py:199
  247.8 1.5 copy-start.5
  247.8 9.9 %collective-permute-start.2 = (f32[384,128]{1,0:T(8,128)S(1)}, f32[384,128]{1,0:T(8,128)}, u32[]{:S(2)}, u32[]{:S(2)}) collective-permute-start(f32[384,128]{1,0:T(8,128)S(1)} %get-tuple-element.28), channel_id=1, source_target_pairs={{0,2},{1,3},{2,4},{3,5},{4,6},{5,7},{6,8},{7,9},{8,10},{9,11},{10,... | collective-permute-start | bytes 589832 | tf_op jit(solution)/shard_map/ppermute | solution.py:199
  247.9 1.5 copy-start.6
  247.9 9.9 %collective-permute-start.1 = (f32[384,128]{1,0:T(8,128)S(1)}, f32[384,128]{1,0:T(8,128)}, u32[]{:S(2)}, u32[]{:S(2)}) collective-permute-start(f32[384,128]{1,0:T(8,128)S(1)} %get-tuple-element.29), channel_id=1, source_target_pairs={{0,1},{1,2},{2,3},{3,4},{4,5},{5,6},{6,7},{7,8},{8,9},{9,10},{10,1... | collective-permute-start | bytes 589832 | tf_op jit(solution)/shard_map/ppermute | solution.py:199
  268.0 1.0 copy-start.1

commit v2 on v0

--- a/solution.py
+++ b/solution.py
@@ -90,7 +90,7 @@
 
 def interpolate(grid_rows, lattice, high, low, mrows):
     rows = grid_rows.shape[0]
-    step = min(rows, 256)
+    step = max(n for n in range(8, 257, 8) if rows % n == 0)
     whole = lambda a: pl.BlockSpec(a.shape, lambda i: (0, 0))
     return pl.pallas_call(
         lambda *refs: interpolate_kernel(*refs, mrows=mrows),
@@ -231,7 +231,8 @@
     grid_rows = known.transpose(0, 2, 1).astype(jnp.float32)
     turned_rows = lax.dynamic_slice_in_dim(jnp.concatenate([grid_rows, grid_rows], 0), me, devices, 0)
     lattice_rows = jnp.concatenate([lattice, jnp.zeros((5, vectors), jnp.int32)], 0).astype(jnp.float32)
-    cuts = [(0, kpoints // 4 * 3, by_shift), (kpoints // 4 * 3, kpoints, False)]
+    edges = [0, kpoints // 2, kpoints // 8 * 7, kpoints]
+    cuts = [(start, end, by_shift and c != 2) for c, (start, end) in enumerate(zip(edges, edges[1:]))]
     sent = []
     for start, end, shifted in cuts:
         rows = (turned_rows if shifted else grid_rows)[:, start:end].reshape(devices * (end - start), 8)
@@ -247,8 +248,8 @@
             sent.append([got.transpose(1, 0, 2, 3).reshape(end - start, devices * mrows, lanes)])
     out = None
     place = me.astype(jnp.int32).reshape(1)
-    for (start, end, shifted), pieces in zip(cuts, sent):
-        out = rotate(pieces, eigen_vectors, far, mrows if tiled else 0, modes, start, place, out)
+    for c, pieces in enumerate(sent):
+        out = rotate(pieces, eigen_vectors, far, mrows if tiled else 0, modes, edges[c], place, out)
     return out
 
 

time: 244 us -> 248 us (1.016)
  the two profiles are of different devices: /device:TPU:0 before, /device:TPU:9 now
where the time goes in v2:
time: 248 us; the launch traced here: 243 us
  starting transfers between devices  80.3 us (32%)
  waiting for transfers between devices  80.1 us (32%)
  Pallas kernels  59.8 us (24%)
  local copies, waits for them, and re-layouts  19.7 us (8%)
  other arithmetic  3.1 us (1%)
    ppermute x30, starting transfers between devices, spread(): lax.ppermute(blocks(s), 'ka', [(d, (d + s) % devices) for d in range(devi...  60.8 us
    all_to_all x3, waiting for transfers between devices, exchange(): return lax.all_to_all(x, 'ka', split_axis=0, concat_axis=0, tiled=True)  49.9 us
    pallas_call x3, Pallas kernels, interpolate(): pl.pallas_call(lambda *refs: interpolate_kernel(*refs, mrows=mrows), out_...  32.3 us
    ppermute x30, waiting for transfers between devices, spread(): lax.ppermute(blocks(s), 'ka', [(d, (d + s) % devices) for d in range(devi...  30.2 us
    all_to_all x3, starting transfers between devices, exchange(): return lax.all_to_all(x, 'ka', split_axis=0, concat_axis=0, tiled=True)  19.6 us
    pallas_call x3, Pallas kernels, rotate(): pl.pallas_call(lambda *refs: rotate_kernel(*refs, block=block, mrows=mrow...  16.8 us
    pallas_call x1, Pallas kernels, prepare_table(): pl.pallas_call(table_kernel, out_shape=[jax.ShapeDtypeStruct((2 * vectors...  10.6 us
  transfers between devices with their start and end apart: 33, of which 6 were waited for; matrix products, arithmetic and copies ran while one was open for 5% of the time, Pallas kernels for 23%

profile of v2, /device:TPU:9, one launch (start us, length us, event | category | flops | bytes accessed | tf_op | source)
XLA Modules:
  0.0 243.5 jit_solution(3086427350850380104)
XLA Ops:
  1.6 6.6 %all-to-all-start = ((s32[16,1,512]{2,1,0:T(1,128)}), s32[16,1,512]{2,1,0:T(1,128)S(1)}, u32[]{:S(2)}, u32[]{:S(2)}) async-start(s32[16,1,512]{2,1,0:T(1,128)} %reshape.152), calls=%async_computation | async-start | bytes 65536 | tf_op jit(solution)/shard_map/all_to_all | solution.py:183
  8.2 5.0 %all-to-all-done = s32[16,1,512]{2,1,0:T(1,128)S(1)} async-done(((s32[16,1,512]{2,1,0:T(1,128)}), s32[16,1,512]{2,1,0:T(1,128)S(1)}, u32[]{:S(2)}, u32[]{:S(2)}) %all-to-all-start) | async-done | bytes 32800 | tf_op jit(solution)/shard_map/all_to_all | solution.py:183
  15.3 4.4 %gather_fusion = f32[128,64,128]{2,1,0:T(8,128)} fusion(f32[64,64,128]{2,1,0:T(8,128)} %refs_2_.1, s32[1024]{0:T(1024)S(1)} %pad_clamp_fusion.1), kind=kCustom, calls=%fused_computation | custom fusion | bytes 8389120 | tf_op jit(solution)/shard_map/gather | solution.py:223
  19.7 6.0 %all-to-all-start.2 = ((f32[16,512,128]{2,1,0:T(8,128)}), f32[16,512,128]{2,1,0:T(8,128)}, u32[]{:S(2)}, u32[]{:S(2)}) async-start(f32[16,512,128]{2,1,0:T(8,128)} %bitcast.19), calls=%async_computation.2 | async-start | bytes 8388608 | tf_op jit(solution)/shard_map/all_to_all | solution.py:183
  25.7 10.6 %table.2 = (bf16[2048,1024]{1,0:T(8,128)(2,1)}, bf16[2048,1024]{1,0:T(8,128)(2,1)}) custom-call(f32[2,1024,512]{2,1,0:T(8,128)} %table.3), custom_call_target="tpu_custom_call" | custom-call | tf_op jit(solution)/shard_map/table/pallas_call | solution.py:68
  37.8 11.6 %interpolate.4 = f32[3072,128]{1,0:T(8,128)} custom-call(f32[384,8]{1,0:T(8,128)} %bitcast.21, f32[8,1024]{1,0:T(8,128)} %pad_convert_fusion.refs_1_, bf16[2048,1024]{1,0:T(8,128)(2,1)} %get-tuple-element.7.refs_2_, bf16[2048,1024]{1,0:T(8,128)(2,1)} %get-tuple-element.8.refs_3_), custom_call_target="tpu_custom_call" | custom-call | tf_op jit(solution)/shard_map/interpolate/pallas_call | solution.py:95
  49.4 2.4 fusion.6
  53.4 4.4 %collective-permute-start.12 = (f32[192,128]{1,0:T(8,128)S(1)}, f32[192,128]{1,0:T(8,128)S(1)}, u32[]{:S(2)}, u32[]{:S(2)}) collective-permute-start(f32[192,128]{1,0:T(8,128)S(1)} %get-tuple-element.29), channel_id=1, source_target_pairs={{0,13},{1,14},{2,15},{3,0},{4,1},{5,2},{6,3},{7,4},{8,5},{9,6},{10... | collective-permute-start | bytes 294920 | tf_op jit(solution)/shard_map/ppermute | solution.py:199
  59.7 6.8 %interpolate.3 = f32[1024,128]{1,0:T(8,128)} custom-call(f32[128,8]{1,0:T(8,128)} %bitcast.23, f32[8,1024]{1,0:T(8,128)} %pad_convert_fusion.refs_1_, bf16[2048,1024]{1,0:T(8,128)(2,1)} %get-tuple-element.7.refs_2_, bf16[2048,1024]{1,0:T(8,128)(2,1)} %get-tuple-element.8.refs_3_), custom_call_target="tpu_custom_call" | custom-call | tf_op jit(solution)/shard_map/interpolate/pallas_call | solution.py:95
  66.6 13.9 %interpolate.5 = f32[4096,128]{1,0:T(8,128)} custom-call(f32[512,8]{1,0:T(8,128)} %bitcast.20, f32[8,1024]{1,0:T(8,128)} %pad_convert_fusion.refs_1_, bf16[2048,1024]{1,0:T(8,128)(2,1)} %get-tuple-element.7.refs_2_, bf16[2048,1024]{1,0:T(8,128)(2,1)} %get-tuple-element.8.refs_3_), custom_call_target="tpu_custom_call" | custom-call | tf_op jit(solution)/shard_map/interpolate/pallas_call | solution.py:95
  80.5 44.9 %all-to-all-done.2 = f32[16,512,128]{2,1,0:T(8,128)} async-done(((f32[16,512,128]{2,1,0:T(8,128)}), f32[16,512,128]{2,1,0:T(8,128)}, u32[]{:S(2)}, u32[]{:S(2)}) %all-to-all-start.2) | async-done | bytes 4194336 | tf_op jit(solution)/shard_map/all_to_all | solution.py:183
  125.3 7.0 %all-to-all-start.1 = ((f32[16,64,128]{2,1,0:T(8,128)}), f32[16,64,128]{2,1,0:T(8,128)S(1)}, u32[]{:S(2)}, u32[]{:S(2)}) async-start(f32[16,64,128]{2,1,0:T(8,128)} %bitcast.5), calls=%async_computation.1 | async-start | bytes 1048576 | tf_op jit(solution)/shard_map/all_to_all | solution.py:183
  132.4 3.0 %collective-permute-start.9 = (f32[192,128]{1,0:T(8,128)}, f32[192,128]{1,0:T(8,128)S(1)}, u32[]{:S(2)}, u32[]{:S(2)}) collective-permute-start(f32[192,128]{1,0:T(8,128)} %get-tuple-element.32), channel_id=1, source_target_pairs={{0,10},{1,11},{2,12},{3,13},{4,14},{5,15},{6,0},{7,1},{8,2},{9,3},... | collective-permute-start | bytes 294920 | tf_op jit(solution)/shard_map/ppermute | solution.py:199
  136.3 2.4 collective-permute-start.6
  138.7 2.0 collective-permute-start.5
  140.7 2.4 fusion.5
  143.2 12.9 %collective-permute-done.9.refs_11_ = f32[192,128]{1,0:T(8,128)S(1)} collective-permute-done((f32[192,128]{1,0:T(8,128)}, f32[192,128]{1,0:T(8,128)S(1)}, u32[]{:S(2)}, u32[]{:S(2)}) %collective-permute-start.9) | collective-permute-done | bytes 98336 | tf_op jit(solution)/shard_map/ppermute | solution.py:199
  157.7 4.4 %collective-permute-start.28 = (f32[256,128]{1,0:T(8,128)S(1)}, f32[256,128]{1,0:T(8,128)S(1)}, u32[]{:S(2)}, u32[]{:S(2)}) collective-permute-start(f32[256,128]{1,0:T(8,128)S(1)} %get-tuple-element.12), channel_id=1, source_target_pairs={{0,14},{1,15},{2,0},{3,1},{4,2},{5,3},{6,4},{7,5},{8,6},{9,7},{10,... | collective-permute-start | bytes 393224 | tf_op jit(solution)/shard_map/ppermute | solution.py:199
  165.6 7.3 %collective-permute-done.5.refs_7_ = f32[192,128]{1,0:T(8,128)S(1)} collective-permute-done((f32[192,128]{1,0:T(8,128)S(1)}, f32[192,128]{1,0:T(8,128)S(1)}, u32[]{:S(2)}, u32[]{:S(2)}) %collective-permute-start.5) | collective-permute-done | bytes 98336 | tf_op jit(solution)/shard_map/ppermute | solution.py:199
  172.9 5.3 %collective-permute-start.24 = (f32[256,128]{1,0:T(8,128)S(1)}, f32[256,128]{1,0:T(8,128)S(1)}, u32[]{:S(2)}, u32[]{:S(2)}) collective-permute-start(f32[256,128]{1,0:T(8,128)S(1)} %get-tuple-element.16), channel_id=1, source_target_pairs={{0,10},{1,11},{2,12},{3,13},{4,14},{5,15},{6,0},{7,1},{8,2},{9,3},... | collective-permute-start | bytes 393224 | tf_op jit(solution)/shard_map/ppermute | solution.py:199
  178.3 2.9 %collective-permute-start.22 = (f32[256,128]{1,0:T(8,128)S(1)}, f32[256,128]{1,0:T(8,128)S(1)}, u32[]{:S(2)}, u32[]{:S(2)}) collective-permute-start(f32[256,128]{1,0:T(8,128)S(1)} %get-tuple-element.18), channel_id=1, source_target_pairs={{0,8},{1,9},{2,10},{3,11},{4,12},{5,13},{6,14},{7,15},{8,0},{9,1},... | collective-permute-start | bytes 393224 | tf_op jit(solution)/shard_map/ppermute | solution.py:199
  181.2 2.9 %collective-permute-start.20 = (f32[256,128]{1,0:T(8,128)S(1)}, f32[256,128]{1,0:T(8,128)S(1)}, u32[]{:S(2)}, u32[]{:S(2)}) collective-permute-start(f32[256,128]{1,0:T(8,128)S(1)} %get-tuple-element.20), channel_id=1, source_target_pairs={{0,6},{1,7},{2,8},{3,9},{4,10},{5,11},{6,12},{7,13},{8,14},{9,15},... | collective-permute-start | bytes 393224 | tf_op jit(solution)/shard_map/ppermute | solution.py:199
  184.5 7.3 %collective-permute-done.24.refs_11_ = f32[256,128]{1,0:T(8,128)S(1)} collective-permute-done((f32[256,128]{1,0:T(8,128)S(1)}, f32[256,128]{1,0:T(8,128)S(1)}, u32[]{:S(2)}, u32[]{:S(2)}) %collective-permute-start.24) | collective-permute-done | bytes 131104 | tf_op jit(solution)/shard_map/ppermute | solution.py:199
  192.0 2.6 %collective-permute-done.23.refs_10_ = f32[256,128]{1,0:T(8,128)S(1)} collective-permute-done((f32[256,128]{1,0:T(8,128)S(1)}, f32[256,128]{1,0:T(8,128)S(1)}, u32[]{:S(2)}, u32[]{:S(2)}) %collective-permute-start.23) | collective-permute-done | bytes 131104 | tf_op jit(solution)/shard_map/ppermute | solution.py:199
  194.6 4.3 %collective-permute-start.18 = (f32[256,128]{1,0:T(8,128)S(1)}, f32[256,128]{1,0:T(8,128)S(1)}, u32[]{:S(2)}, u32[]{:S(2)}) collective-permute-start(f32[256,128]{1,0:T(8,128)S(1)} %get-tuple-element.22), channel_id=1, source_target_pairs={{0,4},{1,5},{2,6},{3,7},{4,8},{5,9},{6,10},{7,11},{8,12},{9,13},{1... | collective-permute-start | bytes 393224 | tf_op jit(solution)/shard_map/ppermute | solution.py:199
  198.9 6.5 %collective-permute-start.17 = (f32[256,128]{1,0:T(8,128)S(1)}, f32[256,128]{1,0:T(8,128)S(1)}, u32[]{:S(2)}, u32[]{:S(2)}) collective-permute-start(f32[256,128]{1,0:T(8,128)S(1)} %get-tuple-element.23), channel_id=1, source_target_pairs={{0,3},{1,4},{2,5},{3,6},{4,7},{5,8},{6,9},{7,10},{8,11},{9,12},{10... | collective-permute-start | bytes 393224 | tf_op jit(solution)/shard_map/ppermute | solution.py:199
  206.9 6.4 %collective-permute-start.4 = (f32[192,128]{1,0:T(8,128)}, f32[192,128]{1,0:T(8,128)S(1)}, u32[]{:S(2)}, u32[]{:S(2)}) collective-permute-start(f32[192,128]{1,0:T(8,128)} %get-tuple-element.37), channel_id=1, source_target_pairs={{0,5},{1,6},{2,7},{3,8},{4,9},{5,10},{6,11},{7,12},{8,13},{9,14},{... | collective-permute-start | bytes 294920 | tf_op jit(solution)/shard_map/ppermute | solution.py:199
  214.2 4.9 %collective-permute-start.1 = (f32[192,128]{1,0:T(8,128)}, f32[192,128]{1,0:T(8,128)S(1)}, u32[]{:S(2)}, u32[]{:S(2)}) collective-permute-start(f32[192,128]{1,0:T(8,128)} %get-tuple-element.40), channel_id=1, source_target_pairs={{0,2},{1,3},{2,4},{3,5},{4,6},{5,7},{6,8},{7,9},{8,10},{9,11},{10,... | collective-permute-start | bytes 294920 | tf_op jit(solution)/shard_map/ppermute | solution.py:199
  220.6 4.2 %gather_fusion.1 = f32[64,64,128]{2,1,0:T(8,128)} fusion(f32[128,64,128]{2,1,0:T(8,128)} %bitcast.10, s32[1024]{0:T(1024)S(1)} %pad_clamp_fusion), kind=kCustom, calls=%fused_computation.1 | custom fusion | bytes 4194560 | tf_op jit(solution)/shard_map/gather | solution.py:229
  225.0 7.5 %rotate.3.refs_19_ = f32[64,2,64,128]{3,2,1,0:T(8,128)} custom-call(s32[1]{0:T(128)} %bitcast.refs_0_, f32[256,128]{1,0:T(8,128)} %get-tuple-element.26.refs_1_, f32[256,128]{1,0:T(8,128)} %copy-done.15, f32[256,128]{1,0:T(8,128)} %copy-done.14, f32[256,128]{1,0:T(8,128)} %copy-done.13, f32[256,128]{1,0:T(8,128)} %copy-done.12, f32[256,128]{1,0:T(8,128)} %copy-done.11, ...), custom_call_target="tpu_custom_call" | custom-call | tf_op jit(solution)/shard_map/rotate/pallas_call | solution.py:160
  233.3 6.1 %rotate.4.refs_4_ = f32[64,2,64,128]{3,2,1,0:T(8,128)} custom-call(s32[1]{0:T(128)} %bitcast.refs_0_, f32[192,128]{1,0:T(8,128)} %get-tuple-element.42.refs_1_, f32[192,128]{1,0:T(8,128)} %copy-done.30, f32[192,128]{1,0:T(8,128)} %copy-done.29, f32[192,128]{1,0:T(8,128)} %copy-done.28, f32[192,128]{1,0:T(8,128)} %copy-done.27, ...), custom_call_target="tpu_custom_call", output_to_operand_aliasing={{}: (19, {})} | custom-call | tf_op jit(solution)/shard_map/rotate/pallas_call | solution.py:160
  240.2 3.2 %rotate.5 = f32[64,2,64,128]{3,2,1,0:T(8,128)} custom-call(s32[1]{0:T(128)} %bitcast.refs_0_, f32[16,64,128]{2,1,0:T(8,128)} %copy-done, f32[64,64,128]{2,1,0:T(8,128)} %refs_2_.1, f32[64,64,128]{2,1,0:T(8,128)} %gather_fusion.1, f32[64,2,64,128]{3,2,1,0:T(8,128)} %rotate.4.refs_4_), custom_call_target="tpu_custom_call", output_to_operand_aliasing={{}: (4, {})} | custom-call | tf_op jit(solution)/shard_map/rotate/pallas_call | solution.py:160
  (140 shorter events, 20.7 us)
Async XLA Ops:
  1.6 11.6 %all-to-all-start = ((s32[16,1,512]{2,1,0:T(1,128)}), s32[16,1,512]{2,1,0:T(1,128)S(1)}, u32[]{:S(2)}, u32[]{:S(2)}) async-start(s32[16,1,512]{2,1,0:T(1,128)} %reshape.152), calls=%async_computation | async-start | bytes 65536 | tf_op jit(solution)/shard_map/all_to_all | solution.py:183
  19.7 105.7 %all-to-all-start.2 = ((f32[16,512,128]{2,1,0:T(8,128)}), f32[16,512,128]{2,1,0:T(8,128)}, u32[]{:S(2)}, u32[]{:S(2)}) async-start(f32[16,512,128]{2,1,0:T(8,128)} %bitcast.19), calls=%async_computation.2 | async-start | bytes 8388608 | tf_op jit(solution)/shard_map/all_to_all | solution.py:183
  51.8 80.6 %collective-permute-start.14 = (f32[192,128]{1,0:T(8,128)S(1)}, f32[192,128]{1,0:T(8,128)S(1)}, u32[]{:S(2)}, u32[]{:S(2)}) collective-permute-start(f32[192,128]{1,0:T(8,128)S(1)} %get-tuple-element.27), channel_id=1, source_target_pairs={{0,15},{1,0},{2,1},{3,2},{4,3},{5,4},{6,5},{7,6},{8,7},{9,8},{10,9... | collective-permute-start | bytes 294920 | tf_op jit(solution)/shard_map/ppermute | solution.py:199
  52.2 83.2 %collective-permute-start.13 = (f32[192,128]{1,0:T(8,128)S(1)}, f32[192,128]{1,0:T(8,128)S(1)}, u32[]{:S(2)}, u32[]{:S(2)}) collective-permute-start(f32[192,128]{1,0:T(8,128)S(1)} %get-tuple-element.28), channel_id=1, source_target_pairs={{0,14},{1,15},{2,0},{3,1},{4,2},{5,3},{6,4},{7,5},{8,6},{9,7},{10,... | collective-permute-start | bytes 294920 | tf_op jit(solution)/shard_map/ppermute | solution.py:199
  53.4 82.9 %collective-permute-start.12 = (f32[192,128]{1,0:T(8,128)S(1)}, f32[192,128]{1,0:T(8,128)S(1)}, u32[]{:S(2)}, u32[]{:S(2)}) collective-permute-start(f32[192,128]{1,0:T(8,128)S(1)} %get-tuple-element.29), channel_id=1, source_target_pairs={{0,13},{1,14},{2,15},{3,0},{4,1},{5,2},{6,3},{7,4},{8,5},{9,6},{10... | collective-permute-start | bytes 294920 | tf_op jit(solution)/shard_map/ppermute | solution.py:199
  57.8 78.5 %collective-permute-start.11 = (f32[192,128]{1,0:T(8,128)S(1)}, f32[192,128]{1,0:T(8,128)S(1)}, u32[]{:S(2)}, u32[]{:S(2)}) collective-permute-start(f32[192,128]{1,0:T(8,128)S(1)} %get-tuple-element.30), channel_id=1, source_target_pairs={{0,12},{1,13},{2,14},{3,15},{4,0},{5,1},{6,2},{7,3},{8,4},{9,5},{1... | collective-permute-start | bytes 294920 | tf_op jit(solution)/shard_map/ppermute | solution.py:199
  58.1 80.7 %collective-permute-start.10 = (f32[192,128]{1,0:T(8,128)S(1)}, f32[192,128]{1,0:T(8,128)S(1)}, u32[]{:S(2)}, u32[]{:S(2)}) collective-permute-start(f32[192,128]{1,0:T(8,128)S(1)} %get-tuple-element.31), channel_id=1, source_target_pairs={{0,11},{1,12},{2,13},{3,14},{4,15},{5,0},{6,1},{7,2},{8,3},{9,4},{... | collective-permute-start | bytes 294920 | tf_op jit(solution)/shard_map/ppermute | solution.py:199
  125.3 114.1 %all-to-all-start.1 = ((f32[16,64,128]{2,1,0:T(8,128)}), f32[16,64,128]{2,1,0:T(8,128)S(1)}, u32[]{:S(2)}, u32[]{:S(2)}) async-start(f32[16,64,128]{2,1,0:T(8,128)} %bitcast.5), calls=%async_computation.1 | async-start | bytes 1048576 | tf_op jit(solution)/shard_map/all_to_all | solution.py:183
  132.4 23.7 %collective-permute-start.9 = (f32[192,128]{1,0:T(8,128)}, f32[192,128]{1,0:T(8,128)S(1)}, u32[]{:S(2)}, u32[]{:S(2)}) collective-permute-start(f32[192,128]{1,0:T(8,128)} %get-tuple-element.32), channel_id=1, source_target_pairs={{0,10},{1,11},{2,12},{3,13},{4,14},{5,15},{6,0},{7,1},{8,2},{9,3},... | collective-permute-start | bytes 294920 | tf_op jit(solution)/shard_map/ppermute | solution.py:199
  135.4 22.2 %collective-permute-start.8 = (f32[192,128]{1,0:T(8,128)}, f32[192,128]{1,0:T(8,128)S(1)}, u32[]{:S(2)}, u32[]{:S(2)}) collective-permute-start(f32[192,128]{1,0:T(8,128)} %get-tuple-element.33), channel_id=1, source_target_pairs={{0,9},{1,10},{2,11},{3,12},{4,13},{5,14},{6,15},{7,0},{8,1},{9,2},... | collective-permute-start | bytes 294920 | tf_op jit(solution)/shard_map/ppermute | solution.py:199
  136.3 25.8 %collective-permute-start.7 = (f32[192,128]{1,0:T(8,128)}, f32[192,128]{1,0:T(8,128)S(1)}, u32[]{:S(2)}, u32[]{:S(2)}) collective-permute-start(f32[192,128]{1,0:T(8,128)} %get-tuple-element.34), channel_id=1, source_target_pairs={{0,8},{1,9},{2,10},{3,11},{4,12},{5,13},{6,14},{7,15},{8,0},{9,1},... | collective-permute-start | bytes 294920 | tf_op jit(solution)/shard_map/ppermute | solution.py:199
  136.3 27.1 %collective-permute-start.6 = (f32[192,128]{1,0:T(8,128)}, f32[192,128]{1,0:T(8,128)S(1)}, u32[]{:S(2)}, u32[]{:S(2)}) collective-permute-start(f32[192,128]{1,0:T(8,128)} %get-tuple-element.35), channel_id=1, source_target_pairs={{0,7},{1,8},{2,9},{3,10},{4,11},{5,12},{6,13},{7,14},{8,15},{9,0},... | collective-permute-start | bytes 294920 | tf_op jit(solution)/shard_map/ppermute | solution.py:199
  138.7 34.2 %collective-permute-start.5 = (f32[192,128]{1,0:T(8,128)S(1)}, f32[192,128]{1,0:T(8,128)S(1)}, u32[]{:S(2)}, u32[]{:S(2)}) collective-permute-start(f32[192,128]{1,0:T(8,128)S(1)} %get-tuple-element.36), channel_id=1, source_target_pairs={{0,6},{1,7},{2,8},{3,9},{4,10},{5,11},{6,12},{7,13},{8,14},{9,15},... | collective-permute-start | bytes 294920 | tf_op jit(solution)/shard_map/ppermute | solution.py:199
  156.1 16.9 %collective-permute-start.29 = (f32[256,128]{1,0:T(8,128)S(1)}, f32[256,128]{1,0:T(8,128)S(1)}, u32[]{:S(2)}, u32[]{:S(2)}) collective-permute-start(f32[256,128]{1,0:T(8,128)S(1)} %get-tuple-element.11), channel_id=1, source_target_pairs={{0,15},{1,0},{2,1},{3,2},{4,3},{5,4},{6,5},{7,6},{8,7},{9,8},{10,9... | collective-permute-start | bytes 393224 | tf_op jit(solution)/shard_map/ppermute | solution.py:199
  157.7 20.6 %collective-permute-start.28 = (f32[256,128]{1,0:T(8,128)S(1)}, f32[256,128]{1,0:T(8,128)S(1)}, u32[]{:S(2)}, u32[]{:S(2)}) collective-permute-start(f32[256,128]{1,0:T(8,128)S(1)} %get-tuple-element.12), channel_id=1, source_target_pairs={{0,14},{1,15},{2,0},{3,1},{4,2},{5,3},{6,4},{7,5},{8,6},{9,7},{10,... | collective-permute-start | bytes 393224 | tf_op jit(solution)/shard_map/ppermute | solution.py:199
  162.1 16.2 %collective-permute-start.27 = (f32[256,128]{1,0:T(8,128)S(1)}, f32[256,128]{1,0:T(8,128)S(1)}, u32[]{:S(2)}, u32[]{:S(2)}) collective-permute-start(f32[256,128]{1,0:T(8,128)S(1)} %get-tuple-element.13), channel_id=1, source_target_pairs={{0,13},{1,14},{2,15},{3,0},{4,1},{5,2},{6,3},{7,4},{8,5},{9,6},{10... | collective-permute-start | bytes 393224 | tf_op jit(solution)/shard_map/ppermute | solution.py:199
  164.1 17.1 %collective-permute-start.26 = (f32[256,128]{1,0:T(8,128)S(1)}, f32[256,128]{1,0:T(8,128)S(1)}, u32[]{:S(2)}, u32[]{:S(2)}) collective-permute-start(f32[256,128]{1,0:T(8,128)S(1)} %get-tuple-element.14), channel_id=1, source_target_pairs={{0,12},{1,13},{2,14},{3,15},{4,0},{5,1},{6,2},{7,3},{8,4},{9,5},{1... | collective-permute-start | bytes 393224 | tf_op jit(solution)/shard_map/ppermute | solution.py:199
  172.9 18.8 %collective-permute-start.24 = (f32[256,128]{1,0:T(8,128)S(1)}, f32[256,128]{1,0:T(8,128)S(1)}, u32[]{:S(2)}, u32[]{:S(2)}) collective-permute-start(f32[256,128]{1,0:T(8,128)S(1)} %get-tuple-element.16), channel_id=1, source_target_pairs={{0,10},{1,11},{2,12},{3,13},{4,14},{5,15},{6,0},{7,1},{8,2},{9,3},... | collective-permute-start | bytes 393224 | tf_op jit(solution)/shard_map/ppermute | solution.py:199
  178.2 16.4 %collective-permute-start.23 = (f32[256,128]{1,0:T(8,128)S(1)}, f32[256,128]{1,0:T(8,128)S(1)}, u32[]{:S(2)}, u32[]{:S(2)}) collective-permute-start(f32[256,128]{1,0:T(8,128)S(1)} %get-tuple-element.17), channel_id=1, source_target_pairs={{0,9},{1,10},{2,11},{3,12},{4,13},{5,14},{6,15},{7,0},{8,1},{9,2},... | collective-permute-start | bytes 393224 | tf_op jit(solution)/shard_map/ppermute | solution.py:199
  178.3 20.6 %collective-permute-start.22 = (f32[256,128]{1,0:T(8,128)S(1)}, f32[256,128]{1,0:T(8,128)S(1)}, u32[]{:S(2)}, u32[]{:S(2)}) collective-permute-start(f32[256,128]{1,0:T(8,128)S(1)} %get-tuple-element.18), channel_id=1, source_target_pairs={{0,8},{1,9},{2,10},{3,11},{4,12},{5,13},{6,14},{7,15},{8,0},{9,1},... | collective-permute-start | bytes 393224 | tf_op jit(solution)/shard_map/ppermute | solution.py:199
  181.2 24.1 %collective-permute-start.21 = (f32[256,128]{1,0:T(8,128)S(1)}, f32[256,128]{1,0:T(8,128)S(1)}, u32[]{:S(2)}, u32[]{:S(2)}) collective-permute-start(f32[256,128]{1,0:T(8,128)S(1)} %get-tuple-element.19), channel_id=1, source_target_pairs={{0,7},{1,8},{2,9},{3,10},{4,11},{5,12},{6,13},{7,14},{8,15},{9,0},... | collective-permute-start | bytes 393224 | tf_op jit(solution)/shard_map/ppermute | solution.py:199
  181.2 24.1 %collective-permute-start.20 = (f32[256,128]{1,0:T(8,128)S(1)}, f32[256,128]{1,0:T(8,128)S(1)}, u32[]{:S(2)}, u32[]{:S(2)}) collective-permute-start(f32[256,128]{1,0:T(8,128)S(1)} %get-tuple-element.20), channel_id=1, source_target_pairs={{0,6},{1,7},{2,8},{3,9},{4,10},{5,11},{6,12},{7,13},{8,14},{9,15},... | collective-permute-start | bytes 393224 | tf_op jit(solution)/shard_map/ppermute | solution.py:199
  191.8 15.1 %collective-permute-start.19 = (f32[256,128]{1,0:T(8,128)S(1)}, f32[256,128]{1,0:T(8,128)S(1)}, u32[]{:S(2)}, u32[]{:S(2)}) collective-permute-start(f32[256,128]{1,0:T(8,128)S(1)} %get-tuple-element.21), channel_id=1, source_target_pairs={{0,5},{1,6},{2,7},{3,8},{4,9},{5,10},{6,11},{7,12},{8,13},{9,14},{... | collective-permute-start | bytes 393224 | tf_op jit(solution)/shard_map/ppermute | solution.py:199
  194.6 18.7 %collective-permute-start.18 = (f32[256,128]{1,0:T(8,128)S(1)}, f32[256,128]{1,0:T(8,128)S(1)}, u32[]{:S(2)}, u32[]{:S(2)}) collective-permute-start(f32[256,128]{1,0:T(8,128)S(1)} %get-tuple-element.22), channel_id=1, source_target_pairs={{0,4},{1,5},{2,6},{3,7},{4,8},{5,9},{6,10},{7,11},{8,12},{9,13},{1... | collective-permute-start | bytes 393224 | tf_op jit(solution)/shard_map/ppermute | solution.py:199
  198.9 14.8 %collective-permute-start.17 = (f32[256,128]{1,0:T(8,128)S(1)}, f32[256,128]{1,0:T(8,128)S(1)}, u32[]{:S(2)}, u32[]{:S(2)}) collective-permute-start(f32[256,128]{1,0:T(8,128)S(1)} %get-tuple-element.23), channel_id=1, source_target_pairs={{0,3},{1,4},{2,5},{3,6},{4,7},{5,8},{6,9},{7,10},{8,11},{9,12},{10... | collective-permute-start | bytes 393224 | tf_op jit(solution)/shard_map/ppermute | solution.py:199
  205.4 8.8 %collective-permute-start.16 = (f32[256,128]{1,0:T(8,128)S(1)}, f32[256,128]{1,0:T(8,128)S(1)}, u32[]{:S(2)}, u32[]{:S(2)}) collective-permute-start(f32[256,128]{1,0:T(8,128)S(1)} %get-tuple-element.24), channel_id=1, source_target_pairs={{0,2},{1,3},{2,4},{3,5},{4,6},{5,7},{6,8},{7,9},{8,10},{9,11},{10,... | collective-permute-start | bytes 393224 | tf_op jit(solution)/shard_map/ppermute | solution.py:199
  205.4 13.7 %collective-permute-start.15 = (f32[256,128]{1,0:T(8,128)S(1)}, f32[256,128]{1,0:T(8,128)S(1)}, u32[]{:S(2)}, u32[]{:S(2)}) collective-permute-start(f32[256,128]{1,0:T(8,128)S(1)} %get-tuple-element.25), channel_id=1, source_target_pairs={{0,1},{1,2},{2,3},{3,4},{4,5},{5,6},{6,7},{7,8},{8,9},{9,10},{10,1... | collective-permute-start | bytes 393224 | tf_op jit(solution)/shard_map/ppermute | solution.py:199
  206.9 25.6 %collective-permute-start.4 = (f32[192,128]{1,0:T(8,128)}, f32[192,128]{1,0:T(8,128)S(1)}, u32[]{:S(2)}, u32[]{:S(2)}) collective-permute-start(f32[192,128]{1,0:T(8,128)} %get-tuple-element.37), channel_id=1, source_target_pairs={{0,5},{1,6},{2,7},{3,8},{4,9},{5,10},{6,11},{7,12},{8,13},{9,14},{... | collective-permute-start | bytes 294920 | tf_op jit(solution)/shard_map/ppermute | solution.py:199
  213.3 19.2 %collective-permute-start.3 = (f32[192,128]{1,0:T(8,128)}, f32[192,128]{1,0:T(8,128)S(1)}, u32[]{:S(2)}, u32[]{:S(2)}) collective-permute-start(f32[192,128]{1,0:T(8,128)} %get-tuple-element.38), channel_id=1, source_target_pairs={{0,4},{1,5},{2,6},{3,7},{4,8},{5,9},{6,10},{7,11},{8,12},{9,13},{1... | collective-permute-start | bytes 294920 | tf_op jit(solution)/shard_map/ppermute | solution.py:199
  213.7 18.8 %collective-permute-start.2 = (f32[192,128]{1,0:T(8,128)}, f32[192,128]{1,0:T(8,128)S(1)}, u32[]{:S(2)}, u32[]{:S(2)}) collective-permute-start(f32[192,128]{1,0:T(8,128)} %get-tuple-element.39), channel_id=1, source_target_pairs={{0,3},{1,4},{2,5},{3,6},{4,7},{5,8},{6,9},{7,10},{8,11},{9,12},{10... | collective-permute-start | bytes 294920 | tf_op jit(solution)/shard_map/ppermute | solution.py:199
  214.2 18.3 %collective-permute-start.1 = (f32[192,128]{1,0:T(8,128)}, f32[192,128]{1,0:T(8,128)S(1)}, u32[]{:S(2)}, u32[]{:S(2)}) collective-permute-start(f32[192,128]{1,0:T(8,128)} %get-tuple-element.40), channel_id=1, source_target_pairs={{0,2},{1,3},{2,4},{3,5},{4,6},{5,7},{6,8},{7,9},{8,10},{9,11},{10,... | collective-permute-start | bytes 294920 | tf_op jit(solution)/shard_map/ppermute | solution.py:199
  219.1 13.4 %collective-permute-start = (f32[192,128]{1,0:T(8,128)}, f32[192,128]{1,0:T(8,128)S(1)}, u32[]{:S(2)}, u32[]{:S(2)}) collective-permute-start(f32[192,128]{1,0:T(8,128)} %get-tuple-element.41), channel_id=1, source_target_pairs={{0,1},{1,2},{2,3},{3,4},{4,5},{5,6},{6,7},{7,8},{8,9},{9,10},{10,1... | collective-permute-start | bytes 294920 | tf_op jit(solution)/shard_map/ppermute | solution.py:199
  (34 other events, 872.0 us)

commit v3 on v0

v3 whole, which is shorter than its diff:
```python
import math

import jax
import jax.numpy as jnp
from jax import lax
from jax.experimental import pallas as pl
from jax.experimental.pallas import tpu as pltpu
from jax.sharding import PartitionSpec as P


KMESH = 64
RELAYED = 16
CROSSING = 48
FORCE = 0
LEADING = 2

SIN_TERMS = [(-1.0) ** i * math.pi ** (2 * i + 1) / math.factorial(2 * i + 1) for i in range(7)]
COS_TERMS = [(-1.0) ** i * math.pi ** (2 * i) / math.factorial(2 * i) for i in range(8)]


def horner(terms, x):
    total = jnp.full_like(x, terms[-1])
    for term in terms[-2::-1]:
        total = total * x + term
    return total


def split(x):
    high = x.astype(jnp.bfloat16)
    return high, (x - high.astype(jnp.float32)).astype(jnp.bfloat16)


def dot(a, b):
    return jnp.dot(a, b, preferred_element_type=jnp.float32)


def dot3(a, b):
    return dot(a[0], b[0]) + dot(a[0], b[1]) + dot(a[1], b[0])


def table_kernel(table, high, low):
    lane = lax.broadcasted_iota(jnp.int32, (table.shape[1], 128), 1)
    first = lane < 64

    def put(half, at, value):
        a, b = split(value)
        high[half, :, at * 128 : (at + 1) * 128] = a
        low[half, :, at * 128 : (at + 1) * 128] = b

    for block in range(table.shape[2] // 128):
        cut = slice(block * 128, (block + 1) * 128)
        real, imag = table[0, :, cut], table[1, :, cut]
        real_turned, imag_turned = pltpu.roll(real, 64, 1), pltpu.roll(imag, 64, 1)
        put(0, 2 * block, jnp.where(first, real, imag_turned))
        put(0, 2 * block + 1, jnp.where(first, real_turned, imag))
        put(1, 2 * block, jnp.where(first, -imag, real_turned))
        put(1, 2 * block + 1, jnp.where(first, -imag_turned, real))


def prepare_table(table):
    vectors, pairs = table.shape[1:]
    rows = math.gcd(vectors, 128)
    high, low = pl.pallas_call(
        table_kernel,
        out_shape=[jax.ShapeDtypeStruct((2, vectors, 2 * pairs), jnp.bfloat16)] * 2,
        grid=(vectors // rows,),
        in_specs=[pl.BlockSpec((2, rows, pairs), lambda i: (0, i, 0))],
        out_specs=[pl.BlockSpec((2, rows, 2 * pairs), lambda i: (0, i, 0))] * 2,
        name="table",
    )(table)
    return high.reshape(2 * vectors, 2 * pairs), low.reshape(2 * vectors, 2 * pairs)


def interpolate_kernel(grid_rows, lattice, high, low, *refs, mrows, parts):
    outs = refs[-parts:]
    turns = dot(grid_rows[...].astype(jnp.bfloat16), lattice[...].astype(jnp.bfloat16)) * (1.0 / KMESH)
    part = turns - jnp.round(turns)
    square = part * part
    sine = horner(SIN_TERMS, square) * part
    cosine = horner(COS_TERMS, square)
    phase = jnp.concatenate([1.0 - 2.0 * sine * sine, 2.0 * sine * cosine], 1)
    result = dot3(split(phase), (high[...], low[...]))
    rows = result.shape[0]

    def store(out, first, count):
        for m in range(mrows):
            out[pl.ds(m, count, stride=mrows), :] = result[first : first + count, m * 128 : (m + 1) * 128]

    if parts == 1:
        store(outs[0], 0, rows)
        return
    each = outs[0].shape[0] // mrows
    per_step = rows // each
    for i in range(parts // per_step):

        @pl.when(pl.program_id(0) == i)
        def _():
            for j in range(per_step):
                store(outs[i * per_step + j], j * each, each)


def interpolate(grid_rows, lattice, high, low, mrows, parts, ready):
    rows = grid_rows.shape[0]
    unit = rows // parts if parts > 1 else 8
    step = max(n for n in range(unit, 257, unit) if rows % n == 0)
    whole = lambda a: pl.BlockSpec(a.shape, lambda i: (0, 0))
    if parts == 1:
        out_specs = [pl.BlockSpec((step * mrows, 128), lambda i: (i, 0))]
    else:
        out_specs = [pl.BlockSpec((unit * mrows, 128), lambda i: (0, 0))] * parts
    return pl.pallas_call(
        lambda *refs: interpolate_kernel(*refs, mrows=mrows, parts=parts),
        out_shape=[jax.ShapeDtypeStruct((rows // parts * mrows, 128), jnp.float32)] * parts,
        grid=(rows // step,),
        in_specs=[
            pl.BlockSpec((step, grid_rows.shape[1]), lambda i: (i, 0)),
            whole(lattice),
            whole(high),
            whole(low),
        ]
        + [pl.BlockSpec(memory_space=pl.ANY)] * len(ready),
        out_specs=out_specs,
        name="interpolate",
    )(grid_rows, lattice, high, low, *ready)


def rotate_one(values, u, far, orbitals):
    lanes = 2 * orbitals
    first = lax.broadcasted_iota(jnp.int32, (orbitals, lanes), 1) < orbitals
    first_all = lax.broadcasted_iota(jnp.int32, (values.shape[0], lanes), 1) < orbitals
    u_turned = pltpu.roll(u, orbitals, 1)
    u_full = jnp.concatenate([u, jnp.where(first, -u_turned, u_turned)], 0)
    right = dot3(split(values), split(u_full))
    turned = pltpu.roll(right, orbitals, 1)
    turned = jnp.where(first_all, turned, -turned)
    v = far.T
    left = jnp.concatenate([v[:orbitals], v[orbitals:]], 1)
    modes = values.shape[0] // orbitals
    by_mode = lambda x: jnp.concatenate([x[a * orbitals : (a + 1) * orbitals] for a in range(modes)], 1)
    done = dot3(split(left), split(jnp.concatenate([by_mode(right), by_mode(turned)], 0)))
    return [done[:, a * lanes : (a + 1) * lanes] for a in range(modes)]


def rotate_kernel(place, far_at, *refs, block, mrows, parts, stores, held, start):
    pieces = refs[:parts]
    near = refs[parts]
    far_stores = refs[parts + 1 : parts + 1 + stores * block]
    out, gathered = refs[-2:]
    orbitals = near.shape[1]
    for k in range(block):
        if parts == 1 and mrows:
            values = pieces[0][:, k * mrows : (k + 1) * mrows, :].reshape(gathered.shape[1:])
        elif mrows:
            for s in range(parts):
                at = pl.multiple_of((place[0] ^ s) * mrows, mrows)
                gathered[k, pl.ds(at, mrows), :] = pieces[s][k * mrows : (k + 1) * mrows, :]
            values = gathered[k]
        else:
            values = pieces[0][k]
        at = far_at[start + pl.program_id(0) * block + k]
        far = far_stores[k][0]
        for n in range(1, stores):
            far = jnp.where(at >= n * held, far_stores[n * block + k][0], far)
        for a, done in enumerate(rotate_one(values, near[k], far, orbitals)):
            out[k, a] = done


def rotate(pieces, near, far_stores, far_at, mrows, modes, start, place, before):
    total, orbitals = near.shape[:2]
    block = 8
    first = start // block
    lanes = 2 * orbitals
    if mrows and len(pieces) == 1:
        kpoints = pieces[0].shape[1] // mrows
        piece_spec = pl.BlockSpec((pieces[0].shape[0], block * mrows, lanes), lambda i, *_: (0, i, 0))
    elif mrows:
        kpoints = pieces[0].shape[0] // mrows
        piece_spec = pl.BlockSpec((block * mrows, lanes), lambda i, *_: (i, 0))
    else:
        kpoints = pieces[0].shape[0]
        piece_spec = pl.BlockSpec((block, modes * orbitals, lanes), lambda i, *_: (i, 0, 0))
    prior = [] if before is None else [before]
    stores = len(far_stores)
    held = far_stores[0].shape[0]

    def far_spec(k):
        return pl.BlockSpec(
            (1, orbitals, lanes), lambda i, _, at: (lax.rem(at[start + i * block + k], held), 0, 0)
        )

    return pl.pallas_call(
        lambda *refs: rotate_kernel(
            *refs, block=block, mrows=mrows, parts=len(pieces), stores=stores, held=held, start=start
        ),
        out_shape=jax.ShapeDtypeStruct((total, modes, orbitals, lanes), jnp.float32),
        grid_spec=pltpu.PrefetchScalarGridSpec(
            num_scalar_prefetch=2,
            grid=(kpoints // block,),
            in_specs=[piece_spec] * len(pieces)
            + [pl.BlockSpec((block, orbitals, lanes), lambda i, *_: (first + i, 0, 0))]
            + [far_spec(k) for k in range(block)] * stores
            + [pl.BlockSpec(memory_space=pl.ANY)] * len(prior),
            out_specs=pl.BlockSpec((block, modes, orbitals, lanes), lambda i, *_: (first + i, 0, 0, 0)),
            scratch_shapes=[pltpu.VMEM((block, modes * orbitals, lanes), jnp.float32)],
        ),
        input_output_aliases={len(pieces) + stores * block + 3: 0} if prior else {},
        name="rotate",
    )(place, far_at, *pieces, near, *[x for x in far_stores for _ in range(block)], *prior)


def exchange(x):
    return lax.all_to_all(x, "ka", split_axis=0, concat_axis=0, tiled=True)


def send(blocks, patterns, devices):
    return [lax.ppermute(blocks[s], "ka", [(d, d ^ s) for d in range(devices)]) for s in patterns]


def picks(asked, value, capacity):
    position = jnp.cumsum(asked.astype(jnp.int32), -1) - 1
    chosen = asked[..., None, :] & (position[..., None, :] == jnp.arange(capacity)[:, None])
    return jnp.sum(jnp.where(chosen, value[..., None, :], 0), -1)


def rank(owner, devices):
    same = (owner[:, None] == jnp.arange(devices, dtype=jnp.int32)[None, :]).astype(jnp.int32)
    return jnp.sum((jnp.cumsum(same, 0) - same) * same, 1)


def placed_local(wannier_table, lattice, kpoint_grid, eigen_vectors, target_owner, target_slot):
    kpoints, orbitals = eigen_vectors.shape[:2]
    vectors, pairs = wannier_table.shape[1:]
    devices = lax.axis_size("ka")
    groups = lax.axis_size("grp")
    me = lax.axis_index("ka")
    mrows = pairs // orbitals
    modes = devices * mrows // orbitals
    lanes = 2 * orbitals
    capacity = 2 * kpoints // devices
    tiled = mrows % 8 == 0
    relayed = devices <= RELAYED and devices & (devices - 1) == 0 and tiled
    place = me.astype(jnp.int32).reshape(1)
    lattice_rows = jnp.concatenate([lattice, jnp.zeros((5, vectors), jnp.int32)], 0).astype(jnp.float32)

    own = jnp.concatenate(
        [kpoint_grid, target_owner[None], target_slot[None], jnp.zeros((3, kpoints), jnp.int32)], 0
    )
    everyone = lax.all_to_all(
        jnp.broadcast_to(own[None], (groups * devices, 8, kpoints)),
        ("grp", "ka"),
        split_axis=0,
        concat_axis=0,
        tiled=True,
    ).reshape(groups, devices, 8, kpoints)
    known = lax.dynamic_index_in_dim(everyone, lax.axis_index("grp"), 0, keepdims=False)
    far_rank = rank(target_owner, devices)

    def fill(rows, high, low, parts, ready=()):
        count = rows.shape[0] * rows.shape[1]
        return interpolate(rows.reshape(count, 8), lattice_rows, high, low, mrows, parts, ready)

    def plain():
        wanted = picks(known[:, 3] == me, known[:, 4], capacity)
        picked = eigen_vectors[wanted.reshape(-1)].reshape(devices, capacity * orbitals, lanes)
        fetched = exchange(picked).reshape(devices * capacity, orbitals, lanes)
        far_at = target_owner * capacity + far_rank
        high, low = prepare_table(wannier_table)
        [values] = fill(known.transpose(0, 2, 1).astype(jnp.float32), high, low, 1)
        pieces = exchange(values.reshape(devices, kpoints * mrows, lanes))
        if not tiled:
            pieces = pieces.reshape(devices, kpoints, mrows, lanes).transpose(1, 0, 2, 3)
            pieces = pieces.reshape(kpoints, devices * mrows, lanes)
        mrows_or_none = mrows if tiled else 0
        return rotate([pieces], eigen_vectors, [fetched], far_at, mrows_or_none, modes, 0, place, None)

    if not relayed:
        return plain()

    half = devices // 2
    side = me // half
    mirror = me ^ half
    in_half = [list(range(half)), list(range(half, devices))]
    near_known = lax.dynamic_slice_in_dim(known, side * half, half, 0)
    away_known = lax.dynamic_slice_in_dim(known, (1 - side) * half, half, 0)
    side_of = jnp.arange(devices, dtype=jnp.int32)[None, :, None] // half
    crossing = everyone[:, :, 3] // half != side_of
    owners = jnp.arange(devices, dtype=jnp.int32)
    counts = jnp.sum(
        (crossing & (everyone[:, :, 3] == owners[:, None, None, None])).astype(jnp.int32), (2, 3)
    )
    fits = jnp.max(counts) <= CROSSING * kpoints // 64

    def serve(held, wanted):
        picked = held[wanted.reshape(-1)].reshape(half, capacity * orbitals, lanes)
        got = lax.all_to_all(
            picked, "ka", split_axis=0, concat_axis=0, tiled=True, axis_index_groups=in_half
        )
        return got.reshape(half * capacity, orbitals, lanes)

    def asked_slots(block, owner):
        hit = (block[:, 3] == owner)[..., None] & (block[:, 4][..., None] == jnp.arange(kpoints))
        return jnp.any(hit, (0, 1))

    def relay(room):
        slots = jnp.arange(kpoints, dtype=jnp.int32)
        leaving = picks(asked_slots(away_known, me), slots, room)
        mirrored = lax.ppermute(
            eigen_vectors[leaving], "ka", [(d, d ^ half) for d in range(devices)]
        )
        from_near = serve(eigen_vectors, picks(near_known[:, 3] == me, near_known[:, 4], capacity))
        arrived = jnp.cumsum(asked_slots(near_known, mirror).astype(jnp.int32)) - 1
        at_slot = near_known[:, 4][..., None] == slots
        row_of = jnp.sum(jnp.where(at_slot, arrived, 0), -1)
        from_far = serve(mirrored, picks(near_known[:, 3] == mirror, row_of, capacity))

        at = target_owner % half * capacity + far_rank
        far_at = jnp.where(target_owner // half == side, at, at + half * capacity)

        high, low = prepare_table(wannier_table)
        grid_rows = known.transpose(0, 2, 1).astype(jnp.float32)
        turned_rows = grid_rows[me ^ owners]
        edges = [0, kpoints // 2, kpoints // 4 * 3, kpoints]
        sent = []
        for start, end in zip(edges, edges[1:]):
            last = end == kpoints
            rows = (grid_rows if last else turned_rows)[:, start:end]
            values = fill(rows, high, low, 1 if last else devices, [far_at])
            if last:
                sent.append([exchange(values[0].reshape(devices, (end - start) * mrows, lanes))])
            else:
                crossed = send(values, range(half, half + LEADING), devices)
                crossed += send(values, range(half + LEADING, devices), devices)
                sent.append([values[0]] + send(values, range(1, half), devices) + crossed)

        out = None
        for c, pieces in enumerate(sent):
            out = rotate(
                pieces, eigen_vectors, [from_near, from_far], far_at, mrows, modes, edges[c], place, out
            )
        return out

    if FORCE:
        return relay(FORCE)
    return lax.cond(fits, lambda: relay(CROSSING * kpoints // 64), plain)


def solution(mesh):
    placed = (
        P(None, "grp", "ka"),
        P(None, "grp"),
        P(None, ("grp", "ka")),
        P(("grp", "ka"), None, None),
        P(("grp", "ka")),
        P(("grp", "ka")),
    )
    return jax.shard_map(
        placed_local,
        mesh=mesh,
        in_specs=placed,
        out_specs=P(("grp", "ka"), None, None, None),
        check_vma=False,
    )
```

time: 244 us -> 273 us (1.12)
  the two profiles are of different devices: /device:TPU:0 before, /device:TPU:9 now
where the time goes in v3:
time: 273 us; the launch traced here: 271 us
  waiting for transfers between devices  102 us (37%)
  starting transfers between devices  79.2 us (29%)
  Pallas kernels  61.9 us (23%)
  local copies, waits for them, and re-layouts  18.8 us (7%)
  other arithmetic  8.14 us (3%)
    ppermute x1, waiting for transfers between devices, relay(): lax.ppermute(eigen_vectors[leaving], 'ka', [(d, d ^ half) for d in range(...  66 us
    ppermute x30, starting transfers between devices, send(): lax.ppermute(blocks[s], 'ka', [(d, d ^ s) for d in range(devices)])  53.5 us
    pallas_call x3, Pallas kernels, interpolate(): pl.pallas_call(lambda *refs: interpolate_kernel(*refs, mrows=mrows, parts...  33 us
    ppermute x30, waiting for transfers between devices, send(): lax.ppermute(blocks[s], 'ka', [(d, d ^ s) for d in range(devices)])  26.9 us
    pallas_call x3, Pallas kernels, rotate(): pl.pallas_call(lambda *refs: rotate_kernel(*refs, block=block, mrows=mrow...  20.8 us
    all_to_all x2, starting transfers between devices, serve(): lax.all_to_all(picked, 'ka', split_axis=0, concat_axis=0, tiled=True, axi...  13.5 us
    pallas_call x1, Pallas kernels, prepare_table(): pl.pallas_call(table_kernel, out_shape=[jax.ShapeDtypeStruct((2, vectors,...  8.13 us
    gather x2, local copies, waits for them, and re-layouts, serve(): picked = held[wanted.reshape(-1)].reshape(half, capacity * orbitals, lanes)  7.05 us
  transfers between devices with their start and end apart: 35, of which 15 were waited for; matrix products, arithmetic and copies ran while one was open for 5% of the time, Pallas kernels for 21%

profile of v3, /device:TPU:9, one launch (start us, length us, event | category | flops | bytes accessed | tf_op | source)
XLA Modules:
  0.0 271.1 jit_solution(11114497167080509147)
XLA Ops:
  1.6 6.3 %all-to-all-start.5 = ((s32[32,1,512]{2,1,0:T(1,128)}), s32[32,1,512]{2,1,0:T(1,128)S(1)}, u32[]{:S(2)}, u32[]{:S(2)}) async-start(s32[32,1,512]{2,1,0:T(1,128)} %reshape.380), calls=%async_computation.5 | async-start | bytes 131072 | tf_op jit(solution)/shard_map/all_to_all | solution.py:248
  10.4 3.6 %all-to-all-done.5 = s32[32,1,512]{2,1,0:T(1,128)S(1)} async-done(((s32[32,1,512]{2,1,0:T(1,128)}), s32[32,1,512]{2,1,0:T(1,128)S(1)}, u32[]{:S(2)}, u32[]{:S(2)}) %all-to-all-start.5) | async-done | bytes 65568 | tf_op jit(solution)/shard_map/all_to_all | solution.py:248
  17.4 253.5 %conditional.1 = (f32[64,2,64,128]{3,2,1,0:T(8,128)}) conditional(s32[]{:T(128)} %convert_element_type.59, (s32[64]{0:T(128)}, s32[64]{0:T(128)S(1)}, s32[16,8,64]{2,1,0:T(8,128)S(1)}, f32[2,1024,512]{2,1,0:T(8,128)}, f32[8,1024]{1,0:T(8,128)S(1)}, /*index=5*/s32[]{:T(128)}, f32[64,64,128]{2,1,0:T(8,128)}, s32[1]{0:T(128)}) %tuple.42, (s32[64]{0:T(128)}, ...), branch_computations={%region_4.7_spmd, %region_7.18_spmd} | conditional | flops 430009 | bytes 70533424 | solution.py:344
  18.1 3.6 %gather_fusion = f32[64,64,128]{2,1,0:T(8,128)} fusion(f32[64,64,128]{2,1,0:T(8,128)} %get-tuple-element.140.refs_18_.refs_3_, s32[1024]{0:T(1024)S(1)} %pad_clamp_fusion.4), kind=kCustom, calls=%fused_computation.1 | custom fusion | bytes 4194560 | tf_op jit(solution)/shard_map/cond/branch_1_fun/gather | solution.py:294
  21.7 5.2 %all-to-all-start.1 = ((f32[8,512,128]{2,1,0:T(8,128)}), f32[8,512,128]{2,1,0:T(8,128)S(1)}, u32[]{:S(2)}, u32[]{:S(2)}) async-start(f32[8,512,128]{2,1,0:T(8,128)} %bitcast.94), calls=%async_computation.1 | async-start | bytes 4194304 | tf_op jit(solution)/shard_map/cond/branch_1_fun/all_to_all | solution.py:295
  27.6 3.4 %gather_fusion.1 = f32[48,64,128]{2,1,0:T(8,128)} fusion(f32[64,64,128]{2,1,0:T(8,128)} %get-tuple-element.140.refs_18_.refs_3_, s32[1024]{0:T(1024)S(1)} %pad_clamp_fusion.3), kind=kCustom, calls=%fused_computation.2 | custom fusion | bytes 3145920 | tf_op jit(solution)/shard_map/cond/branch_1_fun/gather | solution.py:308
  32.8 66.0 %collective-permute-done = f32[48,64,128]{2,1,0:T(8,128)} collective-permute-done((f32[48,64,128]{2,1,0:T(8,128)}, f32[48,64,128]{2,1,0:T(8,128)}, u32[]{:S(2)}, u32[]{:S(2)}) %collective-permute-start) | collective-permute-done | bytes 1572896 | tf_op jit(solution)/shard_map/cond/branch_1_fun/ppermute | solution.py:307
  98.8 3.5 %gather_fusion.2 = f32[64,64,128]{2,1,0:T(8,128)} fusion(f32[48,64,128]{2,1,0:T(8,128)} %collective-permute-done, s32[1024]{0:T(1024)S(1)} %pad_clamp_fusion.2), kind=kCustom, calls=%fused_computation.3 | custom fusion | bytes 4194560 | tf_op jit(solution)/shard_map/cond/branch_1_fun/gather | solution.py:294
  103.6 8.2 %all-to-all-start.2 = ((f32[8,512,128]{2,1,0:T(8,128)}), f32[8,512,128]{2,1,0:T(8,128)}, u32[]{:S(2)}, u32[]{:S(2)}) async-start(f32[8,512,128]{2,1,0:T(8,128)} %bitcast.95), calls=%async_computation.2 | async-start | bytes 4194304 | tf_op jit(solution)/shard_map/cond/branch_1_fun/all_to_all | solution.py:295
  112.7 8.1 %table.3 = (bf16[2,1024,1024]{2,1,0:T(8,128)(2,1)}, bf16[2,1024,1024]{2,1,0:T(8,128)(2,1)}) custom-call(f32[2,1024,512]{2,1,0:T(8,128)} %get-tuple-element.137.table), custom_call_target="tpu_custom_call" | custom-call | tf_op jit(solution)/shard_map/cond/branch_1_fun/table/pallas_call | solution.py:63
  121.4 9.2 %interpolate.5 = f32[2048,128]{1,0:T(8,128)} custom-call(f32[256,8]{1,0:T(8,128)} %bitcast.105, f32[8,1024]{1,0:T(8,128)S(1)} %get-tuple-element.136.refs_1_, bf16[2048,1024]{1,0:T(8,128)(2,1)} %bitcast.86, bf16[2048,1024]{1,0:T(8,128)(2,1)} %bitcast.89, s32[64]{0:T(128)} %compare_select_fusion.5.refs_4_.refs_1_), custom_call_target="tpu_custom_call" | custom-call | tf_op jit(solution)/shard_map/cond/branch_1_fun/interpolate/pallas_call | solution.py:111
  130.6 5.0 %all-to-all-done.2 = f32[8,512,128]{2,1,0:T(8,128)} async-done(((f32[8,512,128]{2,1,0:T(8,128)}), f32[8,512,128]{2,1,0:T(8,128)}, u32[]{:S(2)}, u32[]{:S(2)}) %all-to-all-start.2) | async-done | bytes 2097184 | tf_op jit(solution)/shard_map/cond/branch_1_fun/all_to_all | solution.py:295
  135.6 5.5 %all-to-all-start = ((f32[16,128,128]{2,1,0:T(8,128)}), f32[16,128,128]{2,1,0:T(8,128)S(1)}, u32[]{:S(2)}, u32[]{:S(2)}) async-start(f32[16,128,128]{2,1,0:T(8,128)} %bitcast.98), calls=%async_computation | async-start | bytes 2097152 | tf_op jit(solution)/shard_map/cond/branch_1_fun/all_to_all | solution.py:212
  142.4 9.2 %interpolate.6 = (f32[128,128]{1,0:T(8,128)}, f32[128,128]{1,0:T(8,128)}, f32[128,128]{1,0:T(8,128)}, f32[128,128]{1,0:T(8,128)}, f32[128,128]{1,0:T(8,128)}, /*...) custom-call(f32[256,8]{1,0:T(8,128)} %bitcast.104, ...), custom_call_target="tpu_custom_call" | custom-call | tf_op jit(solution)/shard_map/cond/branch_1_fun/interpolate/pallas_call | solution.py:111
  157.0 3.3 %collective-permute-start.7 = (f32[128,128]{1,0:T(8,128)}, f32[128,128]{1,0:T(8,128)S(1)}, u32[]{:S(2)}, u32[]{:S(2)}) collective-permute-start(f32[128,128]{1,0:T(8,128)} %get-tuple-element.151), channel_id=1, source_target_pairs={{0,7},{1,6},{2,5},{3,4},{4,3},{5,2},{6,1},{7,0},{8,15},{9,14},{10,... | collective-permute-start | bytes 196616 | tf_op jit(solution)/shard_map/cond/branch_1_fun/ppermute | solution.py:216
  161.7 2.1 collective-permute-start.9
  163.8 3.2 %collective-permute-start.10 = (f32[128,128]{1,0:T(8,128)}, f32[128,128]{1,0:T(8,128)}, u32[]{:S(2)}, u32[]{:S(2)}) collective-permute-start(f32[128,128]{1,0:T(8,128)} %get-tuple-element.154), channel_id=1, source_target_pairs={{0,10},{1,11},{2,8},{3,9},{4,14},{5,15},{6,12},{7,13},{8,2},{9,3},... | collective-permute-start | bytes 196616 | tf_op jit(solution)/shard_map/cond/branch_1_fun/ppermute | solution.py:216
  167.8 14.7 %interpolate.7 = (f32[256,128]{1,0:T(8,128)}, f32[256,128]{1,0:T(8,128)}, f32[256,128]{1,0:T(8,128)}, f32[256,128]{1,0:T(8,128)}, f32[256,128]{1,0:T(8,128)}, /*...) custom-call(f32[512,8]{1,0:T(8,128)} %bitcast.100, ...), custom_call_target="tpu_custom_call" | custom-call | tf_op jit(solution)/shard_map/cond/branch_1_fun/interpolate/pallas_call | solution.py:111
  189.1 1.8 collective-permute-start.22
  190.9 1.7 collective-permute-done.18.refs_5_
  192.9 2.0 collective-permute-start.24
  198.1 7.7 %collective-permute-start.26 = (f32[256,128]{1,0:T(8,128)}, f32[256,128]{1,0:T(8,128)}, u32[]{:S(2)}, u32[]{:S(2)}) collective-permute-start(f32[256,128]{1,0:T(8,128)} %get-tuple-element.171), channel_id=1, source_target_pairs={{0,11},{1,10},{2,9},{3,8},{4,15},{5,14},{6,13},{7,12},{8,3},{9,2},... | collective-permute-start | bytes 393224 | tf_op jit(solution)/shard_map/cond/branch_1_fun/ppermute | solution.py:216
  206.8 10.7 %collective-permute-start.29 = (f32[256,128]{1,0:T(8,128)}, f32[256,128]{1,0:T(8,128)}, u32[]{:S(2)}, u32[]{:S(2)}) collective-permute-start(f32[256,128]{1,0:T(8,128)} %get-tuple-element.174), channel_id=1, source_target_pairs={{0,14},{1,15},{2,12},{3,13},{4,10},{5,11},{6,8},{7,9},{8,6},{9,7},... | collective-permute-start | bytes 393224 | tf_op jit(solution)/shard_map/cond/branch_1_fun/ppermute | solution.py:216
  220.3 4.1 %collective-permute-done.26.refs_13_ = f32[256,128]{1,0:T(8,128)} collective-permute-done((f32[256,128]{1,0:T(8,128)}, f32[256,128]{1,0:T(8,128)}, u32[]{:S(2)}, u32[]{:S(2)}) %collective-permute-start.26) | collective-permute-done | bytes 131104 | tf_op jit(solution)/shard_map/cond/branch_1_fun/ppermute | solution.py:216
  224.4 4.3 %collective-permute-start.11 = (f32[128,128]{1,0:T(8,128)}, f32[128,128]{1,0:T(8,128)}, u32[]{:S(2)}, u32[]{:S(2)}) collective-permute-start(f32[128,128]{1,0:T(8,128)} %get-tuple-element.155), channel_id=1, source_target_pairs={{0,11},{1,10},{2,9},{3,8},{4,15},{5,14},{6,13},{7,12},{8,3},{9,2},... | collective-permute-start | bytes 196616 | tf_op jit(solution)/shard_map/cond/branch_1_fun/ppermute | solution.py:216
  228.6 9.3 %collective-permute-done.27.refs_14_ = f32[256,128]{1,0:T(8,128)} collective-permute-done((f32[256,128]{1,0:T(8,128)}, f32[256,128]{1,0:T(8,128)}, u32[]{:S(2)}, u32[]{:S(2)}) %collective-permute-start.27) | collective-permute-done | bytes 131104 | tf_op jit(solution)/shard_map/cond/branch_1_fun/ppermute | solution.py:216
  239.2 3.0 %collective-permute-done.28.refs_15_ = f32[256,128]{1,0:T(8,128)} collective-permute-done((f32[256,128]{1,0:T(8,128)}, f32[256,128]{1,0:T(8,128)}, u32[]{:S(2)}, u32[]{:S(2)}) %collective-permute-start.28) | collective-permute-done | bytes 131104 | tf_op jit(solution)/shard_map/cond/branch_1_fun/ppermute | solution.py:216
  242.3 2.3 collective-permute-done.29.refs_16_
  245.7 1.7 collective-permute-done.30.refs_17_
  248.8 9.4 %rotate.5.refs_35_ = f32[64,2,64,128]{3,2,1,0:T(8,128)} custom-call(s32[1]{0:T(128)} %get-tuple-element.128.refs_0_, s32[64]{0:T(128)} %compare_select_fusion.5.refs_4_.refs_1_, f32[256,128]{1,0:T(8,128)} %get-tuple-element.160.refs_2_, f32[256,128]{1,0:T(8,128)} %copy-done.4, f32[256,128]{1,0:T(8,128)} %copy-done.5, f32[256,128]{1,0:T(8,128)} %copy-done.6, ...), custom_call_target="tpu_custom_call" | custom-call | tf_op jit(solution)/shard_map/cond/branch_1_fun/rotate/pallas_call | solution.py:191
  258.3 5.8 %rotate.6.refs_20_ = f32[64,2,64,128]{3,2,1,0:T(8,128)} custom-call(s32[1]{0:T(128)} %get-tuple-element.128.refs_0_, s32[64]{0:T(128)} %compare_select_fusion.5.refs_4_.refs_1_, f32[128,128]{1,0:T(8,128)} %get-tuple-element.144.refs_2_, f32[128,128]{1,0:T(8,128)} %copy-done.7, f32[128,128]{1,0:T(8,128)} %copy-done.8, ...), custom_call_target="tpu_custom_call", output_to_operand_aliasing={{}: (35, {})} | custom-call | tf_op jit(solution)/shard_map/cond/branch_1_fun/rotate/pallas_call | solution.py:191
  265.1 5.6 %rotate.7 = f32[64,2,64,128]{3,2,1,0:T(8,128)} custom-call(s32[1]{0:T(128)} %get-tuple-element.128.refs_0_, s32[64]{0:T(128)} %compare_select_fusion.5.refs_4_.refs_1_, f32[16,128,128]{2,1,0:T(8,128)} %copy-done.3, f32[64,64,128]{2,1,0:T(8,128)S(1)} %copy-done.2, f32[64,64,128]{2,1,0:T(8,128)} %bitcast.78, ...), custom_call_target="tpu_custom_call", output_to_operand_aliasing={{}: (20, {})} | custom-call | tf_op jit(solution)/shard_map/cond/branch_1_fun/rotate/pallas_call | solution.py:191
  (138 shorter events, 39.9 us)
Async XLA Ops:
  1.6 12.3 %all-to-all-start.5 = ((s32[32,1,512]{2,1,0:T(1,128)}), s32[32,1,512]{2,1,0:T(1,128)S(1)}, u32[]{:S(2)}, u32[]{:S(2)}) async-start(s32[32,1,512]{2,1,0:T(1,128)} %reshape.380), calls=%async_computation.5 | async-start | bytes 131072 | tf_op jit(solution)/shard_map/all_to_all | solution.py:248
  21.7 80.5 %all-to-all-start.1 = ((f32[8,512,128]{2,1,0:T(8,128)}), f32[8,512,128]{2,1,0:T(8,128)S(1)}, u32[]{:S(2)}, u32[]{:S(2)}) async-start(f32[8,512,128]{2,1,0:T(8,128)} %bitcast.94), calls=%async_computation.1 | async-start | bytes 4194304 | tf_op jit(solution)/shard_map/cond/branch_1_fun/all_to_all | solution.py:295
  31.0 67.8 %collective-permute-start = (f32[48,64,128]{2,1,0:T(8,128)}, f32[48,64,128]{2,1,0:T(8,128)}, u32[]{:S(2)}, u32[]{:S(2)}) collective-permute-start(f32[48,64,128]{2,1,0:T(8,128)} %gather_fusion.1), channel_id=1, source_target_pairs={{0,8},{1,9},{2,10},{3,11},{4,12},{5,13},{6,14},{7,15},{8,0},{9,1},... | collective-permute-start | bytes 4718600 | tf_op jit(solution)/shard_map/cond/branch_1_fun/ppermute | solution.py:307
  103.6 32.0 %all-to-all-start.2 = ((f32[8,512,128]{2,1,0:T(8,128)}), f32[8,512,128]{2,1,0:T(8,128)}, u32[]{:S(2)}, u32[]{:S(2)}) async-start(f32[8,512,128]{2,1,0:T(8,128)} %bitcast.95), calls=%async_computation.2 | async-start | bytes 4194304 | tf_op jit(solution)/shard_map/cond/branch_1_fun/all_to_all | solution.py:295
  135.6 128.5 %all-to-all-start = ((f32[16,128,128]{2,1,0:T(8,128)}), f32[16,128,128]{2,1,0:T(8,128)S(1)}, u32[]{:S(2)}, u32[]{:S(2)}) async-start(f32[16,128,128]{2,1,0:T(8,128)} %bitcast.98), calls=%async_computation | async-start | bytes 2097152 | tf_op jit(solution)/shard_map/cond/branch_1_fun/all_to_all | solution.py:212
  153.1 7.5 %collective-permute-start.3 = (f32[128,128]{1,0:T(8,128)}, f32[128,128]{1,0:T(8,128)S(1)}, u32[]{:S(2)}, u32[]{:S(2)}) collective-permute-start(f32[128,128]{1,0:T(8,128)} %get-tuple-element.147), channel_id=1, source_target_pairs={{0,3},{1,2},{2,1},{3,0},{4,7},{5,6},{6,5},{7,4},{8,11},{9,10},{10,... | collective-permute-start | bytes 196616 | tf_op jit(solution)/shard_map/cond/branch_1_fun/ppermute | solution.py:216
  153.7 8.0 %collective-permute-start.4 = (f32[128,128]{1,0:T(8,128)}, f32[128,128]{1,0:T(8,128)S(1)}, u32[]{:S(2)}, u32[]{:S(2)}) collective-permute-start(f32[128,128]{1,0:T(8,128)} %get-tuple-element.148), channel_id=1, source_target_pairs={{0,4},{1,5},{2,6},{3,7},{4,0},{5,1},{6,2},{7,3},{8,12},{9,13},{10,... | collective-permute-start | bytes 196616 | tf_op jit(solution)/shard_map/cond/branch_1_fun/ppermute | solution.py:216
  153.8 10.0 %collective-permute-start.5 = (f32[128,128]{1,0:T(8,128)}, f32[128,128]{1,0:T(8,128)S(1)}, u32[]{:S(2)}, u32[]{:S(2)}) collective-permute-start(f32[128,128]{1,0:T(8,128)} %get-tuple-element.149), channel_id=1, source_target_pairs={{0,5},{1,4},{2,7},{3,6},{4,1},{5,0},{6,3},{7,2},{8,13},{9,12},{10,... | collective-permute-start | bytes 196616 | tf_op jit(solution)/shard_map/cond/branch_1_fun/ppermute | solution.py:216
  155.4 27.0 %collective-permute-start.6 = (f32[128,128]{1,0:T(8,128)}, f32[128,128]{1,0:T(8,128)S(1)}, u32[]{:S(2)}, u32[]{:S(2)}) collective-permute-start(f32[128,128]{1,0:T(8,128)} %get-tuple-element.150), channel_id=1, source_target_pairs={{0,6},{1,7},{2,4},{3,5},{4,2},{5,3},{6,0},{7,1},{8,14},{9,15},{10,... | collective-permute-start | bytes 196616 | tf_op jit(solution)/shard_map/cond/branch_1_fun/ppermute | solution.py:216
  157.0 26.1 %collective-permute-start.7 = (f32[128,128]{1,0:T(8,128)}, f32[128,128]{1,0:T(8,128)S(1)}, u32[]{:S(2)}, u32[]{:S(2)}) collective-permute-start(f32[128,128]{1,0:T(8,128)} %get-tuple-element.151), channel_id=1, source_target_pairs={{0,7},{1,6},{2,5},{3,4},{4,3},{5,2},{6,1},{7,0},{8,15},{9,14},{10,... | collective-permute-start | bytes 196616 | tf_op jit(solution)/shard_map/cond/branch_1_fun/ppermute | solution.py:216
  160.6 24.8 %collective-permute-start.8 = (f32[128,128]{1,0:T(8,128)}, f32[128,128]{1,0:T(8,128)S(1)}, u32[]{:S(2)}, u32[]{:S(2)}) collective-permute-start(f32[128,128]{1,0:T(8,128)} %get-tuple-element.152), channel_id=1, source_target_pairs={{0,8},{1,9},{2,10},{3,11},{4,12},{5,13},{6,14},{7,15},{8,0},{9,1},... | collective-permute-start | bytes 196616 | tf_op jit(solution)/shard_map/cond/branch_1_fun/ppermute | solution.py:216
  161.7 24.8 %collective-permute-start.9 = (f32[128,128]{1,0:T(8,128)}, f32[128,128]{1,0:T(8,128)}, u32[]{:S(2)}, u32[]{:S(2)}) collective-permute-start(f32[128,128]{1,0:T(8,128)} %get-tuple-element.153), channel_id=1, source_target_pairs={{0,9},{1,8},{2,11},{3,10},{4,13},{5,12},{6,15},{7,14},{8,1},{9,0},... | collective-permute-start | bytes 196616 | tf_op jit(solution)/shard_map/cond/branch_1_fun/ppermute | solution.py:216
  163.8 22.6 %collective-permute-start.10 = (f32[128,128]{1,0:T(8,128)}, f32[128,128]{1,0:T(8,128)}, u32[]{:S(2)}, u32[]{:S(2)}) collective-permute-start(f32[128,128]{1,0:T(8,128)} %get-tuple-element.154), channel_id=1, source_target_pairs={{0,10},{1,11},{2,8},{3,9},{4,14},{5,15},{6,12},{7,13},{8,2},{9,3},... | collective-permute-start | bytes 196616 | tf_op jit(solution)/shard_map/cond/branch_1_fun/ppermute | solution.py:216
  182.5 5.6 %collective-permute-start.16 = (f32[256,128]{1,0:T(8,128)}, f32[256,128]{1,0:T(8,128)S(1)}, u32[]{:S(2)}, u32[]{:S(2)}) collective-permute-start(f32[256,128]{1,0:T(8,128)} %get-tuple-element.161), channel_id=1, source_target_pairs={{0,1},{1,0},{2,3},{3,2},{4,5},{5,4},{6,7},{7,6},{8,9},{9,8},{10,11... | collective-permute-start | bytes 393224 | tf_op jit(solution)/shard_map/cond/branch_1_fun/ppermute | solution.py:216
  186.1 6.6 %collective-permute-start.18 = (f32[256,128]{1,0:T(8,128)}, f32[256,128]{1,0:T(8,128)S(1)}, u32[]{:S(2)}, u32[]{:S(2)}) collective-permute-start(f32[256,128]{1,0:T(8,128)} %get-tuple-element.163), channel_id=1, source_target_pairs={{0,3},{1,2},{2,1},{3,0},{4,7},{5,6},{6,5},{7,4},{8,11},{9,10},{10,... | collective-permute-start | bytes 393224 | tf_op jit(solution)/shard_map/cond/branch_1_fun/ppermute | solution.py:216
  186.5 6.4 %collective-permute-start.19 = (f32[256,128]{1,0:T(8,128)}, f32[256,128]{1,0:T(8,128)}, u32[]{:S(2)}, u32[]{:S(2)}) collective-permute-start(f32[256,128]{1,0:T(8,128)} %get-tuple-element.164), channel_id=1, source_target_pairs={{0,4},{1,5},{2,6},{3,7},{4,0},{5,1},{6,2},{7,3},{8,12},{9,13},{10,... | collective-permute-start | bytes 393224 | tf_op jit(solution)/shard_map/cond/branch_1_fun/ppermute | solution.py:216
  186.5 8.8 %collective-permute-start.20 = (f32[256,128]{1,0:T(8,128)}, f32[256,128]{1,0:T(8,128)}, u32[]{:S(2)}, u32[]{:S(2)}) collective-permute-start(f32[256,128]{1,0:T(8,128)} %get-tuple-element.165), channel_id=1, source_target_pairs={{0,5},{1,4},{2,7},{3,6},{4,1},{5,0},{6,3},{7,2},{8,13},{9,12},{10,... | collective-permute-start | bytes 393224 | tf_op jit(solution)/shard_map/cond/branch_1_fun/ppermute | solution.py:216
  188.1 10.0 %collective-permute-start.21 = (f32[256,128]{1,0:T(8,128)}, f32[256,128]{1,0:T(8,128)}, u32[]{:S(2)}, u32[]{:S(2)}) collective-permute-start(f32[256,128]{1,0:T(8,128)} %get-tuple-element.166), channel_id=1, source_target_pairs={{0,6},{1,7},{2,4},{3,5},{4,2},{5,3},{6,0},{7,1},{8,14},{9,15},{10,... | collective-permute-start | bytes 393224 | tf_op jit(solution)/shard_map/cond/branch_1_fun/ppermute | solution.py:216
  189.1 16.8 %collective-permute-start.22 = (f32[256,128]{1,0:T(8,128)}, f32[256,128]{1,0:T(8,128)}, u32[]{:S(2)}, u32[]{:S(2)}) collective-permute-start(f32[256,128]{1,0:T(8,128)} %get-tuple-element.167), channel_id=1, source_target_pairs={{0,7},{1,6},{2,5},{3,4},{4,3},{5,2},{6,1},{7,0},{8,15},{9,14},{10,... | collective-permute-start | bytes 393224 | tf_op jit(solution)/shard_map/cond/branch_1_fun/ppermute | solution.py:216
  192.6 13.3 %collective-permute-start.23 = (f32[256,128]{1,0:T(8,128)}, f32[256,128]{1,0:T(8,128)}, u32[]{:S(2)}, u32[]{:S(2)}) collective-permute-start(f32[256,128]{1,0:T(8,128)} %get-tuple-element.168), channel_id=1, source_target_pairs={{0,8},{1,9},{2,10},{3,11},{4,12},{5,13},{6,14},{7,15},{8,0},{9,1},... | collective-permute-start | bytes 393224 | tf_op jit(solution)/shard_map/cond/branch_1_fun/ppermute | solution.py:216
  192.9 13.9 %collective-permute-start.24 = (f32[256,128]{1,0:T(8,128)}, f32[256,128]{1,0:T(8,128)}, u32[]{:S(2)}, u32[]{:S(2)}) collective-permute-start(f32[256,128]{1,0:T(8,128)} %get-tuple-element.169), channel_id=1, source_target_pairs={{0,9},{1,8},{2,11},{3,10},{4,13},{5,12},{6,15},{7,14},{8,1},{9,0},... | collective-permute-start | bytes 393224 | tf_op jit(solution)/shard_map/cond/branch_1_fun/ppermute | solution.py:216
  195.3 23.5 %collective-permute-start.25 = (f32[256,128]{1,0:T(8,128)}, f32[256,128]{1,0:T(8,128)}, u32[]{:S(2)}, u32[]{:S(2)}) collective-permute-start(f32[256,128]{1,0:T(8,128)} %get-tuple-element.170), channel_id=1, source_target_pairs={{0,10},{1,11},{2,8},{3,9},{4,14},{5,15},{6,12},{7,13},{8,2},{9,3},... | collective-permute-start | bytes 393224 | tf_op jit(solution)/shard_map/cond/branch_1_fun/ppermute | solution.py:216
  198.1 26.2 %collective-permute-start.26 = (f32[256,128]{1,0:T(8,128)}, f32[256,128]{1,0:T(8,128)}, u32[]{:S(2)}, u32[]{:S(2)}) collective-permute-start(f32[256,128]{1,0:T(8,128)} %get-tuple-element.171), channel_id=1, source_target_pairs={{0,11},{1,10},{2,9},{3,8},{4,15},{5,14},{6,13},{7,12},{8,3},{9,2},... | collective-permute-start | bytes 393224 | tf_op jit(solution)/shard_map/cond/branch_1_fun/ppermute | solution.py:216
  205.9 32.1 %collective-permute-start.27 = (f32[256,128]{1,0:T(8,128)}, f32[256,128]{1,0:T(8,128)}, u32[]{:S(2)}, u32[]{:S(2)}) collective-permute-start(f32[256,128]{1,0:T(8,128)} %get-tuple-element.172), channel_id=1, source_target_pairs={{0,12},{1,13},{2,14},{3,15},{4,8},{5,9},{6,10},{7,11},{8,4},{9,5},... | collective-permute-start | bytes 393224 | tf_op jit(solution)/shard_map/cond/branch_1_fun/ppermute | solution.py:216
  205.9 36.3 %collective-permute-start.28 = (f32[256,128]{1,0:T(8,128)}, f32[256,128]{1,0:T(8,128)}, u32[]{:S(2)}, u32[]{:S(2)}) collective-permute-start(f32[256,128]{1,0:T(8,128)} %get-tuple-element.173), channel_id=1, source_target_pairs={{0,13},{1,12},{2,15},{3,14},{4,9},{5,8},{6,11},{7,10},{8,5},{9,4},... | collective-permute-start | bytes 393224 | tf_op jit(solution)/shard_map/cond/branch_1_fun/ppermute | solution.py:216
  206.8 37.9 %collective-permute-start.29 = (f32[256,128]{1,0:T(8,128)}, f32[256,128]{1,0:T(8,128)}, u32[]{:S(2)}, u32[]{:S(2)}) collective-permute-start(f32[256,128]{1,0:T(8,128)} %get-tuple-element.174), channel_id=1, source_target_pairs={{0,14},{1,15},{2,12},{3,13},{4,10},{5,11},{6,8},{7,9},{8,6},{9,7},... | collective-permute-start | bytes 393224 | tf_op jit(solution)/shard_map/cond/branch_1_fun/ppermute | solution.py:216
  218.7 28.7 %collective-permute-start.30 = (f32[256,128]{1,0:T(8,128)}, f32[256,128]{1,0:T(8,128)}, u32[]{:S(2)}, u32[]{:S(2)}) collective-permute-start(f32[256,128]{1,0:T(8,128)} %get-tuple-element.175), channel_id=1, source_target_pairs={{0,15},{1,14},{2,13},{3,12},{4,11},{5,10},{6,9},{7,8},{8,7},{9,6},... | collective-permute-start | bytes 393224 | tf_op jit(solution)/shard_map/cond/branch_1_fun/ppermute | solution.py:216
  224.4 33.9 %collective-permute-start.11 = (f32[128,128]{1,0:T(8,128)}, f32[128,128]{1,0:T(8,128)}, u32[]{:S(2)}, u32[]{:S(2)}) collective-permute-start(f32[128,128]{1,0:T(8,128)} %get-tuple-element.155), channel_id=1, source_target_pairs={{0,11},{1,10},{2,9},{3,8},{4,15},{5,14},{6,13},{7,12},{8,3},{9,2},... | collective-permute-start | bytes 196616 | tf_op jit(solution)/shard_map/cond/branch_1_fun/ppermute | solution.py:216
  238.0 20.3 %collective-permute-start.12 = (f32[128,128]{1,0:T(8,128)}, f32[128,128]{1,0:T(8,128)}, u32[]{:S(2)}, u32[]{:S(2)}) collective-permute-start(f32[128,128]{1,0:T(8,128)} %get-tuple-element.156), channel_id=1, source_target_pairs={{0,12},{1,13},{2,14},{3,15},{4,8},{5,9},{6,10},{7,11},{8,4},{9,5},... | collective-permute-start | bytes 196616 | tf_op jit(solution)/shard_map/cond/branch_1_fun/ppermute | solution.py:216
  242.2 16.1 %collective-permute-start.13 = (f32[128,128]{1,0:T(8,128)}, f32[128,128]{1,0:T(8,128)}, u32[]{:S(2)}, u32[]{:S(2)}) collective-permute-start(f32[128,128]{1,0:T(8,128)} %get-tuple-element.157), channel_id=1, source_target_pairs={{0,13},{1,12},{2,15},{3,14},{4,9},{5,8},{6,11},{7,10},{8,5},{9,4},... | collective-permute-start | bytes 196616 | tf_op jit(solution)/shard_map/cond/branch_1_fun/ppermute | solution.py:216
  244.6 13.6 %collective-permute-start.14 = (f32[128,128]{1,0:T(8,128)}, f32[128,128]{1,0:T(8,128)}, u32[]{:S(2)}, u32[]{:S(2)}) collective-permute-start(f32[128,128]{1,0:T(8,128)} %get-tuple-element.158), channel_id=1, source_target_pairs={{0,14},{1,15},{2,12},{3,13},{4,10},{5,11},{6,8},{7,9},{8,6},{9,7},... | collective-permute-start | bytes 196616 | tf_op jit(solution)/shard_map/cond/branch_1_fun/ppermute | solution.py:216
  247.4 10.9 %collective-permute-start.15 = (f32[128,128]{1,0:T(8,128)}, f32[128,128]{1,0:T(8,128)}, u32[]{:S(2)}, u32[]{:S(2)}) collective-permute-start(f32[128,128]{1,0:T(8,128)} %get-tuple-element.159), channel_id=1, source_target_pairs={{0,15},{1,14},{2,13},{3,12},{4,11},{5,10},{6,9},{7,8},{8,7},{9,6},... | collective-permute-start | bytes 196616 | tf_op jit(solution)/shard_map/cond/branch_1_fun/ppermute | solution.py:216
  (18 other events, 354.0 us)

commit v4 on v3

--- a/solution.py
+++ b/solution.py
@@ -124,48 +124,82 @@
     )(grid_rows, lattice, high, low, *ready)
 
 
-def rotate_one(values, u, far, orbitals):
-    lanes = 2 * orbitals
+def right_turn(values, u):
+    orbitals, lanes = u.shape
     first = lax.broadcasted_iota(jnp.int32, (orbitals, lanes), 1) < orbitals
-    first_all = lax.broadcasted_iota(jnp.int32, (values.shape[0], lanes), 1) < orbitals
     u_turned = pltpu.roll(u, orbitals, 1)
     u_full = jnp.concatenate([u, jnp.where(first, -u_turned, u_turned)], 0)
-    right = dot3(split(values), split(u_full))
+    return dot3(split(values), split(u_full))
+
+
+def left_turn(right, far):
+    orbitals, lanes = far.shape
+    first = lax.broadcasted_iota(jnp.int32, right.shape, 1) < orbitals
     turned = pltpu.roll(right, orbitals, 1)
-    turned = jnp.where(first_all, turned, -turned)
+    turned = jnp.where(first, turned, -turned)
     v = far.T
     left = jnp.concatenate([v[:orbitals], v[orbitals:]], 1)
-    modes = values.shape[0] // orbitals
+    modes = right.shape[0] // orbitals
     by_mode = lambda x: jnp.concatenate([x[a * orbitals : (a + 1) * orbitals] for a in range(modes)], 1)
     done = dot3(split(left), split(jnp.concatenate([by_mode(right), by_mode(turned)], 0)))
     return [done[:, a * lanes : (a + 1) * lanes] for a in range(modes)]
 
 
-def rotate_kernel(place, far_at, *refs, block, mrows, parts, stores, held, start):
+def collect(place, pieces, gathered, k, mrows):
+    parts = len(pieces)
+    if not mrows:
+        return pieces[0][k]
+    if parts == 1:
+        return pieces[0][:, k * mrows : (k + 1) * mrows, :].reshape(gathered.shape[1:])
+    for s in range(parts):
+        at = pl.multiple_of((place[0] ^ s) * mrows, mrows)
+        gathered[k, pl.ds(at, mrows), :] = pieces[s][k * mrows : (k + 1) * mrows, :]
+    return gathered[k]
+
+
+def right_kernel(place, *refs, block, mrows, parts):
+    near, out, gathered = refs[parts:]
+    for k in range(block):
+        out[k] = right_turn(collect(place, refs[:parts], gathered, k, mrows), near[k])
+
+
+def turn_right(pieces, near, mrows, rows, start, place):
+    lanes = near.shape[2]
+    block = 8
+    first = start // block
+    kpoints = pieces[0].shape[0] // mrows
+    return pl.pallas_call(
+        lambda *refs: right_kernel(*refs, block=block, mrows=mrows, parts=len(pieces)),
+        out_shape=jax.ShapeDtypeStruct((kpoints, rows, lanes), jnp.float32),
+        grid_spec=pltpu.PrefetchScalarGridSpec(
+            num_scalar_prefetch=1,
+            grid=(kpoints // block,),
+            in_specs=[pl.BlockSpec((block * mrows, lanes), lambda i, *_: (i, 0))] * len(pieces)
+            + [pl.BlockSpec((block,) + near.shape[1:], lambda i, *_: (first + i, 0, 0))],
+            out_specs=pl.BlockSpec((block, rows, lanes), lambda i, *_: (i, 0, 0)),
+            scratch_shapes=[pltpu.VMEM((block, rows, lanes), jnp.float32)],
+        ),
+        name="turn_right",
+    )(place, *pieces, near)
+
+
+def rotate_kernel(place, far_at, *refs, block, mrows, parts, stores, held, start, turned):
     pieces = refs[:parts]
     near = refs[parts]
     far_stores = refs[parts + 1 : parts + 1 + stores * block]
     out, gathered = refs[-2:]
-    orbitals = near.shape[1]
     for k in range(block):
-        if parts == 1 and mrows:
-            values = pieces[0][:, k * mrows : (k + 1) * mrows, :].reshape(gathered.shape[1:])
-        elif mrows:
-            for s in range(parts):
-                at = pl.multiple_of((place[0] ^ s) * mrows, mrows)
-                gathered[k, pl.ds(at, mrows), :] = pieces[s][k * mrows : (k + 1) * mrows, :]
-            values = gathered[k]
-        else:
-            values = pieces[0][k]
+        values = collect(place, pieces, gathered, k, mrows)
         at = far_at[start + pl.program_id(0) * block + k]
         far = far_stores[k][0]
         for n in range(1, stores):
             far = jnp.where(at >= n * held, far_stores[n * block + k][0], far)
-        for a, done in enumerate(rotate_one(values, near[k], far, orbitals)):
+        right = values if turned else right_turn(values, near[k])
+        for a, done in enumerate(left_turn(right, far)):
             out[k, a] = done
 
 
-def rotate(pieces, near, far_stores, far_at, mrows, modes, start, place, before):
+def rotate(pieces, near, far_stores, far_at, mrows, modes, start, place, before, turned=False):
     total, orbitals = near.shape[:2]
     block = 8
     first = start // block
@@ -190,7 +224,8 @@
 
     return pl.pallas_call(
         lambda *refs: rotate_kernel(
-            *refs, block=block, mrows=mrows, parts=len(pieces), stores=stores, held=held, start=start
+            *refs, block=block, mrows=mrows, parts=len(pieces), stores=stores, held=held, start=start,
+            turned=turned
         ),
         out_shape=jax.ShapeDtypeStruct((total, modes, orbitals, lanes), jnp.float32),
         grid_spec=pltpu.PrefetchScalarGridSpec(
@@ -319,10 +354,10 @@
         high, low = prepare_table(wannier_table)
         grid_rows = known.transpose(0, 2, 1).astype(jnp.float32)
         turned_rows = grid_rows[me ^ owners]
-        edges = [0, kpoints // 2, kpoints // 4 * 3, kpoints]
+        edges = [0, kpoints // 8 * 5, kpoints]
         sent = []
         for start, end in zip(edges, edges[1:]):
-            last = end == kpoints
+            last = False
             rows = (grid_rows if last else turned_rows)[:, start:end]
             values = fill(rows, high, low, 1 if last else devices, [far_at])
             if last:
@@ -334,8 +369,20 @@
 
         out = None
         for c, pieces in enumerate(sent):
+            early = c == 0
+            if early:
+                pieces = [turn_right(pieces, eigen_vectors, mrows, modes * orbitals, edges[c], place)]
             out = rotate(
-                pieces, eigen_vectors, [from_near, from_far], far_at, mrows, modes, edges[c], place, out
+                pieces,
+                eigen_vectors,
+                [from_near, from_far],
+                far_at,
+                0 if early else mrows,
+                modes,
+                edges[c],
+                place,
+                out,
+                early,
             )
         return out
 

time: 273 us -> 272 us (level)
  waiting for transfers between devices: 102 us -> 116 us
  starting transfers between devices: 79.2 us -> 68.5 us
    ppermute x30, waiting for transfers between devices: 26.9 us -> 46.1 us  [send(): lax.ppermute(blocks[s], 'ka', [(d, d ^ s) for d in range(devices)])]
    pallas_call x0 -> x1, Pallas kernels: none -> 5.57 us  [turn_right(): pl.pallas_call(lambda *refs: right_kernel(*refs, block=block, mrows=mrows...]
    all_to_all x1 -> x0, starting transfers between devices: 5.54 us -> none  [exchange(): return lax.all_to_all(x, 'ka', split_axis=0, concat_axis=0, tiled=True)]
    pallas_call x3 -> x2, Pallas kernels: 20.8 us -> 15.5 us  [rotate(): pl.pallas_call(lambda *refs: rotate_kernel(*refs, block=block, mrows=mrow...]
    ppermute x30, starting transfers between devices: 53.5 us -> 48.4 us  [send(): lax.ppermute(blocks[s], 'ka', [(d, d ^ s) for d in range(devices)])]
    all_to_all x2, waiting for transfers between devices: 5.01 us -> 0.01 us  [serve(): lax.all_to_all(picked, 'ka', split_axis=0, concat_axis=0, tiled=True, axi...]
    pallas_call x3 -> x2, Pallas kernels: 33 us -> 30 us  [interpolate(): pl.pallas_call(lambda *refs: interpolate_kernel(*refs, mrows=mrows, parts...]
  transfers between devices with their start and end apart: 35 -> 34, of which waited for: 15 -> 14; matrix products, arithmetic and copies ran while one was open for 5% -> 5% of each run, Pallas kernels for 21% -> 19%
where the time goes in v4:
time: 272 us; the launch traced here: 270 us
  waiting for transfers between devices  116 us (43%)
  starting transfers between devices  68.5 us (25%)
  Pallas kernels  59.3 us (22%)
  local copies, waits for them, and re-layouts  17.3 us (6%)
  other arithmetic  8.09 us (3%)
    ppermute x1, waiting for transfers between devices, relay(): lax.ppermute(eigen_vectors[leaving], 'ka', [(d, d ^ half) for d in range(...  66 us
    ppermute x30, starting transfers between devices, send(): lax.ppermute(blocks[s], 'ka', [(d, d ^ s) for d in range(devices)])  48.4 us
    ppermute x30, waiting for transfers between devices, send(): lax.ppermute(blocks[s], 'ka', [(d, d ^ s) for d in range(devices)])  46.1 us
    pallas_call x2, Pallas kernels, interpolate(): pl.pallas_call(lambda *refs: interpolate_kernel(*refs, mrows=mrows, parts...  30 us
    pallas_call x2, Pallas kernels, rotate(): pl.pallas_call(lambda *refs: rotate_kernel(*refs, block=block, mrows=mrow...  15.5 us
    all_to_all x2, starting transfers between devices, serve(): lax.all_to_all(picked, 'ka', split_axis=0, concat_axis=0, tiled=True, axi...  13.5 us
    pallas_call x1, Pallas kernels, prepare_table(): pl.pallas_call(table_kernel, out_shape=[jax.ShapeDtypeStruct((2, vectors,...  8.14 us
    gather x2, local copies, waits for them, and re-layouts, serve(): picked = held[wanted.reshape(-1)].reshape(half, capacity * orbitals, lanes)  7.06 us
  transfers between devices with their start and end apart: 34, of which 14 were waited for; matrix products, arithmetic and copies ran while one was open for 5% of the time, Pallas kernels for 19%

profile of v4, /device:TPU:9, one launch (start us, length us, event | category | flops | bytes accessed | tf_op | source)
XLA Modules:
  0.0 270.4 jit_solution(4434971504702246414)
XLA Ops:
  1.6 6.3 %all-to-all-start.4 = ((s32[32,1,512]{2,1,0:T(1,128)}), s32[32,1,512]{2,1,0:T(1,128)S(1)}, u32[]{:S(2)}, u32[]{:S(2)}) async-start(s32[32,1,512]{2,1,0:T(1,128)} %reshape.374), calls=%async_computation.4 | async-start | bytes 131072 | tf_op jit(solution)/shard_map/all_to_all | solution.py:283
  10.4 3.6 %all-to-all-done.4 = s32[32,1,512]{2,1,0:T(1,128)S(1)} async-done(((s32[32,1,512]{2,1,0:T(1,128)}), s32[32,1,512]{2,1,0:T(1,128)S(1)}, u32[]{:S(2)}, u32[]{:S(2)}) %all-to-all-start.4) | async-done | bytes 65568 | tf_op jit(solution)/shard_map/all_to_all | solution.py:283
  17.4 252.8 %conditional.1 = (f32[64,2,64,128]{3,2,1,0:T(8,128)}) conditional(s32[]{:T(128)} %convert_element_type.59, (s32[64]{0:T(128)}, s32[64]{0:T(128)S(1)}, s32[16,8,64]{2,1,0:T(8,128)S(1)}, f32[2,1024,512]{2,1,0:T(8,128)}, f32[8,1024]{1,0:T(8,128)S(1)}, /*index=5*/s32[]{:T(128)}, f32[64,64,128]{2,1,0:T(8,128)}, s32[1]{0:T(128)}) %tuple.42, (s32[64]{0:T(128)}, ...), branch_computations={%region_4.7_spmd, %region_7.18_spmd} | conditional | flops 430009 | bytes 72982984 | solution.py:391
  18.1 3.6 %gather_fusion.1 = f32[64,64,128]{2,1,0:T(8,128)} fusion(f32[64,64,128]{2,1,0:T(8,128)} %get-tuple-element.157.refs_17_.refs_3_.refs_18_, s32[1024]{0:T(1024)S(1)} %pad_clamp_fusion.3), kind=kCustom, calls=%fused_computation.2 | custom fusion | bytes 4194560 | tf_op jit(solution)/shard_map/cond/branch_1_fun/gather | solution.py:329
  21.7 5.2 %all-to-all-start = ((f32[8,512,128]{2,1,0:T(8,128)}), f32[8,512,128]{2,1,0:T(8,128)S(1)}, u32[]{:S(2)}, u32[]{:S(2)}) async-start(f32[8,512,128]{2,1,0:T(8,128)} %bitcast.84), calls=%async_computation | async-start | bytes 4194304 | tf_op jit(solution)/shard_map/cond/branch_1_fun/all_to_all | solution.py:330
  27.6 3.4 %gather_fusion.2 = f32[48,64,128]{2,1,0:T(8,128)} fusion(f32[64,64,128]{2,1,0:T(8,128)} %get-tuple-element.157.refs_17_.refs_3_.refs_18_, s32[1024]{0:T(1024)S(1)} %pad_clamp_fusion.2), kind=kCustom, calls=%fused_computation.3 | custom fusion | bytes 3145920 | tf_op jit(solution)/shard_map/cond/branch_1_fun/gather | solution.py:343
  32.8 66.0 %collective-permute-done.15 = f32[48,64,128]{2,1,0:T(8,128)} collective-permute-done((f32[48,64,128]{2,1,0:T(8,128)}, f32[48,64,128]{2,1,0:T(8,128)}, u32[]{:S(2)}, u32[]{:S(2)}) %collective-permute-start.15) | collective-permute-done | bytes 1572896 | tf_op jit(solution)/shard_map/cond/branch_1_fun/ppermute | solution.py:342
  98.8 3.5 %gather_fusion.3 = f32[64,64,128]{2,1,0:T(8,128)} fusion(f32[48,64,128]{2,1,0:T(8,128)} %collective-permute-done.15, s32[1024]{0:T(1024)S(1)} %pad_clamp_fusion.1), kind=kCustom, calls=%fused_computation.4 | custom fusion | bytes 4194560 | tf_op jit(solution)/shard_map/cond/branch_1_fun/gather | solution.py:329
  103.6 8.3 %all-to-all-start.1 = ((f32[8,512,128]{2,1,0:T(8,128)}), f32[8,512,128]{2,1,0:T(8,128)}, u32[]{:S(2)}, u32[]{:S(2)}) async-start(f32[8,512,128]{2,1,0:T(8,128)} %bitcast.83), calls=%async_computation.1 | async-start | bytes 4194304 | tf_op jit(solution)/shard_map/cond/branch_1_fun/all_to_all | solution.py:330
  113.4 8.1 %table.3 = (bf16[2,1024,1024]{2,1,0:T(8,128)(2,1)}, bf16[2,1024,1024]{2,1,0:T(8,128)(2,1)}) custom-call(f32[2,1024,512]{2,1,0:T(8,128)} %get-tuple-element.138.table), custom_call_target="tpu_custom_call" | custom-call | tf_op jit(solution)/shard_map/cond/branch_1_fun/table/pallas_call | solution.py:63
  122.0 12.1 %interpolate.4 = (f32[192,128]{1,0:T(8,128)}, f32[192,128]{1,0:T(8,128)}, f32[192,128]{1,0:T(8,128)}, f32[192,128]{1,0:T(8,128)}, f32[192,128]{1,0:T(8,128)}, /*...) custom-call(f32[384,8]{1,0:T(8,128)} %bitcast.93, ...), custom_call_target="tpu_custom_call" | custom-call | tf_op jit(solution)/shard_map/cond/branch_1_fun/interpolate/pallas_call | solution.py:111
  139.2 2.4 collective-permute-start.6
  141.9 2.2 collective-permute-start.8
  146.4 18.0 %interpolate.5 = (f32[320,128]{1,0:T(8,128)}, f32[320,128]{1,0:T(8,128)}, f32[320,128]{1,0:T(8,128)}, f32[320,128]{1,0:T(8,128)}, f32[320,128]{1,0:T(8,128)}, /*...) custom-call(f32[640,8]{1,0:T(8,128)} %bitcast.89, ...), custom_call_target="tpu_custom_call" | custom-call | tf_op jit(solution)/shard_map/cond/branch_1_fun/interpolate/pallas_call | solution.py:111
  171.2 2.5 collective-permute-start.22
  175.4 2.2 collective-permute-start.23
  177.7 2.2 collective-permute-start.25
  179.9 5.4 %collective-permute-done.21.refs_7_ = f32[320,128]{1,0:T(8,128)S(1)} collective-permute-done((f32[320,128]{1,0:T(8,128)}, f32[320,128]{1,0:T(8,128)S(1)}, u32[]{:S(2)}, u32[]{:S(2)}) %collective-permute-start.21) | collective-permute-done | bytes 163872 | tf_op jit(solution)/shard_map/cond/branch_1_fun/ppermute | solution.py:251
  185.3 4.3 %collective-permute-start.26 = (f32[320,128]{1,0:T(8,128)}, f32[320,128]{1,0:T(8,128)}, u32[]{:S(2)}, u32[]{:S(2)}) collective-permute-start(f32[320,128]{1,0:T(8,128)} %get-tuple-element.171), channel_id=1, source_target_pairs={{0,11},{1,10},{2,9},{3,8},{4,15},{5,14},{6,13},{7,12},{8,3},{9,2},... | collective-permute-start | bytes 491528 | tf_op jit(solution)/shard_map/cond/branch_1_fun/ppermute | solution.py:251
  191.4 14.7 %collective-permute-done.24.refs_10_ = f32[320,128]{1,0:T(8,128)} collective-permute-done((f32[320,128]{1,0:T(8,128)}, f32[320,128]{1,0:T(8,128)}, u32[]{:S(2)}, u32[]{:S(2)}) %collective-permute-start.24) | collective-permute-done | bytes 163872 | tf_op jit(solution)/shard_map/cond/branch_1_fun/ppermute | solution.py:251
  206.2 3.5 %collective-permute-done.25.refs_11_ = f32[320,128]{1,0:T(8,128)} collective-permute-done((f32[320,128]{1,0:T(8,128)}, f32[320,128]{1,0:T(8,128)}, u32[]{:S(2)}, u32[]{:S(2)}) %collective-permute-start.25) | collective-permute-done | bytes 163872 | tf_op jit(solution)/shard_map/cond/branch_1_fun/ppermute | solution.py:251
  210.7 9.4 %collective-permute-done.26.refs_12_ = f32[320,128]{1,0:T(8,128)} collective-permute-done((f32[320,128]{1,0:T(8,128)}, f32[320,128]{1,0:T(8,128)}, u32[]{:S(2)}, u32[]{:S(2)}) %collective-permute-start.26) | collective-permute-done | bytes 163872 | tf_op jit(solution)/shard_map/cond/branch_1_fun/ppermute | solution.py:251
  220.1 4.4 %collective-permute-start.10 = (f32[192,128]{1,0:T(8,128)}, f32[192,128]{1,0:T(8,128)S(1)}, u32[]{:S(2)}, u32[]{:S(2)}) collective-permute-start(f32[192,128]{1,0:T(8,128)} %get-tuple-element.152), channel_id=1, source_target_pairs={{0,11},{1,10},{2,9},{3,8},{4,15},{5,14},{6,13},{7,12},{8,3},{9,2},... | collective-permute-start | bytes 294920 | tf_op jit(solution)/shard_map/cond/branch_1_fun/ppermute | solution.py:251
  224.5 5.4 %collective-permute-done.27.refs_13_ = f32[320,128]{1,0:T(8,128)} collective-permute-done((f32[320,128]{1,0:T(8,128)}, f32[320,128]{1,0:T(8,128)}, u32[]{:S(2)}, u32[]{:S(2)}) %collective-permute-start.27) | collective-permute-done | bytes 163872 | tf_op jit(solution)/shard_map/cond/branch_1_fun/ppermute | solution.py:251
  229.9 6.6 %collective-permute-start.11 = (f32[192,128]{1,0:T(8,128)}, f32[192,128]{1,0:T(8,128)}, u32[]{:S(2)}, u32[]{:S(2)}) collective-permute-start(f32[192,128]{1,0:T(8,128)} %get-tuple-element.153), channel_id=1, source_target_pairs={{0,12},{1,13},{2,14},{3,15},{4,8},{5,9},{6,10},{7,11},{8,4},{9,5},... | collective-permute-start | bytes 294920 | tf_op jit(solution)/shard_map/cond/branch_1_fun/ppermute | solution.py:251
  237.8 2.4 collective-permute-start.12
  240.2 1.9 collective-permute-done.29.refs_15_
  242.1 2.3 collective-permute-start.13
  246.0 2.2 collective-permute-start.14
  248.2 5.6 %turn_right.1.refs_2_ = f32[40,128,128]{2,1,0:T(8,128)} custom-call(s32[1]{0:T(128)} %get-tuple-element.128.refs_0_, f32[320,128]{1,0:T(8,128)} %get-tuple-element.160.refs_1_, f32[320,128]{1,0:T(8,128)} %copy-done.3, f32[320,128]{1,0:T(8,128)} %copy-done.4, f32[320,128]{1,0:T(8,128)} %copy-done.5, f32[320,128]{1,0:T(8,128)} %copy-done.6, ...), custom_call_target="tpu_custom_call" | custom-call | tf_op jit(solution)/shard_map/cond/branch_1_fun/turn_right/pallas_call | solution.py:171
  253.8 8.1 %rotate.4.refs_35_ = f32[64,2,64,128]{3,2,1,0:T(8,128)} custom-call(s32[1]{0:T(128)} %get-tuple-element.128.refs_0_, s32[64]{0:T(128)} %compare_select_fusion.5.refs_4_.refs_1_, f32[40,128,128]{2,1,0:T(8,128)} %turn_right.1.refs_2_, f32[64,64,128]{2,1,0:T(8,128)S(1)} %copy-done.2, f32[64,64,128]{2,1,0:T(8,128)} %bitcast.61, f32[64,64,128]{2,1,0:T(8,128)} %bitcast.62, ...), custom_call_target="tpu_custom_call" | custom-call | tf_op jit(solution)/shard_map/cond/branch_1_fun/rotate/pallas_call | solution.py:225
  262.5 7.5 %rotate.5 = f32[64,2,64,128]{3,2,1,0:T(8,128)} custom-call(s32[1]{0:T(128)} %get-tuple-element.128.refs_0_, s32[64]{0:T(128)} %compare_select_fusion.5.refs_4_.refs_1_, f32[192,128]{1,0:T(8,128)} %get-tuple-element.141.refs_2_, f32[192,128]{1,0:T(8,128)} %copy-done.11, f32[192,128]{1,0:T(8,128)} %copy-done.12, ...), custom_call_target="tpu_custom_call", output_to_operand_aliasing={{}: (35, {})} | custom-call | tf_op jit(solution)/shard_map/cond/branch_1_fun/rotate/pallas_call | solution.py:225
  (148 shorter events, 36.0 us)
Async XLA Ops:
  1.6 12.3 %all-to-all-start.4 = ((s32[32,1,512]{2,1,0:T(1,128)}), s32[32,1,512]{2,1,0:T(1,128)S(1)}, u32[]{:S(2)}, u32[]{:S(2)}) async-start(s32[32,1,512]{2,1,0:T(1,128)} %reshape.374), calls=%async_computation.4 | async-start | bytes 131072 | tf_op jit(solution)/shard_map/all_to_all | solution.py:283
  21.7 80.5 %all-to-all-start = ((f32[8,512,128]{2,1,0:T(8,128)}), f32[8,512,128]{2,1,0:T(8,128)S(1)}, u32[]{:S(2)}, u32[]{:S(2)}) async-start(f32[8,512,128]{2,1,0:T(8,128)} %bitcast.84), calls=%async_computation | async-start | bytes 4194304 | tf_op jit(solution)/shard_map/cond/branch_1_fun/all_to_all | solution.py:330
  31.0 67.8 %collective-permute-start.15 = (f32[48,64,128]{2,1,0:T(8,128)}, f32[48,64,128]{2,1,0:T(8,128)}, u32[]{:S(2)}, u32[]{:S(2)}) collective-permute-start(f32[48,64,128]{2,1,0:T(8,128)} %gather_fusion.2), channel_id=1, source_target_pairs={{0,8},{1,9},{2,10},{3,11},{4,12},{5,13},{6,14},{7,15},{8,0},{9,1},... | collective-permute-start | bytes 4718600 | tf_op jit(solution)/shard_map/cond/branch_1_fun/ppermute | solution.py:342
  103.6 150.2 %all-to-all-start.1 = ((f32[8,512,128]{2,1,0:T(8,128)}), f32[8,512,128]{2,1,0:T(8,128)}, u32[]{:S(2)}, u32[]{:S(2)}) async-start(f32[8,512,128]{2,1,0:T(8,128)} %bitcast.83), calls=%async_computation.1 | async-start | bytes 4194304 | tf_op jit(solution)/shard_map/cond/branch_1_fun/all_to_all | solution.py:330
  134.6 4.7 %collective-permute-start.1 = (f32[192,128]{1,0:T(8,128)}, f32[192,128]{1,0:T(8,128)S(1)}, u32[]{:S(2)}, u32[]{:S(2)}) collective-permute-start(f32[192,128]{1,0:T(8,128)} %get-tuple-element.143), channel_id=1, source_target_pairs={{0,2},{1,3},{2,0},{3,1},{4,6},{5,7},{6,4},{7,5},{8,10},{9,11},{10,... | collective-permute-start | bytes 294920 | tf_op jit(solution)/shard_map/cond/branch_1_fun/ppermute | solution.py:251
  135.8 5.9 %collective-permute-start.2 = (f32[192,128]{1,0:T(8,128)}, f32[192,128]{1,0:T(8,128)S(1)}, u32[]{:S(2)}, u32[]{:S(2)}) collective-permute-start(f32[192,128]{1,0:T(8,128)} %get-tuple-element.144), channel_id=1, source_target_pairs={{0,3},{1,2},{2,1},{3,0},{4,7},{5,6},{6,5},{7,4},{8,11},{9,10},{10,... | collective-permute-start | bytes 294920 | tf_op jit(solution)/shard_map/cond/branch_1_fun/ppermute | solution.py:251
  136.3 5.6 %collective-permute-start.3 = (f32[192,128]{1,0:T(8,128)}, f32[192,128]{1,0:T(8,128)S(1)}, u32[]{:S(2)}, u32[]{:S(2)}) collective-permute-start(f32[192,128]{1,0:T(8,128)} %get-tuple-element.145), channel_id=1, source_target_pairs={{0,4},{1,5},{2,6},{3,7},{4,0},{5,1},{6,2},{7,3},{8,12},{9,13},{10,... | collective-permute-start | bytes 294920 | tf_op jit(solution)/shard_map/cond/branch_1_fun/ppermute | solution.py:251
  136.4 7.6 %collective-permute-start.4 = (f32[192,128]{1,0:T(8,128)}, f32[192,128]{1,0:T(8,128)S(1)}, u32[]{:S(2)}, u32[]{:S(2)}) collective-permute-start(f32[192,128]{1,0:T(8,128)} %get-tuple-element.146), channel_id=1, source_target_pairs={{0,5},{1,4},{2,7},{3,6},{4,1},{5,0},{6,3},{7,2},{8,13},{9,12},{10,... | collective-permute-start | bytes 294920 | tf_op jit(solution)/shard_map/cond/branch_1_fun/ppermute | solution.py:251
  138.1 26.3 %collective-permute-start.5 = (f32[192,128]{1,0:T(8,128)}, f32[192,128]{1,0:T(8,128)S(1)}, u32[]{:S(2)}, u32[]{:S(2)}) collective-permute-start(f32[192,128]{1,0:T(8,128)} %get-tuple-element.147), channel_id=1, source_target_pairs={{0,6},{1,7},{2,4},{3,5},{4,2},{5,3},{6,0},{7,1},{8,14},{9,15},{10,... | collective-permute-start | bytes 294920 | tf_op jit(solution)/shard_map/cond/branch_1_fun/ppermute | solution.py:251
  139.2 26.2 %collective-permute-start.6 = (f32[192,128]{1,0:T(8,128)}, f32[192,128]{1,0:T(8,128)S(1)}, u32[]{:S(2)}, u32[]{:S(2)}) collective-permute-start(f32[192,128]{1,0:T(8,128)} %get-tuple-element.148), channel_id=1, source_target_pairs={{0,7},{1,6},{2,5},{3,4},{4,3},{5,2},{6,1},{7,0},{8,15},{9,14},{10,... | collective-permute-start | bytes 294920 | tf_op jit(solution)/shard_map/cond/branch_1_fun/ppermute | solution.py:251
  141.7 23.9 %collective-permute-start.7 = (f32[192,128]{1,0:T(8,128)}, f32[192,128]{1,0:T(8,128)S(1)}, u32[]{:S(2)}, u32[]{:S(2)}) collective-permute-start(f32[192,128]{1,0:T(8,128)} %get-tuple-element.149), channel_id=1, source_target_pairs={{0,8},{1,9},{2,10},{3,11},{4,12},{5,13},{6,14},{7,15},{8,0},{9,1},... | collective-permute-start | bytes 294920 | tf_op jit(solution)/shard_map/cond/branch_1_fun/ppermute | solution.py:251
  141.9 25.3 %collective-permute-start.8 = (f32[192,128]{1,0:T(8,128)}, f32[192,128]{1,0:T(8,128)S(1)}, u32[]{:S(2)}, u32[]{:S(2)}) collective-permute-start(f32[192,128]{1,0:T(8,128)} %get-tuple-element.150), channel_id=1, source_target_pairs={{0,9},{1,8},{2,11},{3,10},{4,13},{5,12},{6,15},{7,14},{8,1},{9,0},... | collective-permute-start | bytes 294920 | tf_op jit(solution)/shard_map/cond/branch_1_fun/ppermute | solution.py:251
  144.1 23.4 %collective-permute-start.9 = (f32[192,128]{1,0:T(8,128)}, f32[192,128]{1,0:T(8,128)S(1)}, u32[]{:S(2)}, u32[]{:S(2)}) collective-permute-start(f32[192,128]{1,0:T(8,128)} %get-tuple-element.151), channel_id=1, source_target_pairs={{0,10},{1,11},{2,8},{3,9},{4,14},{5,15},{6,12},{7,13},{8,2},{9,3},... | collective-permute-start | bytes 294920 | tf_op jit(solution)/shard_map/cond/branch_1_fun/ppermute | solution.py:251
  165.4 5.8 %collective-permute-start.17 = (f32[320,128]{1,0:T(8,128)}, f32[320,128]{1,0:T(8,128)S(1)}, u32[]{:S(2)}, u32[]{:S(2)}) collective-permute-start(f32[320,128]{1,0:T(8,128)} %get-tuple-element.162), channel_id=1, source_target_pairs={{0,2},{1,3},{2,0},{3,1},{4,6},{5,7},{6,4},{7,5},{8,10},{9,11},{10,... | collective-permute-start | bytes 491528 | tf_op jit(solution)/shard_map/cond/branch_1_fun/ppermute | solution.py:251
  165.7 9.7 %collective-permute-start.18 = (f32[320,128]{1,0:T(8,128)}, f32[320,128]{1,0:T(8,128)S(1)}, u32[]{:S(2)}, u32[]{:S(2)}) collective-permute-start(f32[320,128]{1,0:T(8,128)} %get-tuple-element.163), channel_id=1, source_target_pairs={{0,3},{1,2},{2,1},{3,0},{4,7},{5,6},{6,5},{7,4},{8,11},{9,10},{10,... | collective-permute-start | bytes 491528 | tf_op jit(solution)/shard_map/cond/branch_1_fun/ppermute | solution.py:251
  167.2 10.3 %collective-permute-start.19 = (f32[320,128]{1,0:T(8,128)}, f32[320,128]{1,0:T(8,128)S(1)}, u32[]{:S(2)}, u32[]{:S(2)}) collective-permute-start(f32[320,128]{1,0:T(8,128)} %get-tuple-element.164), channel_id=1, source_target_pairs={{0,4},{1,5},{2,6},{3,7},{4,0},{5,1},{6,2},{7,3},{8,12},{9,13},{10,... | collective-permute-start | bytes 491528 | tf_op jit(solution)/shard_map/cond/branch_1_fun/ppermute | solution.py:251
  167.5 10.2 %collective-permute-start.20 = (f32[320,128]{1,0:T(8,128)}, f32[320,128]{1,0:T(8,128)S(1)}, u32[]{:S(2)}, u32[]{:S(2)}) collective-permute-start(f32[320,128]{1,0:T(8,128)} %get-tuple-element.165), channel_id=1, source_target_pairs={{0,5},{1,4},{2,7},{3,6},{4,1},{5,0},{6,3},{7,2},{8,13},{9,12},{10,... | collective-permute-start | bytes 491528 | tf_op jit(solution)/shard_map/cond/branch_1_fun/ppermute | solution.py:251
  169.1 16.2 %collective-permute-start.21 = (f32[320,128]{1,0:T(8,128)}, f32[320,128]{1,0:T(8,128)S(1)}, u32[]{:S(2)}, u32[]{:S(2)}) collective-permute-start(f32[320,128]{1,0:T(8,128)} %get-tuple-element.166), channel_id=1, source_target_pairs={{0,6},{1,7},{2,4},{3,5},{4,2},{5,3},{6,0},{7,1},{8,14},{9,15},{10,... | collective-permute-start | bytes 491528 | tf_op jit(solution)/shard_map/cond/branch_1_fun/ppermute | solution.py:251
  171.2 18.4 %collective-permute-start.22 = (f32[320,128]{1,0:T(8,128)}, f32[320,128]{1,0:T(8,128)S(1)}, u32[]{:S(2)}, u32[]{:S(2)}) collective-permute-start(f32[320,128]{1,0:T(8,128)} %get-tuple-element.167), channel_id=1, source_target_pairs={{0,7},{1,6},{2,5},{3,4},{4,3},{5,2},{6,1},{7,0},{8,15},{9,14},{10,... | collective-permute-start | bytes 491528 | tf_op jit(solution)/shard_map/cond/branch_1_fun/ppermute | solution.py:251
  175.4 15.5 %collective-permute-start.23 = (f32[320,128]{1,0:T(8,128)}, f32[320,128]{1,0:T(8,128)S(1)}, u32[]{:S(2)}, u32[]{:S(2)}) collective-permute-start(f32[320,128]{1,0:T(8,128)} %get-tuple-element.168), channel_id=1, source_target_pairs={{0,8},{1,9},{2,10},{3,11},{4,12},{5,13},{6,14},{7,15},{8,0},{9,1},... | collective-permute-start | bytes 491528 | tf_op jit(solution)/shard_map/cond/branch_1_fun/ppermute | solution.py:251
  177.5 28.6 %collective-permute-start.24 = (f32[320,128]{1,0:T(8,128)}, f32[320,128]{1,0:T(8,128)}, u32[]{:S(2)}, u32[]{:S(2)}) collective-permute-start(f32[320,128]{1,0:T(8,128)} %get-tuple-element.169), channel_id=1, source_target_pairs={{0,9},{1,8},{2,11},{3,10},{4,13},{5,12},{6,15},{7,14},{8,1},{9,0},... | collective-permute-start | bytes 491528 | tf_op jit(solution)/shard_map/cond/branch_1_fun/ppermute | solution.py:251
  177.7 31.9 %collective-permute-start.25 = (f32[320,128]{1,0:T(8,128)}, f32[320,128]{1,0:T(8,128)}, u32[]{:S(2)}, u32[]{:S(2)}) collective-permute-start(f32[320,128]{1,0:T(8,128)} %get-tuple-element.170), channel_id=1, source_target_pairs={{0,10},{1,11},{2,8},{3,9},{4,14},{5,15},{6,12},{7,13},{8,2},{9,3},... | collective-permute-start | bytes 491528 | tf_op jit(solution)/shard_map/cond/branch_1_fun/ppermute | solution.py:251
  185.3 34.8 %collective-permute-start.26 = (f32[320,128]{1,0:T(8,128)}, f32[320,128]{1,0:T(8,128)}, u32[]{:S(2)}, u32[]{:S(2)}) collective-permute-start(f32[320,128]{1,0:T(8,128)} %get-tuple-element.171), channel_id=1, source_target_pairs={{0,11},{1,10},{2,9},{3,8},{4,15},{5,14},{6,13},{7,12},{8,3},{9,2},... | collective-permute-start | bytes 491528 | tf_op jit(solution)/shard_map/cond/branch_1_fun/ppermute | solution.py:251
  189.6 40.3 %collective-permute-start.27 = (f32[320,128]{1,0:T(8,128)}, f32[320,128]{1,0:T(8,128)}, u32[]{:S(2)}, u32[]{:S(2)}) collective-permute-start(f32[320,128]{1,0:T(8,128)} %get-tuple-element.172), channel_id=1, source_target_pairs={{0,12},{1,13},{2,14},{3,15},{4,8},{5,9},{6,10},{7,11},{8,4},{9,5},... | collective-permute-start | bytes 491528 | tf_op jit(solution)/shard_map/cond/branch_1_fun/ppermute | solution.py:251
  190.8 47.0 %collective-permute-start.28 = (f32[320,128]{1,0:T(8,128)}, f32[320,128]{1,0:T(8,128)}, u32[]{:S(2)}, u32[]{:S(2)}) collective-permute-start(f32[320,128]{1,0:T(8,128)} %get-tuple-element.173), channel_id=1, source_target_pairs={{0,13},{1,12},{2,15},{3,14},{4,9},{5,8},{6,11},{7,10},{8,5},{9,4},... | collective-permute-start | bytes 491528 | tf_op jit(solution)/shard_map/cond/branch_1_fun/ppermute | solution.py:251
  206.2 35.9 %collective-permute-start.29 = (f32[320,128]{1,0:T(8,128)}, f32[320,128]{1,0:T(8,128)}, u32[]{:S(2)}, u32[]{:S(2)}) collective-permute-start(f32[320,128]{1,0:T(8,128)} %get-tuple-element.174), channel_id=1, source_target_pairs={{0,14},{1,15},{2,12},{3,13},{4,10},{5,11},{6,8},{7,9},{8,6},{9,7},... | collective-permute-start | bytes 491528 | tf_op jit(solution)/shard_map/cond/branch_1_fun/ppermute | solution.py:251
  209.7 36.3 %collective-permute-start.30 = (f32[320,128]{1,0:T(8,128)}, f32[320,128]{1,0:T(8,128)}, u32[]{:S(2)}, u32[]{:S(2)}) collective-permute-start(f32[320,128]{1,0:T(8,128)} %get-tuple-element.175), channel_id=1, source_target_pairs={{0,15},{1,14},{2,13},{3,12},{4,11},{5,10},{6,9},{7,8},{8,7},{9,6},... | collective-permute-start | bytes 491528 | tf_op jit(solution)/shard_map/cond/branch_1_fun/ppermute | solution.py:251
  220.1 41.8 %collective-permute-start.10 = (f32[192,128]{1,0:T(8,128)}, f32[192,128]{1,0:T(8,128)S(1)}, u32[]{:S(2)}, u32[]{:S(2)}) collective-permute-start(f32[192,128]{1,0:T(8,128)} %get-tuple-element.152), channel_id=1, source_target_pairs={{0,11},{1,10},{2,9},{3,8},{4,15},{5,14},{6,13},{7,12},{8,3},{9,2},... | collective-permute-start | bytes 294920 | tf_op jit(solution)/shard_map/cond/branch_1_fun/ppermute | solution.py:251
  229.9 32.0 %collective-permute-start.11 = (f32[192,128]{1,0:T(8,128)}, f32[192,128]{1,0:T(8,128)}, u32[]{:S(2)}, u32[]{:S(2)}) collective-permute-start(f32[192,128]{1,0:T(8,128)} %get-tuple-element.153), channel_id=1, source_target_pairs={{0,12},{1,13},{2,14},{3,15},{4,8},{5,9},{6,10},{7,11},{8,4},{9,5},... | collective-permute-start | bytes 294920 | tf_op jit(solution)/shard_map/cond/branch_1_fun/ppermute | solution.py:251
  237.8 24.1 %collective-permute-start.12 = (f32[192,128]{1,0:T(8,128)}, f32[192,128]{1,0:T(8,128)}, u32[]{:S(2)}, u32[]{:S(2)}) collective-permute-start(f32[192,128]{1,0:T(8,128)} %get-tuple-element.154), channel_id=1, source_target_pairs={{0,13},{1,12},{2,15},{3,14},{4,9},{5,8},{6,11},{7,10},{8,5},{9,4},... | collective-permute-start | bytes 294920 | tf_op jit(solution)/shard_map/cond/branch_1_fun/ppermute | solution.py:251
  242.1 19.8 %collective-permute-start.13 = (f32[192,128]{1,0:T(8,128)}, f32[192,128]{1,0:T(8,128)}, u32[]{:S(2)}, u32[]{:S(2)}) collective-permute-start(f32[192,128]{1,0:T(8,128)} %get-tuple-element.155), channel_id=1, source_target_pairs={{0,14},{1,15},{2,12},{3,13},{4,10},{5,11},{6,8},{7,9},{8,6},{9,7},... | collective-permute-start | bytes 294920 | tf_op jit(solution)/shard_map/cond/branch_1_fun/ppermute | solution.py:251
  246.0 16.0 %collective-permute-start.14 = (f32[192,128]{1,0:T(8,128)}, f32[192,128]{1,0:T(8,128)}, u32[]{:S(2)}, u32[]{:S(2)}) collective-permute-start(f32[192,128]{1,0:T(8,128)} %get-tuple-element.156), channel_id=1, source_target_pairs={{0,15},{1,14},{2,13},{3,12},{4,11},{5,10},{6,9},{7,8},{8,7},{9,6},... | collective-permute-start | bytes 294920 | tf_op jit(solution)/shard_map/cond/branch_1_fun/ppermute | solution.py:251
  (24 other events, 793.2 us)
